TPU v7x, 32 devices: a whole 2x2x4 slice. The times are simulated.
32 devices in a mesh: wt: 8 (over z, x), seq: 4 (over y, core).
Axes of the slice: x: 2, y: 2, z: 4, core: 2. Of those that a mesh axis runs over, the one named last changes fastest.
Arguments:
- tokens: bfloat16 [8192, 1024], P(('wt', 'seq')), may hold values from -6 to 6
- positions: int32 [8192], P(('wt', 'seq')), may hold values from 0 to 8191, as said below
- doc_ids: int32 [8192], P('wt'), may hold values from 0 to 15, as said below
- block_ids: int32 [8192], P('wt'), may hold values from 0 to 31, as said below
- entry_gain: bfloat16 [1024], P('wt'), may hold values from 0.5 to 1.5
- query_weight: bfloat16 [1024, 1024], P('wt'), may hold values from -0.1875 to 0.1875
- key_weight: bfloat16 [1024, 1024], P('wt'), may hold values from -0.1875 to 0.1875
- value_weight: bfloat16 [1024, 1024], P('wt'), may hold values from -0.1875 to 0.1875
- output_weight: bfloat16 [1024, 1024], P('wt'), may hold values from -0.1875 to 0.1875
- attend_gain: bfloat16 [1024], P('wt'), may hold values from 0.5 to 1.5
- middle_gain: bfloat16 [1024], P('wt'), may hold values from 0.5 to 1.5
- gate_weight: bfloat16 [1024, 2816], P('wt'), may hold values from -0.1875 to 0.1875
- up_weight: bfloat16 [1024, 2816], P('wt'), may hold values from -0.1875 to 0.1875
- down_weight: bfloat16 [2816, 1024], P('wt'), may hold values from -0.109375 to 0.109375
- closing_gain: bfloat16 [1024], P('wt'), may hold values from 0.5 to 1.5
- cotangent: bfloat16 [8192, 1024], P(('wt', 'seq')), may hold values from -6 to 6
Outputs:
- layer_output: bfloat16 [8192, 1024], P(('wt', 'seq'))
- input_grad: float32 [8192, 1024], P(('wt', 'seq'))
- grad_entry: float32 [1024], P('wt')
- grad_query: float32 [1024, 1024], P('wt')
- grad_key: float32 [1024, 1024], P('wt')
- grad_value: float32 [1024, 1024], P('wt')
- grad_output: float32 [1024, 1024], P('wt')
- grad_attend: float32 [1024], P('wt')
- grad_middle: float32 [1024], P('wt')
- grad_gate: float32 [1024, 2816], P('wt')
- grad_up: float32 [1024, 2816], P('wt')
- grad_down: float32 [2816, 1024], P('wt')
- grad_closing: float32 [1024], P('wt')
Inputs may be any that keep to these rules, and one draw needn't show every extreme that they name: In each window of 1024 tokens the first tokens are the last ones of a document of 8192 tokens, ending at position 8191, and the others begin a new document at position 0; positions rise by one within a document; the boundary lies between a quarter and three quarters of the window. `doc_ids`: each window holds two documents; ids never fall and differ between windows. `block_ids`: A token's block is its position divided by 256, rounded down.
All inputs are finite; a program needn't handle non-finite values.
Results may differ from a plain program's by a relative error of at most 0.02.
Values may be sent and summed in bfloat16 or wider, within the bound.
No kernel may reach another device: no remote copies, remote signals or barrier semaphores. Data moves between devices by JAX's collectives and lax.ppermute only.
A program may use at most 192 MiB of HBM per device.

v0:
```python
import jax
import jax.numpy as jnp
from jax import lax
from jax.sharding import PartitionSpec as P

HEADS = 8


EPSILON = 1e-06
ROTARY_BASE = 50000.0


def norm_rows(values, scales):
    inverse = lax.rsqrt(jnp.mean(values * values, -1, keepdims=True) + EPSILON)
    normed = values * inverse
    return (normed * scales, normed, inverse)


def norm_back(incoming, normed, inverse, scales):
    scaled = incoming * scales
    input_side = inverse * (scaled - normed * jnp.mean(scaled * normed, -1, keepdims=True))
    return (input_side, jnp.sum(incoming * normed, 0))


def rotation(positions, head_width):
    half_width = head_width // 2
    frequency = ROTARY_BASE ** (-2.0 * jnp.arange(half_width, dtype=jnp.float32) / head_width)
    angles = positions.astype(jnp.float32)[:, None] * frequency[None, :]
    return (jnp.cos(angles)[:, None, :], jnp.sin(angles)[:, None, :])


def rotate(tensor, turning, backward):
    cosine, sine_part = turning
    if backward:
        sine_part = -sine_part
    half_width = tensor.shape[-1] // 2
    former = tensor[..., :half_width]
    latter = tensor[..., half_width:]
    return jnp.concatenate(
        [former * cosine - latter * sine_part, latter * cosine + former * sine_part], -1
    )


def scores_for(query_rows, key_rows, query_docs, query_blocks, key_docs, key_blocks):
    factor = query_rows.shape[-1] ** (-0.5)
    logits = (
        jnp.einsum("qhd,khd->hqk", query_rows, key_rows, preferred_element_type=jnp.float32)
        * factor
    )
    visible = (query_docs[:, None] == key_docs[None, :]) & (
        key_blocks[None, :] <= query_blocks[:, None]
    )
    return jnp.where(visible[None], logits, -1e30)


def on_device(
    tokens,
    positions,
    doc_ids,
    block_ids,
    entry_gain,
    query_weight,
    key_weight,
    value_weight,
    output_weight,
    attend_gain,
    middle_gain,
    gate_weight,
    up_weight,
    down_weight,
    closing_gain,
    cotangent,
):
    attention_parts = (
        lax.all_gather(entry_gain, "wt", axis=0, tiled=True),
        lax.all_gather(query_weight, "wt", axis=0, tiled=True),
        lax.all_gather(key_weight, "wt", axis=0, tiled=True),
        lax.all_gather(value_weight, "wt", axis=0, tiled=True),
        lax.all_gather(output_weight, "wt", axis=0, tiled=True),
        lax.all_gather(attend_gain, "wt", axis=0, tiled=True),
    )
    channel_parts = (
        lax.all_gather(middle_gain, "wt", axis=0, tiled=True),
        lax.all_gather(gate_weight, "wt", axis=0, tiled=True),
        lax.all_gather(up_weight, "wt", axis=0, tiled=True),
        lax.all_gather(down_weight, "wt", axis=0, tiled=True),
        lax.all_gather(closing_gain, "wt", axis=0, tiled=True),
    )
    entry_full, query_full, key_full, value_full, output_full, attend_full = attention_parts
    middle_full, gate_full, up_full, down_full, closing_full = channel_parts
    token_rows = tokens.shape[0]
    model_width = tokens.shape[1]
    head_width = model_width // HEADS
    head_shape = (token_rows, HEADS, head_width)
    inputs = tokens.astype(jnp.float32)
    entry_out, entry_normed, entry_inverse = norm_rows(inputs, entry_full.astype(jnp.float32))
    entry_low = entry_out.astype(jnp.bfloat16)
    turning = rotation(positions, head_width)
    query_raw = jnp.dot(entry_low, query_full, preferred_element_type=jnp.float32).reshape(
        head_shape
    )
    key_raw = jnp.dot(entry_low, key_full, preferred_element_type=jnp.float32).reshape(head_shape)
    value_raw = jnp.dot(entry_low, value_full, preferred_element_type=jnp.float32).reshape(
        head_shape
    )
    query_low = rotate(query_raw, turning, False).astype(jnp.bfloat16)
    key_low = rotate(key_raw, turning, False).astype(jnp.bfloat16)
    value_low = value_raw.astype(jnp.bfloat16)
    query_heads, key_heads, value_heads = (
        lax.all_to_all(query_low, "seq", split_axis=1, concat_axis=0, tiled=True),
        lax.all_to_all(key_low, "seq", split_axis=1, concat_axis=0, tiled=True),
        lax.all_to_all(value_low, "seq", split_axis=1, concat_axis=0, tiled=True),
    )
    group_rows = query_heads.shape[0]
    local_heads = query_heads.shape[1]
    row_block = min(512, group_rows)
    block_count = group_rows // row_block
    factor = head_width ** (-0.5)
    query_split = query_heads.reshape(block_count, row_block, local_heads, head_width)
    docs_split = doc_ids.reshape(block_count, row_block)
    blocks_split = block_ids.reshape(block_count, row_block)

    def forward_block(pieces):
        query_rows, query_docs, query_blocks = pieces
        logits = scores_for(query_rows, key_heads, query_docs, query_blocks, doc_ids, block_ids)
        row_max = jnp.max(logits, -1, keepdims=True)
        weights = jnp.exp(logits - row_max)
        totals = jnp.sum(weights, -1, keepdims=True)
        attention_probs = weights / totals
        attended = jnp.einsum(
            "hqk,khd->qhd",
            attention_probs.astype(jnp.bfloat16),
            value_heads,
            preferred_element_type=jnp.float32,
        )
        return (attended.astype(jnp.bfloat16), (row_max + jnp.log(totals))[..., 0])

    attended_split, log_totals = lax.map(forward_block, (query_split, docs_split, blocks_split))
    attended_heads = attended_split.reshape(group_rows, local_heads, head_width)
    attended_tokens = lax.all_to_all(
        attended_heads, "seq", split_axis=0, concat_axis=1, tiled=True
    ).reshape(token_rows, model_width)
    mixed = jnp.dot(attended_tokens, output_full, preferred_element_type=jnp.float32)
    attend_out, attend_normed, attend_inverse = norm_rows(mixed, attend_full.astype(jnp.float32))
    hidden_state = inputs + attend_out
    middle_out, middle_normed, middle_inverse = norm_rows(
        hidden_state, middle_full.astype(jnp.float32)
    )
    middle_low = middle_out.astype(jnp.bfloat16)
    gate_value = jnp.dot(middle_low, gate_full, preferred_element_type=jnp.float32)
    up_value = jnp.dot(middle_low, up_full, preferred_element_type=jnp.float32)
    sigmoid_gate = jax.nn.sigmoid(gate_value)
    activated = (gate_value * sigmoid_gate * up_value).astype(jnp.bfloat16)
    channel_out = jnp.dot(activated, down_full, preferred_element_type=jnp.float32)
    closing_out, closing_normed, closing_inverse = norm_rows(
        channel_out, closing_full.astype(jnp.float32)
    )
    layer_output = (hidden_state + closing_out).astype(jnp.bfloat16)
    incoming = cotangent.astype(jnp.float32)
    channel_grad, closing_local = norm_back(
        incoming, closing_normed, closing_inverse, closing_full.astype(jnp.float32)
    )
    channel_low = channel_grad.astype(jnp.bfloat16)
    down_local = jnp.dot(activated.T, channel_low, preferred_element_type=jnp.float32)
    active_grad = jnp.dot(channel_low, down_full.T, preferred_element_type=jnp.float32)
    gate_grad = (
        active_grad * up_value * sigmoid_gate * (1.0 + gate_value * (1.0 - sigmoid_gate))
    ).astype(jnp.bfloat16)
    up_grad = (active_grad * gate_value * sigmoid_gate).astype(jnp.bfloat16)
    gate_local = jnp.dot(middle_low.T, gate_grad, preferred_element_type=jnp.float32)
    up_local = jnp.dot(middle_low.T, up_grad, preferred_element_type=jnp.float32)
    middle_grad = jnp.dot(gate_grad, gate_full.T, preferred_element_type=jnp.float32) + jnp.dot(
        up_grad, up_full.T, preferred_element_type=jnp.float32
    )
    hidden_back, middle_local = norm_back(
        middle_grad, middle_normed, middle_inverse, middle_full.astype(jnp.float32)
    )
    hidden_grad = incoming + hidden_back
    channel_shares = (
        lax.psum_scatter(middle_local, "wt", scatter_dimension=0, tiled=True),
        lax.psum_scatter(gate_local, "wt", scatter_dimension=0, tiled=True),
        lax.psum_scatter(up_local, "wt", scatter_dimension=0, tiled=True),
        lax.psum_scatter(down_local, "wt", scatter_dimension=0, tiled=True),
        lax.psum_scatter(closing_local, "wt", scatter_dimension=0, tiled=True),
    )
    grad_middle, grad_gate, grad_up, grad_down, grad_closing = (
        lax.psum(channel_shares[0].astype(jnp.bfloat16), "seq").astype(jnp.float32),
        lax.psum(channel_shares[1].astype(jnp.bfloat16), "seq").astype(jnp.float32),
        lax.psum(channel_shares[2].astype(jnp.bfloat16), "seq").astype(jnp.float32),
        lax.psum(channel_shares[3].astype(jnp.bfloat16), "seq").astype(jnp.float32),
        lax.psum(channel_shares[4].astype(jnp.bfloat16), "seq").astype(jnp.float32),
    )
    mixed_grad, attend_local = norm_back(
        hidden_grad, attend_normed, attend_inverse, attend_full.astype(jnp.float32)
    )
    mixed_low = mixed_grad.astype(jnp.bfloat16)
    output_local = jnp.dot(attended_tokens.T, mixed_low, preferred_element_type=jnp.float32)
    attended_grad = jnp.dot(mixed_low, output_full.T, preferred_element_type=jnp.float32).astype(
        jnp.bfloat16
    )
    attended_back = lax.all_to_all(
        attended_grad.reshape(head_shape), "seq", split_axis=1, concat_axis=0, tiled=True
    )
    incoming_split = attended_back.reshape(block_count, row_block, local_heads, head_width)

    def backward_block(running, pieces):
        key_sum, value_sum = running
        query_rows, query_docs, query_blocks, incoming_rows, log_rows = pieces
        logits = scores_for(query_rows, key_heads, query_docs, query_blocks, doc_ids, block_ids)
        attention_probs = jnp.exp(logits - log_rows[..., None])
        value_sum = value_sum + jnp.einsum(
            "hqk,qhd->khd",
            attention_probs.astype(jnp.bfloat16),
            incoming_rows,
            preferred_element_type=jnp.float32,
        )
        prob_grad = jnp.einsum(
            "qhd,khd->hqk", incoming_rows, value_heads, preferred_element_type=jnp.float32
        )
        score_grad = attention_probs * (
            prob_grad - jnp.sum(attention_probs * prob_grad, -1, keepdims=True)
        )
        score_low = score_grad.astype(jnp.bfloat16)
        query_grad = (
            jnp.einsum("hqk,khd->qhd", score_low, key_heads, preferred_element_type=jnp.float32)
            * factor
        )
        key_sum = (
            key_sum
            + jnp.einsum("hqk,qhd->khd", score_low, query_rows, preferred_element_type=jnp.float32)
            * factor
        )
        return ((key_sum, value_sum), query_grad)

    empty_sum = jnp.zeros((group_rows, local_heads, head_width), jnp.float32)
    (key_sum, value_sum), query_back = lax.scan(
        backward_block,
        (empty_sum, empty_sum),
        (query_split, docs_split, blocks_split, incoming_split, log_totals),
    )
    query_back_low = query_back.reshape(group_rows, local_heads, head_width).astype(jnp.bfloat16)
    key_back_low = key_sum.astype(jnp.bfloat16)
    value_back_low = value_sum.astype(jnp.bfloat16)
    query_tokens, key_tokens, value_tokens = (
        lax.all_to_all(query_back_low, "seq", split_axis=0, concat_axis=1, tiled=True),
        lax.all_to_all(key_back_low, "seq", split_axis=0, concat_axis=1, tiled=True),
        lax.all_to_all(value_back_low, "seq", split_axis=0, concat_axis=1, tiled=True),
    )
    query_raw_grad = (
        rotate(query_tokens.astype(jnp.float32), turning, True)
        .reshape(token_rows, model_width)
        .astype(jnp.bfloat16)
    )
    key_raw_grad = (
        rotate(key_tokens.astype(jnp.float32), turning, True)
        .reshape(token_rows, model_width)
        .astype(jnp.bfloat16)
    )
    value_raw_grad = value_tokens.reshape(token_rows, model_width)
    query_local = jnp.dot(entry_low.T, query_raw_grad, preferred_element_type=jnp.float32)
    key_local = jnp.dot(entry_low.T, key_raw_grad, preferred_element_type=jnp.float32)
    value_local = jnp.dot(entry_low.T, value_raw_grad, preferred_element_type=jnp.float32)
    entry_grad = (
        jnp.dot(query_raw_grad, query_full.T, preferred_element_type=jnp.float32)
        + jnp.dot(key_raw_grad, key_full.T, preferred_element_type=jnp.float32)
        + jnp.dot(value_raw_grad, value_full.T, preferred_element_type=jnp.float32)
    )
    input_back, entry_local = norm_back(
        entry_grad, entry_normed, entry_inverse, entry_full.astype(jnp.float32)
    )
    input_grad = hidden_grad + input_back
    attention_shares = (
        lax.psum_scatter(entry_local, "wt", scatter_dimension=0, tiled=True),
        lax.psum_scatter(query_local, "wt", scatter_dimension=0, tiled=True),
        lax.psum_scatter(key_local, "wt", scatter_dimension=0, tiled=True),
        lax.psum_scatter(value_local, "wt", scatter_dimension=0, tiled=True),
        lax.psum_scatter(output_local, "wt", scatter_dimension=0, tiled=True),
        lax.psum_scatter(attend_local, "wt", scatter_dimension=0, tiled=True),
    )
    grad_entry, grad_query, grad_key, grad_value, grad_output, grad_attend = (
        lax.psum(attention_shares[0].astype(jnp.bfloat16), "seq").astype(jnp.float32),
        lax.psum(attention_shares[1].astype(jnp.bfloat16), "seq").astype(jnp.float32),
        lax.psum(attention_shares[2].astype(jnp.bfloat16), "seq").astype(jnp.float32),
        lax.psum(attention_shares[3].astype(jnp.bfloat16), "seq").astype(jnp.float32),
        lax.psum(attention_shares[4].astype(jnp.bfloat16), "seq").astype(jnp.float32),
        lax.psum(attention_shares[5].astype(jnp.bfloat16), "seq").astype(jnp.float32),
    )
    return (
        layer_output,
        input_grad,
        grad_entry,
        grad_query,
        grad_key,
        grad_value,
        grad_output,
        grad_attend,
        grad_middle,
        grad_gate,
        grad_up,
        grad_down,
        grad_closing,
    )


def solution(mesh):
    placed = (
        P(("wt", "seq"), None),
        P(("wt", "seq")),
        P("wt"),
        P("wt"),
        P("wt"),
        P("wt", None),
        P("wt", None),
        P("wt", None),
        P("wt", None),
        P("wt"),
        P("wt"),
        P("wt", None),
        P("wt", None),
        P("wt", None),
        P("wt"),
        P(("wt", "seq"), None),
    )
    return jax.shard_map(
        on_device,
        mesh=mesh,
        in_specs=placed,
        out_specs=(
            P(("wt", "seq"), None),
            P(("wt", "seq"), None),
            P("wt"),
            P("wt", None),
            P("wt", None),
            P("wt", None),
            P("wt", None),
            P("wt"),
            P("wt"),
            P("wt", None),
            P("wt", None),
            P("wt", None),
            P("wt"),
        ),
        check_vma=False,
    )
```

profile of v0, /device:TPU:0, one launch (start us, length us, event | category | flops | bytes accessed | tf_op | source)
XLA Modules:
  0.0 1551.1 jit_solution(16358470651031511610)
XLA Ops:
  13.4 22.1 %all-gather = bf16[8,1,128]{2,1,0:T(2,128)(2,1)S(1)} all-gather(bf16[1,1,128]{2,1,0:T(2,128)(2,1)S(1)} %bitcast.245), channel_id=1, replica_groups=mesh['wt'=8,'seq'=4] {'wt'}, dimensions={0}, use_global_device_ids=true | all-gather | bytes 2304 | tf_op jit(solution)/shard_map/all_gather | solution.py:75
  35.5 26.7 %all-gather.14.cloned.1.call-done = bf16[1024,1024]{1,0:T(8,128)(2,1)} async-done(((bf16[128,1024]{1,0:T(8,128)(2,1)}), bf16[1024,1024]{1,0:T(8,128)(2,1)}) %all-gather.14.cloned.1.call-update) | async-done | bytes 2097168 | tf_op jit(solution)/shard_map/all_gather | solution.py:77
  64.7 47.4 %all-gather.12.cloned.1.call-done = bf16[1024,1024]{1,0:T(8,128)(2,1)} async-done(((bf16[128,1024]{1,0:T(8,128)(2,1)}), bf16[1024,1024]{1,0:T(8,128)(2,1)}) %all-gather.12.cloned.1.call-update) | async-done | bytes 2097168 | tf_op jit(solution)/shard_map/all_gather | solution.py:76
  133.1 29.0 %all-gather.16.cloned.1.call-done = bf16[1024,1024]{1,0:T(8,128)(2,1)} async-done(((bf16[128,1024]{1,0:T(8,128)(2,1)}), bf16[1024,1024]{1,0:T(8,128)(2,1)}) %all-gather.16.cloned.1.call-update) | async-done | bytes 2097168 | tf_op jit(solution)/shard_map/all_gather | solution.py:78
  169.8 7.8 all-to-all-done.2
  178.5 13.2 while.27
  196.5 18.1 %all-gather.1 = bf16[8,1,128]{2,1,0:T(2,128)(2,1)S(1)} all-gather(bf16[1,1,128]{2,1,0:T(2,128)(2,1)S(1)} %bitcast.246), channel_id=1, replica_groups=mesh['wt'=8,'seq'=4] {'wt'}, dimensions={0}, use_global_device_ids=true | all-gather | bytes 2304 | tf_op jit(solution)/shard_map/all_gather | solution.py:80
  214.6 16.6 %all-gather.2 = bf16[8,1,128]{2,1,0:T(2,128)(2,1)S(1)} all-gather(bf16[1,1,128]{2,1,0:T(2,128)(2,1)S(1)} %bitcast.247), channel_id=1, replica_groups=mesh['wt'=8,'seq'=4] {'wt'}, dimensions={0}, use_global_device_ids=true | all-gather | bytes 2304 | tf_op jit(solution)/shard_map/all_gather | solution.py:83
  231.2 18.4 %all-gather.3 = bf16[8,1,128]{2,1,0:T(2,128)(2,1)S(1)} all-gather(bf16[1,1,128]{2,1,0:T(2,128)(2,1)S(1)} %bitcast.248), channel_id=1, replica_groups=mesh['wt'=8,'seq'=4] {'wt'}, dimensions={0}, use_global_device_ids=true | all-gather | bytes 2304 | tf_op jit(solution)/shard_map/all_gather | solution.py:87
  253.1 52.1 %all-gather.20.cloned.1.call-done = bf16[1024,2816]{1,0:T(8,128)(2,1)} async-done(((bf16[128,2816]{1,0:T(8,128)(2,1)}), bf16[1024,2816]{1,0:T(8,128)(2,1)}) %all-gather.20.cloned.1.call-update) | async-done | bytes 5767184 | tf_op jit(solution)/shard_map/all_gather | solution.py:84
  311.0 87.1 %all-gather.22.cloned.1.call-done = bf16[1024,2816]{1,0:T(8,128)(2,1)} async-done(((bf16[128,2816]{1,0:T(8,128)(2,1)}), bf16[1024,2816]{1,0:T(8,128)(2,1)}) %all-gather.22.cloned.1.call-update) | async-done | bytes 5767184 | tf_op jit(solution)/shard_map/all_gather | solution.py:85
  405.3 85.8 %all-gather.24.cloned.1.call-done = bf16[2816,1024]{1,0:T(8,128)(2,1)} async-done(((bf16[352,1024]{1,0:T(8,128)(2,1)}), bf16[2816,1024]{1,0:T(8,128)(2,1)}) %all-gather.24.cloned.1.call-update) | async-done | bytes 5767184 | tf_op jit(solution)/shard_map/all_gather | solution.py:86
  518.4 8.8 all-to-all-done.4
  528.0 30.0 %while.28 = (s32[]{:T(128)}, f32[1024,2,128]{0,2,1:T(8,128)}, f32[1024,2,128]{0,2,1:T(8,128)}, bf16[2,512,2,128]{3,1,0,2:T(8,128)(2,1)}, bf16[2,512,2,128]{3,1,2...) while((s32[]{:T(128)}, f32[1024,2,128]{0,2,1:T(8,128)}, ...), condition=%wide.region_13.14_spmd.clone, body=%wide.region_11.13_spmd.clone.sunk | while | flops 1360919552 | bytes 78692648 | solution.py:236
  576.2 8.7 all-to-all-done.5
  595.4 11.2 all_to_all.114
  633.8 56.0 %reduce-scatter.8.cloned.1.call-done = f32[128,1024]{1,0:T(8,128)} async-done(((f32[1024,1024]{1,0:T(8,128)}), f32[128,1024]{1,0:T(8,128)}) %reduce-scatter.8.cloned.1.call-update) | async-done | bytes 524304 | tf_op jit(solution)/shard_map/reduce_scatter | solution.py:274
  691.6 89.4 %reduce-scatter.10.cloned.1.call-done = f32[128,1024]{1,0:T(8,128)} async-done(((f32[1024,1024]{1,0:T(8,128)}), f32[128,1024]{1,0:T(8,128)}) %reduce-scatter.10.cloned.1.call-update) | async-done | bytes 524304 | tf_op jit(solution)/shard_map/reduce_scatter | solution.py:275
  782.8 90.0 %reduce-scatter.12.cloned.1.call-done = f32[128,1024]{1,0:T(8,128)} async-done(((f32[1024,1024]{1,0:T(8,128)}), f32[128,1024]{1,0:T(8,128)}) %reduce-scatter.12.cloned.1.call-update) | async-done | bytes 524304 | tf_op jit(solution)/shard_map/reduce_scatter | solution.py:276
  874.6 194.2 %reduce-scatter.16.cloned.1.call-done = f32[128,2816]{1,0:T(8,128)} async-done(((f32[1024,2816]{1,0:T(8,128)}), f32[128,2816]{1,0:T(8,128)}) %reduce-scatter.16.cloned.1.call-update) | async-done | bytes 1441808 | tf_op jit(solution)/shard_map/reduce_scatter | solution.py:181
  1071.0 193.1 %reduce-scatter.18.cloned.1.call-done = f32[128,2816]{1,0:T(8,128)} async-done(((f32[1024,2816]{1,0:T(8,128)}), f32[128,2816]{1,0:T(8,128)}) %reduce-scatter.18.cloned.1.call-update) | async-done | bytes 1441808 | tf_op jit(solution)/shard_map/reduce_scatter | solution.py:182
  1266.4 193.0 %reduce-scatter.20.cloned.1.call-done = f32[352,1024]{1,0:T(8,128)} async-done(((f32[2816,1024]{1,0:T(8,128)}), f32[352,1024]{1,0:T(8,128)}) %reduce-scatter.20.cloned.1.call-update) | async-done | bytes 1441808 | tf_op jit(solution)/shard_map/reduce_scatter | solution.py:183
  1467.5 35.1 %all-reduce.4 = (bf16[1024]{0:T(1024)(128)(2,1)S(1)}, bf16[1024]{0:T(1024)(128)(2,1)S(1)}, bf16[1024]{0:T(1024)(128)(2,1)S(1)}, bf16[1024]{0:T(1024)(128)(2,1)S(1)}) all-reduce(f32[1024]{0:T(1024)S(1)} %get-tuple-element.303, f32[1024]{0:T(1024)S(1)} %get-tuple-element.299, ...), channel_id=2, replica_groups=mesh['wt'=8,'seq'=4] {'wt'}, use_global_device_ids=true, to_apply=%region_16.17.clone | all-reduce | flops 4096 | bytes 24576
  1512.3 20.8 %all-reduce.9.cloned.1.call-done = (bf16[128,1024]{1,0:T(8,128)(2,1)}, bf16[128,1024]{1,0:T(8,128)(2,1)}, bf16[128,1024]{1,0:T(8,128)(2,1)}, bf16[128,1024]{1,0:...) async-done(((bf16[128,1024]{1,0:T(8,128)(2,1)}, bf16[128,1024]{1,0:T(8,128)(2,1)}, bf16[128,1024]{1,0:T(8,128)(2,1)}, ...) | async-done | bytes 3211280 | tf_op jit(solution)/shard_map/psum | solution.py:282
  (301 shorter events, 223.8 us)
Async XLA Ops:
  7.2 55.0 %all-gather.14.cloned.1.call-start = ((), (), s32[]{:S(2)}) async-start(), calls=%async_computation.16 | async-start | bytes 2359296 | tf_op jit(solution)/shard_map/all_gather | solution.py:77
  7.9 104.2 %all-gather.12.cloned.1.call-start = ((), (), s32[]{:S(2)}) async-start(), calls=%async_computation.15 | async-start | bytes 2359296 | tf_op jit(solution)/shard_map/all_gather | solution.py:76
  8.7 153.4 %all-gather.16.cloned.1.call-start = ((), (), s32[]{:S(2)}) async-start(), calls=%async_computation.17 | async-start | bytes 2359296 | tf_op jit(solution)/shard_map/all_gather | solution.py:78
  9.4 240.5 %all-gather.18.cloned.1.call-start = ((), (), s32[]{:S(2)}) async-start(), calls=%async_computation.18 | async-start | bytes 2359296 | tf_op jit(solution)/shard_map/all_gather | solution.py:79
  10.0 295.2 %all-gather.20.cloned.1.call-start = ((), (), s32[]{:S(2)}) async-start(), calls=%async_computation.19 | async-start | bytes 6488064 | tf_op jit(solution)/shard_map/all_gather | solution.py:84
  10.6 387.5 %all-gather.22.cloned.1.call-start = ((), (), s32[]{:S(2)}) async-start(), calls=%async_computation.20 | async-start | bytes 6488064 | tf_op jit(solution)/shard_map/all_gather | solution.py:85
  11.2 479.9 %all-gather.24.cloned.1.call-start = ((), (), s32[]{:S(2)}) async-start(), calls=%async_computation.21 | async-start | bytes 6488064 | tf_op jit(solution)/shard_map/all_gather | solution.py:86
  117.3 12.3 all-to-all-start
  129.6 35.7 %all-to-all-start.1 = ((bf16[256,8,128]{2,0,1:T(8,128)(2,1)}), bf16[256,8,128]{2,0,1:T(8,128)(2,1)S(1)}, u32[]{:S(2)}, u32[]{:S(2)}) async-start(bf16[256,8,128]{2,0,1:T(8,128)(2,1)} %pad_maximum_fusion.1), calls=%async_computation.1 | async-start | bytes 1048576 | tf_op jit(solution)/shard_map/all_to_all | solution.py:111
  165.3 12.3 all-to-all-start.2
  193.0 56.6 %all-to-all-start.3 = ((bf16[1024,2,128]{2,1,0:T(2,128)(2,1)}), bf16[1024,2,128]{2,1,0:T(2,128)(2,1)S(1)}, u32[]{:S(2)}, u32[]{:S(2)}) async-start(bf16[1024,2,128]{2,1,0:T(2,128)(2,1)} %copy.129), calls=%async_computation.3 | async-start | bytes 1048576 | tf_op jit(solution)/shard_map/all_to_all | solution.py:140
  196.5 435.6 %reduce-scatter.14.cloned.1.call-start = ((), (), s32[]{:S(2)}) async-start(), calls=%async_computation.25 | async-start | bytes 4718592 | tf_op jit(solution)/shard_map/reduce_scatter | solution.py:277
  514.9 12.3 all-to-all-start.4
  560.3 12.3 all-to-all-start.6
  572.6 12.3 all-to-all-start.5
  576.1 113.8 %reduce-scatter.8.cloned.1.call-start = ((), (), s32[]{:S(2)}) async-start(), calls=%async_computation.22 | async-start | bytes 4718592 | tf_op jit(solution)/shard_map/reduce_scatter | solution.py:274
  589.8 191.2 %reduce-scatter.10.cloned.1.call-start = ((), (), s32[]{:S(2)}) async-start(), calls=%async_computation.23 | async-start | bytes 4718592 | tf_op jit(solution)/shard_map/reduce_scatter | solution.py:275
  593.6 279.2 %reduce-scatter.12.cloned.1.call-start = ((), (), s32[]{:S(2)}) async-start(), calls=%async_computation.24 | async-start | bytes 4718592 | tf_op jit(solution)/shard_map/reduce_scatter | solution.py:276
  609.8 458.9 %reduce-scatter.16.cloned.1.call-start = ((), (), s32[]{:S(2)}) async-start(), calls=%async_computation.26 | async-start | bytes 12976128 | tf_op jit(solution)/shard_map/reduce_scatter | solution.py:181
  617.3 646.9 %reduce-scatter.18.cloned.1.call-start = ((), (), s32[]{:S(2)}) async-start(), calls=%async_computation.27 | async-start | bytes 12976128 | tf_op jit(solution)/shard_map/reduce_scatter | solution.py:182
  624.6 834.8 %reduce-scatter.20.cloned.1.call-start = ((), (), s32[]{:S(2)}) async-start(), calls=%async_computation.28 | async-start | bytes 12976128 | tf_op jit(solution)/shard_map/reduce_scatter | solution.py:183
  632.0 901.1 %all-reduce.9.cloned.1.call-start = ((), (), s32[]{:S(2)}) async-start(), calls=%async_computation.29 | async-start | bytes 6422528 | tf_op jit(solution)/shard_map/psum | solution.py:282
  1266.4 195.3 %copy-start.48 = (u32[32]{0:T(128)S(1)}, u32[32]{0:T(128)}, u32[]{:S(2)}) copy-start(u32[32]{0:T(128)} %constant.75) | copy-start | bytes 388
  1266.4 196.6 %copy-start.6 = (bf16[1024,1024]{1,0:T(8,128)(2,1)S(1)}, bf16[1024,1024]{1,0:T(8,128)(2,1)}, u32[]{:S(2)}) copy-start(bf16[1024,1024]{1,0:T(8,128)(2,1)} %all-gather.12.cloned.1.call-done) | copy-start | bytes 6291460
  (58 other events, 916.6 us)
Sparse Core Ops, SparseCore 0:
  10.2 51.9 all-gather.13
  64.3 47.7 all-gather.11
  114.3 47.7 all-gather.15
  164.0 47.7 all-gather.17
  213.9 91.1 all-gather.19
  307.2 90.8 all-gather.21
  400.2 90.8 all-gather.23
  511.8 86.2 reduce-scatter.13
  602.2 87.6 reduce-scatter.7
  693.3 87.6 reduce-scatter.9
  785.1 87.6 reduce-scatter.11
  876.2 192.4 reduce-scatter.15
  1072.3 191.7 reduce-scatter.17
  1267.6 191.7 reduce-scatter.19
  1463.3 69.8 all-reduce.8
where the time goes:
time: 1560 us; the launch traced here: 1550 us
  waiting for transfers between devices  1210 us (78%)
  blocking collectives  128 us (8%)
  matrix products  103 us (7%)
  other arithmetic  44.7 us (3%)
  starting transfers between devices  25.2 us (2%)
  local copies, waits for them, and re-layouts  24.8 us (2%)
  between operations  15.9 us (1%)
    reduce_scatter x1, waiting for transfers between devices, on_device(): lax.psum_scatter(gate_local, 'wt', scatter_dimension=0, tiled=True)  194 us
    reduce_scatter x1, waiting for transfers between devices, on_device(): lax.psum_scatter(up_local, 'wt', scatter_dimension=0, tiled=True)  193 us
    reduce_scatter x1, waiting for transfers between devices, on_device(): lax.psum_scatter(down_local, 'wt', scatter_dimension=0, tiled=True)  193 us
    reduce_scatter x1, waiting for transfers between devices, on_device(): lax.psum_scatter(value_local, 'wt', scatter_dimension=0, tiled=True)  90 us
    reduce_scatter x1, waiting for transfers between devices, on_device(): lax.psum_scatter(key_local, 'wt', scatter_dimension=0, tiled=True)  89.4 us
    all_gather x1, waiting for transfers between devices, on_device(): lax.all_gather(up_weight, 'wt', axis=0, tiled=True)  87.1 us
    all_gather x1, waiting for transfers between devices, on_device(): lax.all_gather(down_weight, 'wt', axis=0, tiled=True)  85.8 us
    reduce_scatter x1, waiting for transfers between devices, on_device(): lax.psum_scatter(query_local, 'wt', scatter_dimension=0, tiled=True)  56 us
  transfers between devices with their start and end apart: 22, of which 18 were waited for; matrix products, arithmetic and copies ran while one was open for 8% of the time, Pallas kernels for 0%

commit v1 on v0

v1 whole, which is shorter than its diff:
```python
import functools

import jax
import jax.numpy as jnp
from jax import lax
from jax.experimental import pallas as pl
from jax.experimental.pallas import tpu as pltpu
from jax.sharding import PartitionSpec as P

HEADS = 8
EPSILON = 1e-06
ROTARY_BASE = 50000.0
DOC_LEN = 8192
DOC_STRIDE = 64
HIDDEN_LOW = -1e30
LOG2_E = 1.4426950408889634
SEQ = 4

f32 = jnp.float32
bf16 = jnp.bfloat16


def norm_rows(values, scales):
    inverse = lax.rsqrt(jnp.mean(values * values, -1, keepdims=True) + EPSILON)
    normed = values * inverse
    return (normed * scales, normed, inverse)


def norm_back(incoming, normed, inverse, scales):
    scaled = incoming * scales
    input_side = inverse * (scaled - normed * jnp.mean(scaled * normed, -1, keepdims=True))
    return (input_side, jnp.sum(incoming * normed, 0))


def dot(left, right):
    return jnp.dot(left, right, preferred_element_type=f32)


def dot_nt(left, right):
    return lax.dot_general(left, right, (((1,), (1,)), ((), ())), preferred_element_type=f32)


def dot_tn(left, right):
    return lax.dot_general(left, right, (((0,), (0,)), ((), ())), preferred_element_type=f32)


def swap(value, bit):
    return lax.ppermute(value, "seq", [(i, i ^ bit) for i in range(SEQ)])


def gather_blocks(own):
    far = swap(own, 2)
    near = swap(own, 1)
    return own, near, far, swap(far, 1)


def turn(rows, cosine, sine):
    return rows * cosine + pltpu.roll(rows, rows.shape[-1] // 2, axis=1) * sine


def visible(key_code, query_code, tile):
    key_wide = jnp.concatenate([key_code] * (tile // 128), axis=1)
    return (key_wide <= query_code[0:1, :]) & (key_wide >= query_code[1:2, :])


def attend_forward(
    low_ref, weight_ref, cos_ref, sin_ref, key_code_ref, query_code_ref,
    query_ref, key_ref, value_ref, out_ref, log_ref,
):
    window = low_ref.shape[0]
    tiles, _, tile = query_code_ref.shape
    width = cos_ref.shape[1]
    heads = query_ref.shape[1] // width
    scale = LOG2_E * width ** (-0.5)

    def project(step, carry):
        rows = pl.ds(pl.multiple_of(step * tile, tile), tile)
        raw = dot(low_ref[rows, :], weight_ref[...])
        cosine = cos_ref[rows, :]
        sine = sin_ref[rows, :]
        for head in range(heads):
            at = head * width
            query_ref[rows, at:at + width] = turn(raw[:, at:at + width], cosine, sine).astype(bf16)
            at = (heads + head) * width
            key_ref[rows, head * width:(head + 1) * width] = turn(
                raw[:, at:at + width], cosine, sine
            ).astype(bf16)
        value_ref[rows, :] = raw[:, 2 * heads * width:].astype(bf16)
        return carry

    lax.fori_loop(0, window // tile, project, 0)
    for head in range(heads):
        cols = slice(head * width, (head + 1) * width)
        value_turned = value_ref[:, cols].astype(f32).T.astype(bf16)

        def one_tile(step, carry):
            rows = pl.ds(pl.multiple_of(step * tile, tile), tile)
            scores = dot_nt(key_ref[:, cols], query_ref[rows, cols])
            shown = visible(key_code_ref[...], query_code_ref[step], tile)
            scores = jnp.where(shown, scores * scale, HIDDEN_LOW)
            top = jnp.max(scores, 0, keepdims=True)
            weights = jnp.exp2(scores - top)
            total = jnp.sum(weights, 0, keepdims=True)
            result = dot(value_turned, weights.astype(bf16)) * (1.0 / total)
            out_ref[rows, cols] = result.T.astype(bf16)
            log_ref[head, step] = jnp.broadcast_to(top + jnp.log2(total), (8, tile))
            return carry

        lax.fori_loop(0, tiles, one_tile, 0)


def attend_backward(
    query_ref, key_ref, value_ref, incoming_ref, log_ref, cos_ref, sin_ref,
    key_code_ref, query_code_ref,
    grad_ref, key_sum, value_sum,
):
    tiles, _, tile = query_code_ref.shape
    width = cos_ref.shape[1]
    heads = query_ref.shape[1] // width
    factor = width ** (-0.5)
    scale = LOG2_E * factor
    for head in range(heads):
        cols = slice(head * width, (head + 1) * width)
        key_turned = key_ref[:, cols].astype(f32).T.astype(bf16)
        key_sum[...] = jnp.zeros_like(key_sum)
        value_sum[...] = jnp.zeros_like(value_sum)

        def one_tile(step, carry):
            rows = pl.ds(pl.multiple_of(step * tile, tile), tile)
            queries = query_ref[rows, cols]
            incoming = incoming_ref[rows, cols]
            scores = dot_nt(key_ref[:, cols], queries)
            shown = visible(key_code_ref[...], query_code_ref[step], tile)
            probs = jnp.where(shown, jnp.exp2(scores * scale - log_ref[head, step, 0:1, :]), 0.0)
            value_sum[...] += dot(probs.astype(bf16), incoming)
            prob_grad = dot_nt(value_ref[:, cols], incoming)
            inner = jnp.sum(probs * prob_grad, 0, keepdims=True)
            score_grad = (probs * (prob_grad - inner)).astype(bf16)
            key_sum[...] += dot(score_grad, queries)
            query_grad = (dot(key_turned, score_grad) * factor).T
            grad_ref[rows, cols] = turn(query_grad, cos_ref[rows, :], -sin_ref[rows, :]).astype(bf16)
            return carry

        lax.fori_loop(0, tiles, one_tile, 0)
        at = (heads + head) * width
        grad_ref[:, at:at + width] = turn(
            key_sum[...] * factor, cos_ref[...], -sin_ref[...]
        ).astype(bf16)
        at = (2 * heads + head) * width
        grad_ref[:, at:at + width] = value_sum[...].astype(bf16)


def on_device(
    tokens, positions, doc_ids, block_ids, entry_gain, query_weight, key_weight, value_weight,
    output_weight, attend_gain, middle_gain, gate_weight, up_weight, down_weight, closing_gain,
    cotangent,
):
    place = lax.axis_index("seq")
    order = [place ^ step for step in range(SEQ)]
    rows, model = tokens.shape
    window = rows * SEQ
    wt = model // query_weight.shape[0]
    shard = query_weight.shape[0]
    part = model // SEQ
    width = model // HEADS
    heads = HEADS // SEQ
    hidden = gate_weight.shape[1]
    chunk = hidden // (wt * SEQ)
    padded = (hidden // SEQ + 255) // 256 * 256 // wt
    hidden_part = padded * wt

    def by_order(stacked, axis):
        return [lax.dynamic_index_in_dim(stacked, at, axis, keepdims=False) for at in order]

    def restore(blocks):
        stacked = jnp.stack(blocks)
        return [lax.dynamic_index_in_dim(stacked, place ^ at, 0, keepdims=False) for at in range(SEQ)]

    def quarter(weight):
        return lax.dynamic_slice_in_dim(weight, place * part, part, axis=1)

    attention_part = jnp.concatenate(
        [quarter(query_weight), quarter(key_weight), quarter(value_weight), quarter(output_weight)], 1
    )
    down_own = lax.dynamic_slice_in_dim(down_weight, place * chunk, chunk, axis=0)
    down_own = jnp.pad(down_own, ((0, padded - chunk), (0, 0)))
    first = lax.all_gather(jnp.concatenate([attention_part, down_own], 0), "wt", axis=0, tiled=False)

    def hidden_columns(weight):
        split = lax.dynamic_index_in_dim(
            weight.reshape(shard, wt, SEQ, chunk), place, 2, keepdims=False
        )
        return jnp.pad(split, ((0, 0), (0, 0), (0, padded - chunk))).reshape(shard, hidden_part)

    gate_up = lax.all_gather(
        jnp.concatenate([hidden_columns(gate_weight), hidden_columns(up_weight)], 1),
        "wt", axis=0, tiled=True,
    )
    gains = lax.all_gather(
        jnp.stack([entry_gain, attend_gain, middle_gain, closing_gain]), "wt", axis=1, tiled=True
    ).astype(f32)
    entry_full, attend_full, middle_full, closing_full = [gains[at:at + 1] for at in range(4)]

    token_blocks = jnp.concatenate(gather_blocks(tokens), 0)

    offsets = jnp.arange(window, dtype=jnp.int32)
    leading = doc_ids == doc_ids[0]
    boundary = jnp.sum(leading.astype(jnp.int32))
    places = jnp.where(leading, DOC_LEN - boundary + offsets, offsets - boundary)
    codes = doc_ids * DOC_STRIDE + block_ids
    lows = doc_ids * DOC_STRIDE
    packed = jnp.stack([places, codes, lows]).reshape(3, SEQ, rows)
    packed = jnp.concatenate(by_order(packed, 1), 1)
    half = width // 2
    frequency = ROTARY_BASE ** (-2.0 * jnp.arange(half, dtype=f32) / width)
    angles = packed[0].astype(f32)[:, None] * frequency[None, :]
    cosine = jnp.cos(angles)
    sine = jnp.sin(angles)
    cosine = jnp.concatenate([cosine, cosine], 1)
    sine = jnp.concatenate([-sine, sine], 1)
    key_code = jnp.broadcast_to(packed[1][:, None], (window, 128))
    query_code = jnp.broadcast_to(
        packed[1:3].reshape(2, SEQ, rows).transpose(1, 0, 2)[:, :, None, :], (SEQ, 2, 4, rows)
    ).transpose(0, 2, 1, 3).reshape(SEQ, 8, rows)

    all_inputs = token_blocks.astype(f32)
    entry_out, _, _ = norm_rows(all_inputs, entry_full)
    entry_low = entry_out.astype(bf16)
    qkv_weight = first[:, :shard, :3 * part].reshape(model, 3 * part)
    output_own = first[:, :shard, 3 * part:].reshape(model, part)
    down_part = first[:, shard:, :].reshape(hidden_part, model)
    output_full = jnp.concatenate(restore(gather_blocks(output_own)), 1)

    any_vmem = pl.BlockSpec(memory_space=pltpu.VMEM)
    params = pltpu.CompilerParams(vmem_limit_bytes=50 * 1024 * 1024)
    low_shape = jax.ShapeDtypeStruct((window, heads * width), bf16)
    query_low, key_low, value_low, attended, log_totals = pl.pallas_call(
        attend_forward,
        out_shape=(
            low_shape, low_shape, low_shape, low_shape,
            jax.ShapeDtypeStruct((heads, SEQ, 8, rows), f32),
        ),
        in_specs=[any_vmem] * 6,
        out_specs=(any_vmem,) * 5,
        compiler_params=params,
        name="attend_forward",
    )(entry_low, qkv_weight, cosine, sine, key_code, query_code)

    def exchange(blocks):
        return [blocks[0], swap(blocks[1], 1), swap(blocks[2], 2), swap(blocks[3], 3)]

    attended_tokens = jnp.concatenate(
        restore(exchange([attended[at * rows:(at + 1) * rows] for at in range(SEQ)])), 1
    )
    inputs = tokens.astype(f32)
    mixed = dot(attended_tokens, output_full)
    attend_out, attend_normed, attend_inverse = norm_rows(mixed, attend_full)
    hidden_state = inputs + attend_out
    middle_out, middle_normed, middle_inverse = norm_rows(hidden_state, middle_full)
    middle_low = middle_out.astype(bf16)

    def halves(own):
        blocks = gather_blocks(own)
        return jnp.concatenate(blocks[:2], 0), jnp.concatenate(blocks[2:], 0)

    def reduce_blocks(near_pair, far_pair):
        far_sum = far_pair[:rows] + swap(far_pair[rows:].astype(bf16), 1).astype(f32)
        far_got = swap(far_sum.astype(bf16), 2)
        near_sum = near_pair[:rows] + swap(near_pair[rows:].astype(bf16), 1).astype(f32)
        return near_sum + far_got.astype(f32)

    def feed(low_rows):
        both = dot(low_rows, gate_up)
        gate_value = both[:, :hidden_part]
        up_value = both[:, hidden_part:]
        sigmoid_gate = jax.nn.sigmoid(gate_value)
        activated = (gate_value * sigmoid_gate * up_value).astype(bf16)
        return gate_value, up_value, sigmoid_gate, activated, dot(activated, down_part)

    middle_halves = halves(middle_low)
    fed = [feed(low_rows) for low_rows in middle_halves]
    channel_out = reduce_blocks(fed[0][4], fed[1][4])
    closing_out, closing_normed, closing_inverse = norm_rows(channel_out, closing_full)
    layer_output = (hidden_state + closing_out).astype(bf16)
    incoming = cotangent.astype(f32)
    channel_grad, closing_local = norm_back(incoming, closing_normed, closing_inverse, closing_full)
    channel_halves = halves(channel_grad.astype(bf16))

    def feed_back(channel_rows, saved):
        gate_value, up_value, sigmoid_gate, _, _ = saved
        active_grad = dot_nt(channel_rows, down_part)
        gate_grad = (
            active_grad * up_value * sigmoid_gate * (1.0 + gate_value * (1.0 - sigmoid_gate))
        ).astype(bf16)
        up_grad = (active_grad * gate_value * sigmoid_gate).astype(bf16)
        both_grad = jnp.concatenate([gate_grad, up_grad], 1)
        return both_grad, dot_nt(both_grad, gate_up)

    backs = [feed_back(channel_halves[at], fed[at]) for at in range(2)]
    middle_grad = reduce_blocks(backs[0][1], backs[1][1])
    gate_up_local = dot_tn(middle_halves[0], backs[0][0]) + dot_tn(middle_halves[1], backs[1][0])
    gate_up_share = lax.psum_scatter(
        gate_up_local.astype(bf16), "wt", scatter_dimension=0, tiled=True
    )
    down_local = dot_tn(fed[0][3], channel_halves[0]) + dot_tn(fed[1][3], channel_halves[1])

    hidden_back, middle_local = norm_back(middle_grad, middle_normed, middle_inverse, middle_full)
    hidden_grad = incoming + hidden_back
    mixed_grad, attend_local = norm_back(hidden_grad, attend_normed, attend_inverse, attend_full)
    mixed_low = mixed_grad.astype(bf16)
    attended_grad = dot_nt(mixed_low, output_full).astype(bf16)
    attended_back = jnp.concatenate(
        exchange(by_order(attended_grad.reshape(rows, SEQ, part), 1)), 0
    )
    output_local = dot_tn(attended_tokens, mixed_low)
    output_blocks = by_order(output_local.reshape(model, SEQ, part), 1)
    output_share = reduce_output(output_blocks)

    qkv_grad = pl.pallas_call(
        attend_backward,
        out_shape=jax.ShapeDtypeStruct((window, 3 * part), bf16),
        in_specs=[any_vmem] * 9,
        out_specs=any_vmem,
        scratch_shapes=[pltpu.VMEM((window, width), f32), pltpu.VMEM((window, width), f32)],
        compiler_params=params,
        name="attend_backward",
    )(query_low, key_low, value_low, attended_back, log_totals, cosine, sine, key_code, query_code)

    entry_pairs = [
        dot_nt(qkv_grad[:2 * rows], qkv_weight), dot_nt(qkv_grad[2 * rows:], qkv_weight)
    ]
    entry_grad = reduce_blocks(entry_pairs[0], entry_pairs[1])
    qkv_local = dot_tn(entry_low, qkv_grad)
    _, entry_normed, entry_inverse = norm_rows(inputs, entry_full)
    input_back, entry_local = norm_back(entry_grad, entry_normed, entry_inverse, entry_full)
    input_grad = hidden_grad + input_back

    gain_rows = jnp.stack([entry_local, attend_local, middle_local, closing_local])
    gain_rows = gain_rows.reshape(4, wt, shard).transpose(1, 0, 2).reshape(wt, 1, 4 * shard)
    gain_rows = jnp.pad(gain_rows, ((0, 0), (0, 7), (0, model - 4 * shard)))
    last = jnp.concatenate(
        [
            jnp.concatenate([qkv_local.astype(bf16), output_share.astype(bf16)], 1).reshape(
                wt, shard, model
            ),
            down_local.astype(bf16).reshape(wt, padded, model),
            gain_rows.astype(bf16),
        ],
        1,
    )
    last_share = lax.psum_scatter(last, "wt", scatter_dimension=0, tiled=False)

    gate_up_blocks = restore(gather_blocks(gate_up_share))
    last_blocks = restore(gather_blocks(last_share))

    def hidden_restore(at):
        blocks = jnp.stack(
            [
                block[:, at * hidden_part:(at + 1) * hidden_part].reshape(shard, wt, padded)[
                    :, :, :chunk
                ]
                for block in gate_up_blocks
            ],
            2,
        )
        return blocks.reshape(shard, hidden).astype(f32)

    def columns(at):
        return jnp.concatenate(
            [block[:shard, at * part:(at + 1) * part] for block in last_blocks], 1
        ).astype(f32)

    grad_down = jnp.concatenate(
        [block[shard:shard + chunk] for block in last_blocks], 0
    ).astype(f32)
    gain_sums = sum(block[shard + padded].astype(f32) for block in last_blocks)
    grad_entry, grad_attend, grad_middle, grad_closing = [
        gain_sums[at * shard:(at + 1) * shard] for at in range(4)
    ]
    return (
        layer_output, input_grad, grad_entry, columns(0), columns(1), columns(2), columns(3),
        grad_attend, grad_middle, hidden_restore(0), hidden_restore(1), grad_down, grad_closing,
    )


def reduce_output(blocks):
    far_sum = blocks[2] + swap(blocks[3].astype(bf16), 1).astype(f32)
    far_got = swap(far_sum.astype(bf16), 2)
    near_sum = blocks[0] + swap(blocks[1].astype(bf16), 1).astype(f32)
    return near_sum + far_got.astype(f32)


def solution(mesh):
    rows = P(("wt", "seq"), None)
    weight = P("wt", None)
    gain = P("wt")
    return jax.shard_map(
        on_device,
        mesh=mesh,
        in_specs=(
            rows, P(("wt", "seq")), gain, gain, gain, weight, weight, weight, weight, gain, gain,
            weight, weight, weight, gain, rows,
        ),
        out_specs=(
            rows, rows, gain, weight, weight, weight, weight, gain, gain, weight, weight, weight,
            gain,
        ),
        check_vma=False,
    )
```

time: 1560 us -> 406 us (0.26)
  waiting for transfers between devices: 1210 us -> 208 us
  blocking collectives: 128 us -> 21 us
  matrix products: 103 us -> 32.9 us
  Pallas kernels: 0 us -> 24 us
    reduce_scatter x7 -> x2, waiting for transfers between devices: 816 us -> 65.3 us  [the longest x1 65.3 us: on_device(): last_share = lax.psum_scatter(last, 'wt', scatter_dimension=0, tiled=False)]
    all_gather x7 -> x2, waiting for transfers between devices: 328 us -> 46.4 us  [the longest x1 31.4 us: on_device(): lax.all_gather(jnp.concatenate([attention_part, down_own], 0), 'wt', axis...]
    ppermute x0 -> x36, waiting for transfers between devices: none -> 96.1 us  [swap(): return lax.ppermute(value, 'seq', [(i, i ^ bit) for i in range(SEQ)])]
    dot_general x35 -> x18, matrix products: 103 us -> 32.9 us  [the longest x6 12.6 us: dot_tn(): lax.dot_general(left, right, (((0,), (0,)), ((), ())), preferred_element_...]
    all_gather x4 -> x1, blocking collectives: 75.1 us -> 21 us  [on_device(): lax.all_gather(jnp.stack([entry_gain, attend_gain, middle_gain, closing_g...]
    all_to_all x7 -> x0, waiting for transfers between devices: 40.5 us -> none  [the longest x1 8.78 us: on_device(): lax.all_to_all(attended_grad.reshape(head_shape), 'seq', split_axis=1, co...]
    unnamed x1 -> x0, blocking collectives: 35.1 us -> none
    all_to_all x7 -> x0, starting transfers between devices: 24.3 us -> none  [the longest x1 3.49 us: on_device(): lax.all_to_all(attended_grad.reshape(head_shape), 'seq', split_axis=1, co...]
  transfers between devices with their start and end apart: 22 -> 40, of which waited for: 18 -> 17; matrix products, arithmetic and copies ran while one was open for 8% -> 21% of each run, Pallas kernels for 0% -> 6%
where the time goes in v1:
time: 406 us; the launch traced here: 400 us
  waiting for transfers between devices  208 us (51%)
  local copies, waits for them, and re-layouts  38 us (9%)
  other arithmetic  37.5 us (9%)
  matrix products  32.9 us (8%)
  Pallas kernels  24 us (6%)
  starting transfers between devices  22.1 us (5%)
  blocking collectives  21 us (5%)
  between operations  16 us (4%)
    ppermute x36, waiting for transfers between devices, swap(): return lax.ppermute(value, 'seq', [(i, i ^ bit) for i in range(SEQ)])  96.1 us
    reduce_scatter x1, waiting for transfers between devices, on_device(): last_share = lax.psum_scatter(last, 'wt', scatter_dimension=0, tiled=False)  65.3 us
    all_gather x1, waiting for transfers between devices, on_device(): lax.all_gather(jnp.concatenate([attention_part, down_own], 0), 'wt', axis...  31.4 us
    ppermute x36, starting transfers between devices, swap(): return lax.ppermute(value, 'seq', [(i, i ^ bit) for i in range(SEQ)])  21.7 us
    all_gather x1, blocking collectives, on_device(): lax.all_gather(jnp.stack([entry_gain, attend_gain, middle_gain, closing_g...  21 us
    unnamed x131, local copies, waits for them, and re-layouts  16.6 us
    all_gather x1, waiting for transfers between devices, on_device(): lax.all_gather(jnp.concatenate([hidden_columns(gate_weight), hidden_colum...  15 us
    dot_general x6, matrix products, dot_tn(): lax.dot_general(left, right, (((0,), (0,)), ((), ())), preferred_element_...  12.6 us
  transfers between devices with their start and end apart: 40, of which 17 were waited for; matrix products, arithmetic and copies ran while one was open for 21% of the time, Pallas kernels for 6%

profile of v1, /device:TPU:0, one launch (start us, length us, event | category | flops | bytes accessed | tf_op | source)
XLA Modules:
  0.0 399.5 jit_solution(6087490470085358057)
XLA Ops:
  11.1 3.0 collective-permute-start.1
  22.2 3.9 collective-permute-done.1
  26.1 21.0 %all_gather.12 = bf16[4,1024]{1,0:T(4,128)(2,1)S(1)} all-gather(bf16[4,128]{1,0:T(4,128)(2,1)S(1)} %pad_maximum_fusion.30), channel_id=1, replica_groups=mesh['wt'=8,'seq'=4] {'wt'}, dimensions={1}, use_global_device_ids=true | all-gather | bytes 9216 | tf_op jit(solution)/shard_map/all_gather | solution.py:199
  49.3 31.4 %all-gather.6.cloned.1.call-done = bf16[1792,1024]{1,0:T(8,128)(2,1)} async-done(((bf16[224,1024]{1,0:T(8,128)(2,1)}), bf16[1792,1024]{1,0:T(8,128)(2,1)}) %all-gather.6.cloned.1.call-update) | async-done | bytes 3670032 | tf_op jit(solution)/shard_map/all_gather | solution.py:187
  83.4 3.2 fusion.3.low_ref
  88.1 11.9 %attend_forward.1 = (bf16[1024,256]{1,0:T(8,128)(2,1)S(1)}, bf16[1024,256]{1,0:T(8,128)(2,1)S(1)}, bf16[1024,256]{1,0:T(8,128)(2,1)S(1)}, bf16[1024,256]{1,0:T(8,128)(2,1)S(1)}, f32[2,4,8,256]{3,2,1,0:T(8,128)S(1)}) custom-call(bf16[1024,1024]{1,0:T(8,128)(2,1)} %fusion.3.low_ref, bf16[1024,768]{1,0:T(8,128)(2,1)} %bitcast.201, ...), custom_call_target="tpu_custom_call" | custom-call | tf_op jit(solution)/shard_map/attend_forward/pallas_call | solution.py:237
  102.5 3.7 collective-permute-done.5
  106.2 3.0 collective-permute-done.4
  115.6 12.4 %collective-permute-done.11 = bf16[256,1024]{1,0:T(8,128)(2,1)} collective-permute-done((bf16[256,1024]{1,0:T(8,128)(2,1)}, bf16[256,1024]{1,0:T(8,128)(2,1)}, u32[]{:S(2)}, u32[]{:S(2)}) %collective-permute-start.11) | collective-permute-done | bytes 524320 | tf_op jit(solution)/shard_map/ppermute | solution.py:48
  129.9 15.0 %all-gather.4.cloned.1.call-done = bf16[1024,1536]{0,1:T(8,128)(2,1)} async-done(((bf16[128,1536]{0,1:T(8,128)(2,1)}), bf16[1024,1536]{0,1:T(8,128)(2,1)}) %all-gather.4.cloned.1.call-update) | async-done | bytes 3145744 | tf_op jit(solution)/shard_map/all_gather | solution.py:195
  144.9 4.2 %fusion.39 = f32[512,1536]{1,0:T(8,128)S(1)} fusion(bf16[1024,1536]{0,1:T(8,128)(2,1)} %all-gather.4.cloned.1.call-done, bf16[256,1024]{1,0:T(8,128)(2,1)} %collective-permute-done.9, bf16[256,1024]{1,0:T(8,128)(2,1)} %multiply_convert_fusion.7), kind=kOutput, calls=%fused_computation.104 | convolution fusion | flops 1612709888 | bytes 7340032 | tf_op jit(solution)/shard_map/dot_general | solution.py:36
  158.5 12.4 %collective-permute-done.14 = bf16[256,1024]{1,0:T(8,128)(2,1)S(1)} collective-permute-done((bf16[256,1024]{1,0:T(8,128)(2,1)S(1)}, bf16[256,1024]{1,0:T(8,128)(2,1)S(1)}, u32[]{:S(2)}, u32[]{:S(2)}) %collective-permute-start.14) | collective-permute-done | bytes 524320 | tf_op jit(solution)/shard_map/ppermute | solution.py:48
  174.3 11.5 %collective-permute-done.17 = bf16[256,1024]{1,0:T(8,128)(2,1)S(1)} collective-permute-done((bf16[256,1024]{1,0:T(8,128)(2,1)S(1)}, bf16[256,1024]{1,0:T(8,128)(2,1)S(1)}, u32[]{:S(2)}, u32[]{:S(2)}) %collective-permute-start.17) | collective-permute-done | bytes 524320 | tf_op jit(solution)/shard_map/ppermute | solution.py:48
  192.2 3.0 fusion.30
  200.7 3.7 add_convert_fusion
  211.3 9.6 %collective-permute-done.20 = bf16[256,1024]{1,0:T(8,128)(2,1)S(1)} collective-permute-done((bf16[256,1024]{1,0:T(8,128)(2,1)S(1)}, bf16[256,1024]{1,0:T(8,128)(2,1)S(1)}, u32[]{:S(2)}, u32[]{:S(2)}) %collective-permute-start.20) | collective-permute-done | bytes 524320 | tf_op jit(solution)/shard_map/ppermute | solution.py:48
  230.1 2.9 constant_dynamic-slice_fusion.7
  241.8 12.2 %attend_backward.1 = bf16[1024,768]{1,0:T(8,128)(2,1)} custom-call(bf16[1024,256]{1,0:T(8,128)(2,1)S(1)} %get-tuple-element.19.query_ref, bf16[1024,256]{1,0:T(8,128)(2,1)S(1)} %get-tuple-element.20.key_ref, bf16[1024,256]{1,0:T(8,128)(2,1)S(1)} %get-tuple-element.21.value_ref, bf16[1024,256]{1,0:T(8,128)(2,1)S(1)} %pad_maximum_fusion.24.incoming_ref, ...), custom_call_target="tpu_custom_call" | custom-call | tf_op jit(solution)/shard_map/attend_backward/pallas_call | solution.py:319
  265.2 9.9 %collective-permute-done.29 = bf16[1024,256]{0,1:T(8,128)(2,1)S(1)} collective-permute-done((bf16[1024,256]{0,1:T(8,128)(2,1)S(1)}, bf16[1024,256]{0,1:T(8,128)(2,1)S(1)}, u32[]{:S(2)}, u32[]{:S(2)}) %collective-permute-start.29) | collective-permute-done | bytes 524320 | tf_op jit(solution)/shard_map/ppermute | solution.py:48
  276.9 2.9 copy.61
  279.8 5.9 %collective-permute-done.26 = bf16[256,1024]{1,0:T(8,128)(2,1)} collective-permute-done((bf16[256,1024]{1,0:T(8,128)(2,1)}, bf16[256,1024]{1,0:T(8,128)(2,1)}, u32[]{:S(2)}, u32[]{:S(2)}) %collective-permute-start.26) | collective-permute-done | bytes 524320 | tf_op jit(solution)/shard_map/ppermute | solution.py:48
  291.7 9.1 %collective-permute-done.34 = bf16[128,1536]{1,0:T(8,128)(2,1)S(1)} collective-permute-done((bf16[128,1536]{1,0:T(8,128)(2,1)}, bf16[128,1536]{1,0:T(8,128)(2,1)S(1)}, u32[]{:S(2)}, u32[]{:S(2)}) %collective-permute-start.34) | collective-permute-done | bytes 393248 | tf_op jit(solution)/shard_map/ppermute | solution.py:48
  305.7 65.3 %reduce-scatter.3.cloned.1.call-done = bf16[1,232,1024]{2,1,0:T(8,128)(2,1)} async-done(((bf16[8,232,1024]{2,1,0:T(8,128)(2,1)}), bf16[1,232,1024]{2,1,0:T(8,128)(2,1)}) %reduce-scatter.3.cloned.1.call-update) | async-done | bytes 475152 | tf_op jit(solution)/shard_map/reduce_scatter | solution.py:351
  374.3 9.4 %collective-permute-done.31 = bf16[232,1024]{1,0:T(8,128)(2,1)} collective-permute-done((bf16[232,1024]{1,0:T(8,128)(2,1)}, bf16[232,1024]{1,0:T(8,128)(2,1)}, u32[]{:S(2)}, u32[]{:S(2)}) %collective-permute-start.31) | collective-permute-done | bytes 475168 | tf_op jit(solution)/shard_map/ppermute | solution.py:48
  (331 shorter events, 113.1 us)
Async XLA Ops:
  7.2 73.5 %all-gather.6.cloned.1.call-start = ((), (), s32[]{:S(2)}) async-start(), calls=%async_computation.5 | async-start | bytes 4128768 | tf_op jit(solution)/shard_map/all_gather | solution.py:187
  11.0 133.9 %all-gather.4.cloned.1.call-start = ((), (), s32[]{:S(2)}) async-start(), calls=%async_computation.2 | async-start | bytes 3538944 | tf_op jit(solution)/shard_map/all_gather | solution.py:195
  11.1 15.0 %collective-permute-start.1 = (bf16[256,1024]{1,0:T(8,128)(2,1)S(1)}, bf16[256,1024]{1,0:T(8,128)(2,1)S(1)}, u32[]{:S(2)}, u32[]{:S(2)}) collective-permute-start(bf16[256,1024]{1,0:T(8,128)(2,1)S(1)} %copy-done.5), channel_id=1, source_target_pairs={{0,2},{1,3},{2,0},{3,1},{4,6},{5,7},{6,4},{7,5},{8,10},{9,11},{10,... | collective-permute-start | bytes 1572872 | tf_op jit(solution)/shard_map/ppermute | solution.py:48
  14.1 33.5 %collective-permute-start = (bf16[256,1024]{1,0:T(8,128)(2,1)S(1)}, bf16[256,1024]{1,0:T(8,128)(2,1)}, u32[]{:S(2)}, u32[]{:S(2)}) collective-permute-start(bf16[256,1024]{1,0:T(8,128)(2,1)S(1)} %copy-done.5), channel_id=1, source_target_pairs={{0,1},{1,0},{2,3},{3,2},{4,5},{5,4},{6,7},{7,6},{8,9},{9,8},{10,11... | collective-permute-start | bytes 1572872 | tf_op jit(solution)/shard_map/ppermute | solution.py:48
  16.9 273.2 %reduce-scatter.5.cloned.1.call-start = ((), (), s32[]{:S(2)}) async-start(), calls=%async_computation.4 | async-start | bytes 3538944 | tf_op jit(solution)/shard_map/reduce_scatter | solution.py:302
  26.0 21.6 %collective-permute-start.2 = (bf16[256,1024]{1,0:T(8,128)(2,1)S(1)}, bf16[256,1024]{1,0:T(8,128)(2,1)}, u32[]{:S(2)}, u32[]{:S(2)}) collective-permute-start(bf16[256,1024]{1,0:T(8,128)(2,1)S(1)} %collective-permute-done.1), channel_id=1, source_target_pairs={{0,1},{1,0},{2,3},{3,2},{4,5},{5,4},{6,7},{7,6},{8,9},{9,8},{10,11... | collective-permute-start | bytes 1572872 | tf_op jit(solution)/shard_map/ppermute | solution.py:48
  81.8 18.1 %collective-permute-start.7 = (bf16[1024,256]{1,0:T(8,128)(2,1)S(1)}, bf16[1024,256]{1,0:T(8,128)(2,1)S(1)}, u32[]{:S(2)}, u32[]{:S(2)}) collective-permute-start(bf16[1024,256]{1,0:T(8,128)(2,1)S(1)} %bitcast.207), channel_id=1, source_target_pairs={{0,2},{1,3},{2,0},{3,1},{4,6},{5,7},{6,4},{7,5},{8,10},{9,11},{10,... | collective-permute-start | bytes 1572872 | tf_op jit(solution)/shard_map/ppermute | solution.py:48
  86.6 22.8 %collective-permute-start.6 = (bf16[1024,256]{1,0:T(8,128)(2,1)S(1)}, bf16[1024,256]{1,0:T(8,128)(2,1)S(1)}, u32[]{:S(2)}, u32[]{:S(2)}) collective-permute-start(bf16[1024,256]{1,0:T(8,128)(2,1)S(1)} %bitcast.208), channel_id=1, source_target_pairs={{0,1},{1,0},{2,3},{3,2},{4,5},{5,4},{6,7},{7,6},{8,9},{9,8},{10,11... | collective-permute-start | bytes 1572872 | tf_op jit(solution)/shard_map/ppermute | solution.py:48
  113.9 14.2 %collective-permute-start.11 = (bf16[256,1024]{1,0:T(8,128)(2,1)}, bf16[256,1024]{1,0:T(8,128)(2,1)}, u32[]{:S(2)}, u32[]{:S(2)}) collective-permute-start(bf16[256,1024]{1,0:T(8,128)(2,1)} %multiply_convert_fusion.7), channel_id=1, source_target_pairs={{0,2},{1,3},{2,0},{3,1},{4,6},{5,7},{6,4},{7,5},{8,10},{9,11},{10,... | collective-permute-start | bytes 1572872 | tf_op jit(solution)/shard_map/ppermute | solution.py:48
  114.3 30.6 %collective-permute-start.9 = (bf16[256,1024]{1,0:T(8,128)(2,1)}, bf16[256,1024]{1,0:T(8,128)(2,1)}, u32[]{:S(2)}, u32[]{:S(2)}) collective-permute-start(bf16[256,1024]{1,0:T(8,128)(2,1)} %multiply_convert_fusion.7), channel_id=1, source_target_pairs={{0,1},{1,0},{2,3},{3,2},{4,5},{5,4},{6,7},{7,6},{8,9},{9,8},{10,11... | collective-permute-start | bytes 1572872 | tf_op jit(solution)/shard_map/ppermute | solution.py:48
  128.1 21.0 %collective-permute-start.12 = (bf16[256,1024]{1,0:T(8,128)(2,1)}, bf16[256,1024]{1,0:T(8,128)(2,1)}, u32[]{:S(2)}, u32[]{:S(2)}) collective-permute-start(bf16[256,1024]{1,0:T(8,128)(2,1)} %collective-permute-done.11), channel_id=1, source_target_pairs={{0,1},{1,0},{2,3},{3,2},{4,5},{5,4},{6,7},{7,6},{8,9},{9,8},{10,11... | collective-permute-start | bytes 1572872 | tf_op jit(solution)/shard_map/ppermute | solution.py:48
  157.0 13.9 %collective-permute-start.14 = (bf16[256,1024]{1,0:T(8,128)(2,1)S(1)}, bf16[256,1024]{1,0:T(8,128)(2,1)S(1)}, u32[]{:S(2)}, u32[]{:S(2)}) collective-permute-start(bf16[256,1024]{1,0:T(8,128)(2,1)S(1)} %fusion.24), channel_id=1, source_target_pairs={{0,2},{1,3},{2,0},{3,1},{4,6},{5,7},{6,4},{7,5},{8,10},{9,11},{10,... | collective-permute-start | bytes 1572872 | tf_op jit(solution)/shard_map/ppermute | solution.py:48
  172.8 13.0 %collective-permute-start.17 = (bf16[256,1024]{1,0:T(8,128)(2,1)S(1)}, bf16[256,1024]{1,0:T(8,128)(2,1)S(1)}, u32[]{:S(2)}, u32[]{:S(2)}) collective-permute-start(bf16[256,1024]{1,0:T(8,128)(2,1)S(1)} %get-tuple-element.86), channel_id=1, source_target_pairs={{0,2},{1,3},{2,0},{3,1},{4,6},{5,7},{6,4},{7,5},{8,10},{9,11},{10,... | collective-permute-start | bytes 1572872 | tf_op jit(solution)/shard_map/ppermute | solution.py:48
  174.3 11.5 %collective-permute-start.15 = (bf16[256,1024]{1,0:T(8,128)(2,1)S(1)}, bf16[256,1024]{1,0:T(8,128)(2,1)S(1)}, u32[]{:S(2)}, u32[]{:S(2)}) collective-permute-start(bf16[256,1024]{1,0:T(8,128)(2,1)S(1)} %get-tuple-element.86), channel_id=1, source_target_pairs={{0,1},{1,0},{2,3},{3,2},{4,5},{5,4},{6,7},{7,6},{8,9},{9,8},{10,11... | collective-permute-start | bytes 1572872 | tf_op jit(solution)/shard_map/ppermute | solution.py:48
  191.6 19.7 %collective-permute-start.16 = (bf16[256,1024]{1,0:T(8,128)(2,1)}, bf16[256,1024]{1,0:T(8,128)(2,1)}, u32[]{:S(2)}, u32[]{:S(2)}) collective-permute-start(bf16[256,1024]{1,0:T(8,128)(2,1)} %slice.477), channel_id=1, source_target_pairs={{0,1},{1,0},{2,3},{3,2},{4,5},{5,4},{6,7},{7,6},{8,9},{9,8},{10,11... | collective-permute-start | bytes 1572872 | tf_op jit(solution)/shard_map/ppermute | solution.py:48
  204.5 166.5 %reduce-scatter.3.cloned.1.call-start = ((), (), s32[]{:S(2)}) async-start(), calls=%async_computation.3 | async-start | bytes 4276224 | tf_op jit(solution)/shard_map/reduce_scatter | solution.py:351
  206.5 14.4 %collective-permute-start.20 = (bf16[256,1024]{1,0:T(8,128)(2,1)S(1)}, bf16[256,1024]{1,0:T(8,128)(2,1)S(1)}, u32[]{:S(2)}, u32[]{:S(2)}) collective-permute-start(bf16[256,1024]{1,0:T(8,128)(2,1)S(1)} %fusion.22), channel_id=1, source_target_pairs={{0,2},{1,3},{2,0},{3,1},{4,6},{5,7},{6,4},{7,5},{8,10},{9,11},{10,... | collective-permute-start | bytes 1572872 | tf_op jit(solution)/shard_map/ppermute | solution.py:48
  236.2 24.0 %collective-permute-start.28 = (bf16[1024,256]{0,1:T(8,128)(2,1)S(1)}, bf16[1024,256]{0,1:T(8,128)(2,1)S(1)}, u32[]{:S(2)}, u32[]{:S(2)}) collective-permute-start(bf16[1024,256]{0,1:T(8,128)(2,1)S(1)} %get-tuple-element.69), channel_id=1, source_target_pairs={{0,1},{1,0},{2,3},{3,2},{4,5},{5,4},{6,7},{7,6},{8,9},{9,8},{10,11... | collective-permute-start | bytes 1572872 | tf_op jit(solution)/shard_map/ppermute | solution.py:48
  236.4 28.8 %collective-permute-start.27 = (bf16[1024,256]{0,1:T(8,128)(2,1)S(1)}, bf16[1024,256]{0,1:T(8,128)(2,1)S(1)}, u32[]{:S(2)}, u32[]{:S(2)}) collective-permute-start(bf16[1024,256]{0,1:T(8,128)(2,1)S(1)} %get-tuple-element.68), channel_id=1, source_target_pairs={{0,1},{1,0},{2,3},{3,2},{4,5},{5,4},{6,7},{7,6},{8,9},{9,8},{10,11... | collective-permute-start | bytes 1572872 | tf_op jit(solution)/shard_map/ppermute | solution.py:48
  259.8 20.0 %collective-permute-start.24 = (bf16[256,1024]{1,0:T(8,128)(2,1)}, bf16[256,1024]{1,0:T(8,128)(2,1)S(1)}, u32[]{:S(2)}, u32[]{:S(2)}) collective-permute-start(bf16[256,1024]{1,0:T(8,128)(2,1)} %slice.475), channel_id=1, source_target_pairs={{0,1},{1,0},{2,3},{3,2},{4,5},{5,4},{6,7},{7,6},{8,9},{9,8},{10,11... | collective-permute-start | bytes 1572872 | tf_op jit(solution)/shard_map/ppermute | solution.py:48
  260.3 14.8 %collective-permute-start.29 = (bf16[1024,256]{0,1:T(8,128)(2,1)S(1)}, bf16[1024,256]{0,1:T(8,128)(2,1)S(1)}, u32[]{:S(2)}, u32[]{:S(2)}) collective-permute-start(bf16[1024,256]{0,1:T(8,128)(2,1)S(1)} %fusion.26), channel_id=1, source_target_pairs={{0,2},{1,3},{2,0},{3,1},{4,6},{5,7},{6,4},{7,5},{8,10},{9,11},{10,... | collective-permute-start | bytes 1572872 | tf_op jit(solution)/shard_map/ppermute | solution.py:48
  262.8 22.9 %collective-permute-start.26 = (bf16[256,1024]{1,0:T(8,128)(2,1)}, bf16[256,1024]{1,0:T(8,128)(2,1)}, u32[]{:S(2)}, u32[]{:S(2)}) collective-permute-start(bf16[256,1024]{1,0:T(8,128)(2,1)} %fusion.20), channel_id=1, source_target_pairs={{0,2},{1,3},{2,0},{3,1},{4,6},{5,7},{6,4},{7,5},{8,10},{9,11},{10,... | collective-permute-start | bytes 1572872 | tf_op jit(solution)/shard_map/ppermute | solution.py:48
  291.7 11.9 %collective-permute-start.33 = (bf16[128,1536]{1,0:T(8,128)(2,1)}, bf16[128,1536]{1,0:T(8,128)(2,1)S(1)}, u32[]{:S(2)}, u32[]{:S(2)}) collective-permute-start(bf16[128,1536]{1,0:T(8,128)(2,1)} %reduce-scatter.5.cloned.1.call-done), channel_id=1, source_target_pairs={{0,1},{1,0},{2,3},{3,2},{4,5},{5,4},{6,7},{7,6},{8,9},{9,8},{10,11... | collective-permute-start | bytes 1179656 | tf_op jit(solution)/shard_map/ppermute | solution.py:48
  370.9 12.8 %collective-permute-start.31 = (bf16[232,1024]{1,0:T(8,128)(2,1)}, bf16[232,1024]{1,0:T(8,128)(2,1)}, u32[]{:S(2)}, u32[]{:S(2)}) collective-permute-start(bf16[232,1024]{1,0:T(8,128)(2,1)} %bitcast.56), channel_id=1, source_target_pairs={{0,2},{1,3},{2,0},{3,1},{4,6},{5,7},{6,4},{7,5},{8,10},{9,11},{10,... | collective-permute-start | bytes 1425416 | tf_op jit(solution)/shard_map/ppermute | solution.py:48
  (74 other events, 374.7 us)
Sparse Core Ops, SparseCore 0:
  11.1 69.5 all-gather.5
  83.4 61.4 all-gather.3
  204.6 72.7 reduce-scatter.4
  290.2 80.6 reduce-scatter.2

commit v2 on v1

v2 whole, which is shorter than its diff:
```python
import functools

import jax
import jax.numpy as jnp
from jax import lax
from jax.experimental import pallas as pl
from jax.experimental.pallas import tpu as pltpu
from jax.sharding import PartitionSpec as P

HEADS = 8
EPSILON = 1e-06
ROTARY_BASE = 50000.0
DOC_LEN = 8192
DOC_STRIDE = 64
HIDDEN_LOW = -1e30
LOG2_E = 1.4426950408889634
SEQ = 4
GAIN_ROWS = 8

f32 = jnp.float32
bf16 = jnp.bfloat16


def dot(left, right):
    return jnp.dot(left, right, preferred_element_type=f32)


def dot_nt(left, right):
    return lax.dot_general(left, right, (((1,), (1,)), ((), ())), preferred_element_type=f32)


def dot_tn(left, right):
    return lax.dot_general(left, right, (((0,), (0,)), ((), ())), preferred_element_type=f32)


def normed_of(values):
    inverse = lax.rsqrt(jnp.mean(values * values, -1, keepdims=True) + EPSILON)
    return values * inverse, inverse


def norm_back(incoming, normed, inverse, scales):
    scaled = incoming * scales
    return inverse * (scaled - normed * jnp.mean(scaled * normed, -1, keepdims=True))


def call(kernel, outs, *args, smem=0, flops=0, exps=0, scratch=(), name=None):
    moved = sum(arg.size * arg.dtype.itemsize for arg in args)
    many = isinstance(outs, (list, tuple))
    whole = pl.BlockSpec(memory_space=pltpu.VMEM)
    return pl.pallas_call(
        kernel,
        out_shape=tuple(outs) if many else outs,
        in_specs=[
            pl.BlockSpec(memory_space=pltpu.SMEM) if at < smem else whole
            for at in range(len(args))
        ],
        out_specs=(whole,) * len(outs) if many else whole,
        scratch_shapes=list(scratch),
        compiler_params=pltpu.CompilerParams(vmem_limit_bytes=56 * 1024 * 1024),
        cost_estimate=pl.CostEstimate(flops=flops, transcendentals=exps, bytes_accessed=moved),
        name=name,
    )(*args)


def shaped(*shape, dtype=bf16):
    return jax.ShapeDtypeStruct(shape, dtype)


def after(value, *others):
    return lax.optimization_barrier((value,) + others)[0]


def swap(value, bit):
    return lax.ppermute(value, "seq", [(i, i ^ bit) for i in range(SEQ)])


def chosen(rows, columns, chunk, padded, place):
    row = lax.broadcasted_iota(jnp.int32, (rows, columns), 0)
    column = lax.broadcasted_iota(jnp.int32, (rows, columns), 1)
    block = column // padded
    inside = column - block * padded
    wanted = block * (SEQ * chunk) + place * chunk + inside
    return jnp.where((row == wanted) & (inside < chunk), 1.0, 0.0).astype(bf16)


def pack_first(place_ref, query_ref, key_ref, value_ref, output_ref, down_ref, *refs, padded):
    gain_refs, out_ref = refs[:4], refs[4]
    place = place_ref[0]
    shard, model = query_ref.shape
    part = model // SEQ
    columns = pl.ds(pl.multiple_of(place * part, part), part)
    for at, ref in enumerate((query_ref, key_ref, value_ref, output_ref)):
        out_ref[:shard, at * part:(at + 1) * part] = ref[:, columns]
    out_ref[shard:shard + GAIN_ROWS, :] = jnp.zeros((GAIN_ROWS, model), bf16)
    for at, ref in enumerate(gain_refs):
        out_ref[shard:shard + 1, at * shard:(at + 1) * shard] = ref[...]
    chunk = down_ref.shape[0] // SEQ
    pick_rows = chosen(SEQ * chunk, padded, chunk, padded, place)
    out_ref[shard + GAIN_ROWS:, :] = dot_tn(pick_rows, down_ref[...]).astype(bf16)


def pack_gate_up(place_ref, gate_ref, up_ref, out_ref, *, chunk, padded):
    wide = gate_ref.shape[1] // 2
    narrow = out_ref.shape[1] // 4
    pick = chosen(wide, narrow, chunk, padded, place_ref[0])
    for number, ref in enumerate((gate_ref, up_ref)):
        for half in range(2):
            at = (2 * number + half) * narrow
            out_ref[:, at:at + narrow] = dot(
                ref[:, half * wide:(half + 1) * wide], pick
            ).astype(bf16)


def unpack_feed(place_ref, *refs, shard, padded):
    blocks, (gate_ref, up_ref, down_ref) = refs[:SEQ], refs[SEQ:]
    place = place_ref[0]
    piece = blocks[0].shape[1]
    chunk = down_ref.shape[0] // SEQ
    pieces = (blocks[0].shape[0] - 2 * padded) // shard
    narrow = pieces * piece // 4
    wide = gate_ref.shape[1] // 2
    picks = [chosen(wide, narrow, chunk, padded, place ^ at) for at in range(SEQ)]
    joined = [
        jnp.concatenate([ref[at * shard:(at + 1) * shard, :] for at in range(pieces)], 1)
        for ref in blocks
    ]
    for number, out_ref in enumerate((gate_ref, up_ref)):
        for half in range(2):
            at = (2 * number + half) * narrow
            out_ref[:, half * wide:(half + 1) * wide] = sum(
                dot_nt(joined[step][:, at:at + narrow], picks[step]) for step in range(SEQ)
            )
    below = pieces * shard
    rows = [chosen(SEQ * chunk, padded, chunk, padded, place ^ at) for at in range(SEQ)]
    for at in range(2):
        down_ref[:, at * piece:(at + 1) * piece] = sum(
            dot(rows[step], blocks[step][below + at * padded:below + (at + 1) * padded, :])
            for step in range(SEQ)
        )


def unpack_last(place_ref, *refs, shard):
    blocks, outs = refs[:SEQ], refs[SEQ:]
    place = place_ref[0]
    part = blocks[0].shape[1] // SEQ
    for step, block in enumerate(blocks):
        columns = pl.ds(pl.multiple_of((place ^ step) * part, part), part)
        for at in range(4):
            outs[at][:, columns] = block[:shard, at * part:(at + 1) * part].astype(f32)
    outs[4][...] = sum(block[shard:, :].astype(f32) for block in blocks)


def prepare(
    first_ref, own_ref, near_ref, far_ref, both_ref,
    weight_ref, output_ref, down_ref, gain_ref, low_ref, *, shard,
):
    wt, total, model = first_ref.shape
    part = model // SEQ
    weight_ref[...] = first_ref[:, :shard, :3 * part].reshape(model, 3 * part)
    output_ref[...] = first_ref[:, :shard, 3 * part:].reshape(model, part)
    down_ref[...] = first_ref[:, shard + GAIN_ROWS:, :].reshape(down_ref.shape)
    for at in range(wt):
        for number in range(4):
            gain_ref[number:number + 1, at * shard:(at + 1) * shard] = first_ref[
                at, shard:shard + 1, number * shard:(number + 1) * shard
            ].astype(f32)
    rows = own_ref.shape[0]
    scales = gain_ref[0:1, :]
    step = 32
    for number, ref in enumerate((own_ref, near_ref, far_ref, both_ref)):

        def some(at, carry):
            normed, _ = normed_of(ref[pl.ds(pl.multiple_of(at * step, step), step), :].astype(f32))
            low_ref[pl.ds(pl.multiple_of(number * rows + at * step, step), step), :] = (
                normed * scales
            ).astype(bf16)
            return carry

        lax.fori_loop(0, rows // step, some, 0, unroll=2)


def arrange(place_ref, *refs):
    blocks, out_ref = refs[:SEQ], refs[SEQ]
    place = place_ref[0]
    part = blocks[0].shape[1]
    for step in range(SEQ):
        rows = pl.ds(pl.multiple_of((place ^ step) * part, part), part)
        for other in range(SEQ):
            columns = pl.ds(pl.multiple_of((place ^ other) * part, part), part)
            out_ref[step * part:(step + 1) * part, columns] = blocks[other][rows, :]


def turn(rows, cosine, sine):
    return rows * cosine + pltpu.roll(rows, rows.shape[-1] // 2, axis=1) * sine


def visible(key_code, query_code, tile):
    key_wide = jnp.concatenate([key_code] * (tile // 128), axis=1)
    return (key_wide <= query_code[0:1, :]) & (key_wide >= query_code[1:2, :])


def attend_forward(
    low_ref, weight_ref, cos_ref, sin_ref, key_code_ref, query_code_ref,
    query_ref, key_ref, value_ref, out_ref, log_ref,
):
    window = low_ref.shape[0]
    tiles, _, tile = query_code_ref.shape
    width = cos_ref.shape[1]
    heads = query_ref.shape[1] // width
    scale = LOG2_E * width ** (-0.5)

    def project(step, carry):
        rows = pl.ds(pl.multiple_of(step * tile, tile), tile)
        raw = dot(low_ref[rows, :], weight_ref[...])
        cosine = cos_ref[rows, :]
        sine = sin_ref[rows, :]
        for head in range(heads):
            at = head * width
            query_ref[rows, at:at + width] = turn(raw[:, at:at + width], cosine, sine).astype(bf16)
            at = (heads + head) * width
            key_ref[rows, head * width:(head + 1) * width] = turn(
                raw[:, at:at + width], cosine, sine
            ).astype(bf16)
        value_ref[rows, :] = raw[:, 2 * heads * width:].astype(bf16)
        return carry

    lax.fori_loop(0, window // tile, project, 0)
    for head in range(heads):
        cols = slice(head * width, (head + 1) * width)
        value_turned = value_ref[:, cols].astype(f32).T.astype(bf16)

        def one_tile(step, carry):
            rows = pl.ds(pl.multiple_of(step * tile, tile), tile)
            scores = dot_nt(key_ref[:, cols], query_ref[rows, cols])
            shown = visible(key_code_ref[...], query_code_ref[step], tile)
            scores = jnp.where(shown, scores * scale, HIDDEN_LOW)
            top = jnp.max(scores, 0, keepdims=True)
            weights = jnp.exp2(scores - top)
            total = jnp.sum(weights, 0, keepdims=True)
            result = dot(value_turned, weights.astype(bf16)) * (1.0 / total)
            out_ref[rows, cols] = result.T.astype(bf16)
            log_ref[head, step] = jnp.broadcast_to(top + jnp.log2(total), (8, tile))
            return carry

        lax.fori_loop(0, tiles, one_tile, 0)


def attend_backward(
    query_ref, key_ref, value_ref, log_ref, cos_ref, sin_ref, key_code_ref, query_code_ref,
    *refs,
):
    incoming_refs, (grad_ref, key_sum, value_sum, incoming_ref) = refs[:SEQ], refs[SEQ:]
    tiles, _, tile = query_code_ref.shape
    width = cos_ref.shape[1]
    heads = query_ref.shape[1] // width
    factor = width ** (-0.5)
    scale = LOG2_E * factor
    for step, ref in enumerate(incoming_refs):
        incoming_ref[step * tile:(step + 1) * tile, :] = ref[...]
    for head in range(heads):
        cols = slice(head * width, (head + 1) * width)
        key_turned = key_ref[:, cols].astype(f32).T.astype(bf16)
        key_sum[...] = jnp.zeros_like(key_sum)
        value_sum[...] = jnp.zeros_like(value_sum)

        def one_tile(step, carry):
            rows = pl.ds(pl.multiple_of(step * tile, tile), tile)
            queries = query_ref[rows, cols]
            incoming = incoming_ref[rows, cols]
            scores = dot_nt(key_ref[:, cols], queries)
            shown = visible(key_code_ref[...], query_code_ref[step], tile)
            probs = jnp.where(shown, jnp.exp2(scores * scale - log_ref[head, step, 0:1, :]), 0.0)
            value_sum[...] += dot(probs.astype(bf16), incoming)
            prob_grad = dot_nt(value_ref[:, cols], incoming)
            inner = jnp.sum(probs * prob_grad, 0, keepdims=True)
            score_grad = (probs * (prob_grad - inner)).astype(bf16)
            key_sum[...] += dot(score_grad, queries)
            query_grad = (dot(key_turned, score_grad) * factor).T
            grad_ref[rows, cols] = turn(query_grad, cos_ref[rows, :], -sin_ref[rows, :]).astype(bf16)
            return carry

        lax.fori_loop(0, tiles, one_tile, 0)
        at = (heads + head) * width
        grad_ref[:, at:at + width] = turn(
            key_sum[...] * factor, cos_ref[...], -sin_ref[...]
        ).astype(bf16)
        at = (2 * heads + head) * width
        grad_ref[:, at:at + width] = value_sum[...].astype(bf16)


def feed_weights(*refs, shard, padded):
    lows, refs = refs[:SEQ], refs[SEQ:]
    channels, refs = refs[:SEQ], refs[SEQ:]
    near_grad, far_grad, near_active, far_active, out_ref = refs
    wt, total, piece = out_ref.shape
    pieces = (total - 2 * padded) // shard
    low = jnp.concatenate([ref[...] for ref in lows], 0)
    for at in range(pieces):
        columns = slice(at * piece, (at + 1) * piece)
        grad = jnp.concatenate([near_grad[:, columns], far_grad[:, columns]], 0)
        out_ref[:, at * shard:(at + 1) * shard, :] = (
            dot_tn(low, grad).astype(bf16).reshape(wt, shard, piece)
        )
    active = jnp.concatenate([near_active[...], far_active[...]], 0)
    below = pieces * shard
    for at in range(2):
        columns = slice(at * piece, (at + 1) * piece)
        grad = jnp.concatenate([ref[:, columns] for ref in channels], 0)
        out_ref[:, below + at * padded:below + (at + 1) * padded, :] = (
            dot_tn(active, grad).astype(bf16).reshape(wt, padded, piece)
        )


def output_weights(place_ref, low_ref, *refs):
    pieces, outs = refs[:SEQ], refs[SEQ:]
    place = place_ref[0]
    part = outs[0].shape[1]
    for step in range(SEQ):
        columns = pl.ds(pl.multiple_of((place ^ step) * part, part), part)
        for other in range(SEQ):
            rows = pl.ds(pl.multiple_of((place ^ other) * part, part), part)
            outs[step][rows, :] = dot_tn(pieces[other][...], low_ref[:, columns]).astype(
                outs[step].dtype
            )


def last_weights(at_ref, low_ref, grad_ref, keep_ref, near_ref, far_ref, sum_ref, *refs):
    out_ref, full = refs
    wt, total, model = out_ref.shape
    shard = total - GAIN_ROWS
    part = keep_ref.shape[1]
    full[:, :3 * part] = dot_tn(low_ref[...], grad_ref[...]).astype(bf16)
    full[:, 3 * part:] = (
        keep_ref[...] + near_ref[...].astype(f32) + far_ref[...].astype(f32)
    ).astype(bf16)
    for step in range(wt):
        at = at_ref[step]
        out_ref[step, :shard, :] = full[pl.ds(pl.multiple_of(at * shard, shard), shard), :]
        out_ref[step, shard:, :] = sum_ref[at]


def reduce_lines(blocks, wt):
    def send(value, bit):
        return lax.ppermute(value, "wt", [(at, at ^ bit) for at in range(wt)])

    far_x = send(blocks[6:8], 1)
    near_x = send(blocks[4:6], 1)
    far = (blocks[2:4].astype(f32) + far_x.astype(f32)).astype(bf16)
    got = [send(far[1], 6), send(far[0], 4)]
    near = blocks[0:2].astype(f32) + near_x.astype(f32)
    got.append(send(near[1].astype(bf16), 2))
    return (near[0] + sum(value.astype(f32) for value in got)).astype(bf16)


def on_device(
    tokens, positions, doc_ids, block_ids, entry_gain, query_weight, key_weight, value_weight,
    output_weight, attend_gain, middle_gain, gate_weight, up_weight, down_weight, closing_gain,
    cotangent,
):
    place = lax.axis_index("seq")
    order = [place ^ step for step in range(SEQ)]
    here = jnp.reshape(place, (1,)).astype(jnp.int32)
    rows, model = tokens.shape
    window = rows * SEQ
    shard = query_weight.shape[0]
    wt = model // shard
    part = model // SEQ
    width = model // HEADS
    heads = HEADS // SEQ
    hidden = gate_weight.shape[1]
    chunk = hidden // (wt * SEQ)
    padded = (chunk + 15) // 16 * 16
    hidden_part = padded * wt
    piece = model // 2
    feed_rows = 2 * hidden_part // piece * shard + 2 * padded

    def gather_blocks(own):
        far = swap(own, 2)
        near = swap(own, 1)
        return own, near, far, swap(far, 1)

    first_own = call(
        functools.partial(pack_first, padded=padded),
        shaped(shard + GAIN_ROWS + padded, model),
        here, query_weight, key_weight, value_weight, output_weight, down_weight,
        *(gain[None] for gain in (entry_gain, attend_gain, middle_gain, closing_gain)),
        smem=1, name="pack_first",
    )
    first = lax.all_gather(first_own, "wt", axis=0, tiled=False)
    gate_up_own = call(
        functools.partial(pack_gate_up, chunk=chunk, padded=padded),
        shaped(shard, 2 * hidden_part), here, gate_weight, up_weight, smem=1, name="pack_gate_up",
    )
    gate_up = lax.all_gather(gate_up_own, "wt", axis=0, tiled=True)
    token_blocks = gather_blocks(tokens)

    offsets = jnp.arange(window, dtype=jnp.int32)
    leading = doc_ids == doc_ids[0]
    boundary = jnp.sum(leading.astype(jnp.int32))
    places = jnp.where(leading, DOC_LEN - boundary + offsets, offsets - boundary)
    codes = doc_ids * DOC_STRIDE + block_ids
    lows = doc_ids * DOC_STRIDE
    packed = jnp.stack([places, codes, lows]).reshape(3, SEQ, rows)
    packed = jnp.concatenate(
        [lax.dynamic_index_in_dim(packed, at, 1, keepdims=False) for at in order], 1
    )
    half = width // 2
    frequency = ROTARY_BASE ** (-2.0 * jnp.arange(half, dtype=f32) / width)
    angles = packed[0].astype(f32)[:, None] * frequency[None, :]
    cosine = jnp.cos(angles)
    sine = jnp.sin(angles)
    cosine = jnp.concatenate([cosine, cosine], 1)
    sine = jnp.concatenate([-sine, sine], 1)
    key_code = jnp.broadcast_to(packed[1][:, None], (window, 128))
    query_code = jnp.broadcast_to(
        packed[1:3].reshape(2, SEQ, rows).transpose(1, 0, 2)[:, :, None, :], (SEQ, 2, 4, rows)
    ).transpose(0, 2, 1, 3).reshape(SEQ, 8, rows)

    first = after(first, cosine, sine, key_code, query_code, *token_blocks)
    qkv_weight, output_own, down_part, gains, entry_low = call(
        functools.partial(prepare, shard=shard),
        (shaped(model, 3 * part), shaped(model, part), shaped(hidden_part, model),
         shaped(8, model, dtype=f32), shaped(window, model)),
        first, *token_blocks, name="prepare",
    )
    entry_full, attend_full, middle_full, closing_full = [gains[at:at + 1] for at in range(4)]
    low_shape = shaped(window, heads * width)
    pair_cost = 2 * heads * window * window * width
    query_low, key_low, value_low, attended, log_totals = call(
        attend_forward,
        (low_shape, low_shape, low_shape, low_shape,
         shaped(heads, SEQ, 8, rows, dtype=f32)),
        entry_low, qkv_weight, cosine, sine, key_code, query_code,
        flops=2 * pair_cost + 6 * window * model * part, exps=heads * window * window,
        name="attend_forward",
    )
    output_far = after(swap(output_own, 2), attended)
    output_rows = call(
        arrange, shaped(model, model),
        here, output_own, swap(output_own, 1), output_far, swap(output_far, 1), smem=1,
        name="arrange",
    )

    def exchange(blocks):
        return [blocks[0], swap(blocks[1], 1), swap(blocks[2], 2), swap(blocks[3], 3)]

    joined = exchange([attended[at * rows:(at + 1) * rows] for at in range(SEQ)])
    inputs = tokens.astype(f32)
    mixed = dot(jnp.concatenate(joined, 1), output_rows)
    attend_normed, attend_inverse = normed_of(mixed)
    hidden_state = inputs + attend_normed * attend_full
    middle_normed, middle_inverse = normed_of(hidden_state)
    middle_low = (middle_normed * middle_full).astype(bf16)

    def feed(first_rows, second_rows):
        both = dot(jnp.concatenate([first_rows, second_rows], 0), gate_up)
        gate_value = both[:, :hidden_part]
        up_value = both[:, hidden_part:]
        share = jax.nn.sigmoid(gate_value)
        active = (gate_value * share * up_value).astype(bf16)
        return gate_value, up_value, share, active

    def two_halves(own, work):
        far = swap(own, 2)
        near = swap(own, 1)
        near_done = work(own, near)
        far = after(far, *jax.tree.leaves(near_done))
        return (own, near, far, swap(far, 1)), near_done

    def to_far(values, weights, product):
        second = product(values[rows:], weights).astype(bf16)
        total = product(values[:rows], weights) + swap(second, 1).astype(f32)
        total = total.astype(bf16)
        return swap(total, 2), total

    def add_near(values, weights, product, far_got):
        second = product(values[rows:], weights).astype(bf16)
        return product(values[:rows], weights) + swap(second, 1).astype(f32) + far_got.astype(f32)

    middle_blocks, fed_near = two_halves(middle_low, feed)
    fed_far = feed(middle_blocks[2], middle_blocks[3])
    far_got, far_sum = to_far(fed_far[3], down_part, dot)
    channel_out = add_near(after(fed_near[3], far_sum), down_part, dot, far_got)
    closing_normed, closing_inverse = normed_of(channel_out)
    layer_output = (hidden_state + closing_normed * closing_full).astype(bf16)
    incoming = cotangent.astype(f32)
    channel_low = norm_back(incoming, closing_normed, closing_inverse, closing_full).astype(bf16)
    closing_sum = jnp.sum(incoming * closing_normed, 0)

    def feed_back(first_rows, second_rows, saved):
        gate_value, up_value, share, _ = saved
        active_grad = dot_nt(jnp.concatenate([first_rows, second_rows], 0), down_part)
        gate_grad = active_grad * up_value * share * (1.0 + gate_value * (1.0 - share))
        up_grad = active_grad * gate_value * share
        return jnp.concatenate([gate_grad.astype(bf16), up_grad.astype(bf16)], 1)

    channel_blocks, back_near = two_halves(
        channel_low, lambda first_rows, second_rows: feed_back(first_rows, second_rows, fed_near)
    )
    back_far = feed_back(channel_blocks[2], channel_blocks[3], fed_far)
    far_got, far_sum = to_far(back_far, gate_up, dot_nt)
    feed_local = call(
        functools.partial(feed_weights, shard=shard, padded=padded),
        shaped(wt, feed_rows, piece),
        *middle_blocks, *channel_blocks, back_near, after(back_far, far_sum), fed_near[3],
        fed_far[3], flops=12 * window * model * hidden_part // 2, name="feed_weights",
    )
    feed_share = lax.psum_scatter(feed_local, "wt", scatter_dimension=0, tiled=False)
    middle_grad = add_near(after(back_near, feed_local), gate_up, dot_nt, far_got)

    hidden_grad = incoming + norm_back(middle_grad, middle_normed, middle_inverse, middle_full)
    middle_sum = jnp.sum(middle_grad * middle_normed, 0)
    attend_sum = jnp.sum(hidden_grad * attend_normed, 0)
    mixed_low = norm_back(hidden_grad, attend_normed, attend_inverse, attend_full).astype(bf16)
    attended_grad = dot_nt(mixed_low, output_rows).astype(bf16)
    attended_back = exchange([attended_grad[:, at * part:(at + 1) * part] for at in range(SEQ)])
    output_grads = call(
        output_weights,
        (shaped(model, part, dtype=f32), shaped(model, part), shaped(model, part, dtype=f32),
         shaped(model, part)),
        here, after(mixed_low, attended_grad), *joined, smem=1, flops=2 * rows * model * model,
        name="output_weights",
    )
    output_far = (output_grads[2] + swap(output_grads[3], 1).astype(f32)).astype(bf16)
    output_near = swap(output_grads[1], 1)
    output_got = swap(output_far, 2)
    attended_back[0] = after(attended_back[0], output_far)
    qkv_grad = call(
        attend_backward, shaped(window, 3 * part),
        query_low, key_low, value_low, log_totals, cosine, sine, key_code, query_code,
        *attended_back,
        scratch=(
            pltpu.VMEM((window, width), f32), pltpu.VMEM((window, width), f32),
            pltpu.VMEM((window, heads * width), bf16),
        ),
        flops=5 * pair_cost, exps=heads * window * window, name="attend_backward",
    )
    gain_rows = jnp.stack([attend_sum, middle_sum, closing_sum]).astype(bf16)
    gain_rows = gain_rows.reshape(3, wt, shard).transpose(1, 0, 2).reshape(wt, 1, 3 * shard)
    gain_rows = jnp.pad(gain_rows, ((0, 0), (0, GAIN_ROWS - 1), (0, model - 3 * shard)))
    lines = wt == 8
    mine = lax.axis_index("wt")
    if lines:
        whose = [mine ^ at for at in (0, 2, 4, 6, 1, 3, 5, 7)]
    else:
        whose = list(range(wt))
    last = call(
        last_weights, shaped(wt, shard + GAIN_ROWS, model),
        jnp.stack([jnp.asarray(at, jnp.int32) for at in whose]),
        entry_low, qkv_grad, output_grads[0], output_near, output_got, gain_rows, smem=1,
        scratch=(pltpu.VMEM((model, model), bf16),),
        flops=6 * window * model * part, name="last_weights",
    )
    if lines:
        last_share = reduce_lines(last, wt)
    else:
        last_share = lax.psum_scatter(last, "wt", scatter_dimension=0, tiled=False)

    qkv_grad = after(qkv_grad, last)
    far_got, far_sum = to_far(qkv_grad[2 * rows:], qkv_weight, dot_nt)
    entry_grad = add_near(after(qkv_grad[:2 * rows], far_sum), qkv_weight, dot_nt, far_got)
    entry_normed, entry_inverse = normed_of(inputs)
    input_grad = hidden_grad + norm_back(entry_grad, entry_normed, entry_inverse, entry_full)
    entry_sum = jnp.sum(entry_grad * entry_normed, 0).reshape(8, model // 8)
    for axis, size in (("seq", SEQ), ("wt", wt)):
        bit = 1
        while bit < size:
            entry_sum = entry_sum + lax.ppermute(
                entry_sum, axis, [(at, at ^ bit) for at in range(size)]
            )
            bit *= 2
    grad_entry = lax.dynamic_slice_in_dim(entry_sum.reshape(model), mine * shard, shard)

    feed_blocks = gather_blocks(feed_share)
    grad_gate, grad_up, grad_down = call(
        functools.partial(unpack_feed, shard=shard, padded=padded),
        (shaped(shard, hidden, dtype=f32), shaped(shard, hidden, dtype=f32),
         shaped(SEQ * chunk, model, dtype=f32)),
        here, *feed_blocks, smem=1, name="unpack_feed",
    )
    weight_shape = shaped(shard, model, dtype=f32)
    grad_query, grad_key, grad_value, grad_output, gain_sums = call(
        functools.partial(unpack_last, shard=shard),
        (weight_shape,) * 4 + (shaped(GAIN_ROWS, model, dtype=f32),),
        here, *gather_blocks(last_share), smem=1, name="unpack_last",
    )
    grad_attend, grad_middle, grad_closing = [
        gain_sums[0, at * shard:(at + 1) * shard] for at in range(3)
    ]
    return (
        layer_output, input_grad, grad_entry, grad_query, grad_key, grad_value, grad_output,
        grad_attend, grad_middle, grad_gate, grad_up, grad_down, grad_closing,
    )


def solution(mesh):
    rows = P(("wt", "seq"), None)
    weight = P("wt", None)
    gain = P("wt")
    return jax.shard_map(
        on_device,
        mesh=mesh,
        in_specs=(
            rows, P(("wt", "seq")), gain, gain, gain, weight, weight, weight, weight, gain, gain,
            weight, weight, weight, gain, rows,
        ),
        out_specs=(
            rows, rows, gain, weight, weight, weight, weight, gain, gain, weight, weight, weight,
            gain,
        ),
        check_vma=False,
    )
```

time: 406 us -> 386 us (0.951)
  Pallas kernels: 24 us -> 74.9 us
  blocking collectives: 21 us -> 0 us
  local copies, waits for them, and re-layouts: 38 us -> 18.2 us
  other arithmetic: 37.5 us -> 20.2 us
  waiting for transfers between devices: 208 us -> 191 us
  starting transfers between devices: 22.1 us -> 32.8 us
  matrix products: 32.9 us -> 26.6 us
    reduce_scatter x2 -> x1, waiting for transfers between devices: 65.3 us -> 0.01 us  [on_device(): lax.psum_scatter(feed_local, 'wt', scatter_dimension=0, tiled=False)]
    pallas_call x2 -> x11, Pallas kernels: 24 us -> 74.9 us  [call(): pl.pallas_call(kernel, out_shape=tuple(outs) if many else outs, in_specs=...]
    ppermute x0 -> x10, waiting for transfers between devices: none -> 50.5 us  [the longest x5 43.1 us: send(): return lax.ppermute(value, 'wt', [(at, at ^ bit) for at in range(wt)])]
    ppermute x36, waiting for transfers between devices: 96.1 us -> 66.6 us  [swap(): return lax.ppermute(value, 'seq', [(i, i ^ bit) for i in range(SEQ)])]
    all_gather x2, waiting for transfers between devices: 46.4 us -> 74 us  [the longest x1 49.2 us: on_device(): first = lax.all_gather(first_own, 'wt', axis=0, tiled=False)]
    all_gather x1 -> x0, blocking collectives: 21 us -> none  [on_device(): lax.all_gather(jnp.stack([entry_gain, attend_gain, middle_gain, closing_g...]
    dot_general x6 -> x0, matrix products: 12.6 us -> none  [dot_tn(): lax.dot_general(left, right, (((0,), (0,)), ((), ())), preferred_element_...]
    ppermute x0 -> x10, starting transfers between devices: none -> 9.63 us  [the longest x5 6.48 us: send(): return lax.ppermute(value, 'wt', [(at, at ^ bit) for at in range(wt)])]
  transfers between devices with their start and end apart: 40 -> 49, of which waited for: 17 -> 25; matrix products, arithmetic and copies ran while one was open for 21% -> 12% of each run, Pallas kernels for 6% -> 14%
where the time goes in v2:
time: 386 us; the launch traced here: 380 us
  waiting for transfers between devices  191 us (49%)
  Pallas kernels  74.9 us (19%)
  starting transfers between devices  32.8 us (8%)
  matrix products  26.6 us (7%)
  other arithmetic  20.2 us (5%)
  local copies, waits for them, and re-layouts  18.2 us (5%)
  between operations  15.6 us (4%)
    pallas_call x11, Pallas kernels, call(): pl.pallas_call(kernel, out_shape=tuple(outs) if many else outs, in_specs=...  74.9 us
    ppermute x36, waiting for transfers between devices, swap(): return lax.ppermute(value, 'seq', [(i, i ^ bit) for i in range(SEQ)])  66.6 us
    all_gather x1, waiting for transfers between devices, on_device(): first = lax.all_gather(first_own, 'wt', axis=0, tiled=False)  49.2 us
    ppermute x5, waiting for transfers between devices, send(): return lax.ppermute(value, 'wt', [(at, at ^ bit) for at in range(wt)])  43.1 us
    all_gather x1, waiting for transfers between devices, on_device(): gate_up = lax.all_gather(gate_up_own, 'wt', axis=0, tiled=True)  24.8 us
    ppermute x36, starting transfers between devices, swap(): return lax.ppermute(value, 'seq', [(i, i ^ bit) for i in range(SEQ)])  23.1 us
    dot_general x11, matrix products, dot_nt(): lax.dot_general(left, right, (((1,), (1,)), ((), ())), preferred_element_...  14.7 us
    dot_general x7, matrix products, dot(): return jnp.dot(left, right, preferred_element_type=f32)  11.9 us
  transfers between devices with their start and end apart: 49, of which 25 were waited for; matrix products, arithmetic and copies ran while one was open for 12% of the time, Pallas kernels for 14%

profile of v2, /device:TPU:0, one launch (start us, length us, event | category | flops | bytes accessed | tf_op | source)
XLA Modules:
  0.0 379.5 jit_solution(4006459628063612422)
XLA Ops:
  9.9 3.1 pack_gate_up.1
  13.1 3.0 collective-permute-start.1
  19.4 8.6 %collective-permute-done.1.far_ref = bf16[256,1024]{1,0:T(8,128)(2,1)S(1)} collective-permute-done((bf16[256,1024]{1,0:T(8,128)(2,1)S(1)}, bf16[256,1024]{1,0:T(8,128)(2,1)S(1)}, u32[]{:S(2)}, u32[]{:S(2)}) %collective-permute-start.1) | collective-permute-done | bytes 524320 | tf_op jit(solution)/shard_map/ppermute | solution.py:74
  32.7 49.2 %all-gather.6.cloned.1.call-done = bf16[1856,1024]{1,0:T(8,128)(2,1)} async-done(((bf16[232,1024]{1,0:T(8,128)(2,1)}), bf16[1856,1024]{1,0:T(8,128)(2,1)}) %all-gather.6.cloned.1.call-update) | async-done | bytes 3801104 | tf_op jit(solution)/shard_map/all_gather | solution.py:389
  83.0 7.3 %prepare.1 = (bf16[1024,768]{1,0:T(8,128)(2,1)}, bf16[1024,256]{1,0:T(8,128)(2,1)}, bf16[768,1024]{1,0:T(8,128)(2,1)}, f32[8,1024]{1,0:T(8,128)}, bf16[1024,1024]{1,0:T(8,128)(2,1)}) custom-call(bf16[8,232,1024]{2,1,0:T(8,128)(2,1)} %bitcast.89, bf16[256,1024]{1,0:T(8,128)(2,1)} %own_ref.1, bf16[256,1024]{1,0:T(8,128)(2,1)} %copy-done.17, ...), custom_call_target="tpu_custom_call" | custom-call | bytes 5898240 | tf_op jit(solution)/shard_map/prepare/pallas_call | solution.py:50
  91.8 12.9 %attend_forward.1 = (bf16[1024,256]{1,0:T(8,128)(2,1)}, bf16[1024,256]{1,0:T(8,128)(2,1)}, bf16[1024,256]{1,0:T(8,128)(2,1)}, bf16[1024,256]{1,0:T(8,128)(2,1)}, f32[2,4,8,256]{3,2,1,0:T(8,128)}) custom-call(bf16[1024,1024]{1,0:T(8,128)(2,1)} %get-tuple-element.47.low_ref, bf16[1024,768]{1,0:T(8,128)(2,1)} %get-tuple-element.48.weight_ref, ...), custom_call_target="tpu_custom_call" | custom-call | flops 2684354560 | bytes 5275648 | tf_op jit(solution)/shard_map/attend_forward/pallas_call | solution.py:50
  110.4 3.2 arrange.1
  118.9 24.8 %all-gather.4.cloned.1.call-done = bf16[1024,1536]{1,0:T(8,128)(2,1)} async-done(((bf16[128,1536]{1,0:T(8,128)(2,1)}), bf16[1024,1536]{1,0:T(8,128)(2,1)}) %all-gather.4.cloned.1.call-update) | async-done | bytes 3145744 | tf_op jit(solution)/shard_map/all_gather | solution.py:394
  143.7 3.9 %fusion.19 = f32[512,1536]{1,0:T(8,128)S(1)} fusion(bf16[1024,1536]{1,0:T(8,128)(2,1)} %all-gather.4.cloned.1.call-done, bf16[256,1024]{1,0:T(8,128)(2,1)} %collective-permute-done.9.refs_1_, bf16[256,1024]{1,0:T(8,128)(2,1)S(1)} %multiply_convert_fusion.7.refs_0_), kind=kOutput, calls=%fused_computation.52 | convolution fusion | flops 1612709888 | bytes 7340032 | tf_op jit(solution)/shard_map/dot_general | solution.py:25
  150.3 3.0 fusion.23
  160.5 12.4 %collective-permute-done.14 = bf16[256,1024]{1,0:T(8,128)(2,1)S(1)} collective-permute-done((bf16[256,1024]{1,0:T(8,128)(2,1)S(1)}, bf16[256,1024]{1,0:T(8,128)(2,1)S(1)}, u32[]{:S(2)}, u32[]{:S(2)}) %collective-permute-start.14) | collective-permute-done | bytes 524320 | tf_op jit(solution)/shard_map/ppermute | solution.py:74
  180.1 9.6 %collective-permute-done.16.refs_6_ = bf16[256,1024]{1,0:T(8,128)(2,1)S(1)} collective-permute-done((bf16[256,1024]{1,0:T(8,128)(2,1)S(1)}, bf16[256,1024]{1,0:T(8,128)(2,1)S(1)}, u32[]{:S(2)}, u32[]{:S(2)}) %collective-permute-start.16) | collective-permute-done | bytes 524320 | tf_op jit(solution)/shard_map/ppermute | solution.py:74
  197.4 10.8 %feed_weights.1 = bf16[8,576,512]{2,1,0:T(8,128)(2,1)} custom-call(bf16[256,1024]{1,0:T(8,128)(2,1)} %copy-done.24, bf16[256,1024]{1,0:T(8,128)(2,1)} %collective-permute-done.9.refs_1_, bf16[256,1024]{1,0:T(8,128)(2,1)} %collective-permute-done.10.refs_2_, bf16[256,1024]{1,0:T(8,128)(2,1)} %copy-done.44, bf16[256,1024]{1,0:T(8,128)(2,1)} %copy-done.25, ...), custom_call_target="tpu_custom_call" | custom-call | flops 4831838208 | bytes 8912896 | tf_op jit(solution)/shard_map/feed_weights/pallas_call | solution.py:50
  208.3 3.3 convolution_convert_fusion.3
  213.5 12.4 %collective-permute-done.20 = bf16[256,1024]{1,0:T(8,128)(2,1)S(1)} collective-permute-done((bf16[256,1024]{1,0:T(8,128)(2,1)S(1)}, bf16[256,1024]{1,0:T(8,128)(2,1)S(1)}, u32[]{:S(2)}, u32[]{:S(2)}) %collective-permute-start.20) | collective-permute-done | bytes 524320 | tf_op jit(solution)/shard_map/ppermute | solution.py:74
  230.5 3.2 output_weights.1
  242.6 12.3 %collective-permute-done.23.refs_2_ = bf16[256,256]{1,0:T(8,128)(2,1)S(1)} collective-permute-done((bf16[256,256]{1,0:T(8,128)(2,1)S(1)}, bf16[256,256]{1,0:T(8,128)(2,1)S(1)}, u32[]{:S(2)}, u32[]{:S(2)}) %collective-permute-start.23) | collective-permute-done | bytes 131104 | tf_op jit(solution)/shard_map/ppermute | solution.py:74
  256.9 14.0 %attend_backward.1.grad_ref = bf16[1024,768]{1,0:T(8,128)(2,1)} custom-call(bf16[1024,256]{1,0:T(8,128)(2,1)} %get-tuple-element.59.query_ref, bf16[1024,256]{1,0:T(8,128)(2,1)} %get-tuple-element.60.key_ref, bf16[1024,256]{1,0:T(8,128)(2,1)} %get-tuple-element.61.value_ref, f32[2,4,8,256]{3,2,1,0:T(8,128)} %get-tuple-element.62.log_ref, ...), custom_call_target="tpu_custom_call" | custom-call | flops 2684354560 | bytes 3768320 | tf_op jit(solution)/shard_map/attend_backward/pallas_call | solution.py:50
  271.9 6.5 %last_weights.1 = bf16[8,136,1024]{2,1,0:T(8,128)(2,1)} custom-call(s32[8]{0:T(128)} %stack.63.at_ref, bf16[1024,1024]{1,0:T(8,128)(2,1)} %get-tuple-element.47.low_ref, bf16[1024,768]{1,0:T(8,128)(2,1)} %attend_backward.1.grad_ref, f32[1024,256]{1,0:T(8,128)} %get-tuple-element.67.keep_ref, bf16[1024,256]{1,0:T(8,128)(2,1)} %copy-done.18, ...), custom_call_target="tpu_custom_call" | custom-call | flops 1610612736 | bytes 5898272 | tf_op jit(solution)/shard_map/last_weights/pallas_call | solution.py:50
  285.5 14.6 %collective-permute-done.35 = bf16[2,136,1024]{2,1,0:T(8,128)(2,1)S(1)} collective-permute-done((bf16[2,136,1024]{2,1,0:T(8,128)(2,1)S(1)}, bf16[2,136,1024]{2,1,0:T(8,128)(2,1)S(1)}, u32[]{:S(2)}, u32[]{:S(2)}) %collective-permute-start.35) | collective-permute-done | bytes 557088 | tf_op jit(solution)/shard_map/ppermute | solution.py:344
  300.1 11.9 %collective-permute-done.36 = bf16[2,136,1024]{2,1,0:T(8,128)(2,1)S(1)} collective-permute-done((bf16[2,136,1024]{2,1,0:T(8,128)(2,1)S(1)}, bf16[2,136,1024]{2,1,0:T(8,128)(2,1)S(1)}, u32[]{:S(2)}, u32[]{:S(2)}) %collective-permute-start.36) | collective-permute-done | bytes 557088 | tf_op jit(solution)/shard_map/ppermute | solution.py:344
  313.3 3.5 collective-permute-start.37
  325.1 16.1 %collective-permute-done.38 = bf16[136,1024]{1,0:T(8,128)(2,1)} collective-permute-done((bf16[136,1024]{1,0:T(8,128)(2,1)}, bf16[136,1024]{1,0:T(8,128)(2,1)}, u32[]{:S(2)}, u32[]{:S(2)}) %collective-permute-start.38) | collective-permute-done | bytes 278560 | tf_op jit(solution)/shard_map/ppermute | solution.py:344
  364.0 8.5 %unpack_feed.1 = (f32[128,2816]{1,0:T(8,128)}, f32[128,2816]{1,0:T(8,128)}, f32[352,1024]{1,0:T(8,128)}) custom-call(s32[1]{0:T(128)} %bitcast.place_ref, bf16[576,512]{1,0:T(8,128)(2,1)} %bitcast.91, bf16[576,512]{1,0:T(8,128)(2,1)} %copy-done.14, bf16[576,512]{1,0:T(8,128)(2,1)} %collective-permute-done.44.refs_2_, bf16[576,512]{1,0:T(8,128)(2,1)} %copy-done.15), custom_call_target="tpu_custom_call" | custom-call | bytes 2359300 | tf_op jit(solution)/shard_map/unpack_feed/pallas_call | solution.py:50
  (275 shorter events, 105.5 us)
Async XLA Ops:
  7.2 74.8 %all-gather.6.cloned.1.call-start = ((), (), s32[]{:S(2)}) async-start(), calls=%async_computation.3 | async-start | bytes 4276224 | tf_op jit(solution)/shard_map/all_gather | solution.py:389
  9.8 133.9 %all-gather.4.cloned.1.call-start = ((), (), s32[]{:S(2)}) async-start(), calls=%async_computation.1 | async-start | bytes 3538944 | tf_op jit(solution)/shard_map/all_gather | solution.py:394
  13.0 311.0 %reduce-scatter.2.cloned.1.call-start = ((), (), s32[]{:S(2)}) async-start(), calls=%async_computation.2 | async-start | bytes 5308416 | tf_op jit(solution)/shard_map/reduce_scatter | solution.py:508
  13.1 15.0 %collective-permute-start.1 = (bf16[256,1024]{1,0:T(8,128)(2,1)S(1)}, bf16[256,1024]{1,0:T(8,128)(2,1)S(1)}, u32[]{:S(2)}, u32[]{:S(2)}) collective-permute-start(bf16[256,1024]{1,0:T(8,128)(2,1)S(1)} %copy-done.3), channel_id=1, source_target_pairs={{0,2},{1,3},{2,0},{3,1},{4,6},{5,7},{6,4},{7,5},{8,10},{9,11},{10,... | collective-permute-start | bytes 1572872 | tf_op jit(solution)/shard_map/ppermute | solution.py:74
  16.1 16.6 %collective-permute-start = (bf16[256,1024]{1,0:T(8,128)(2,1)S(1)}, bf16[256,1024]{1,0:T(8,128)(2,1)S(1)}, u32[]{:S(2)}, u32[]{:S(2)}) collective-permute-start(bf16[256,1024]{1,0:T(8,128)(2,1)S(1)} %copy-done.3), channel_id=1, source_target_pairs={{0,1},{1,0},{2,3},{3,2},{4,5},{5,4},{6,7},{7,6},{8,9},{9,8},{10,11... | collective-permute-start | bytes 1572872 | tf_op jit(solution)/shard_map/ppermute | solution.py:74
  90.3 14.3 %collective-permute-start.7 = (bf16[1024,256]{1,0:T(8,128)(2,1)}, bf16[1024,256]{1,0:T(8,128)(2,1)S(1)}, u32[]{:S(2)}, u32[]{:S(2)}) collective-permute-start(bf16[1024,256]{1,0:T(8,128)(2,1)} %get-tuple-element.50.refs_0_), channel_id=1, source_target_pairs={{0,2},{1,3},{2,0},{3,1},{4,6},{5,7},{6,4},{7,5},{8,10},{9,11},{10,... | collective-permute-start | bytes 1572872 | tf_op jit(solution)/shard_map/ppermute | solution.py:74
  91.8 17.1 %collective-permute-start.6 = (bf16[1024,256]{1,0:T(8,128)(2,1)}, bf16[1024,256]{1,0:T(8,128)(2,1)S(1)}, u32[]{:S(2)}, u32[]{:S(2)}) collective-permute-start(bf16[1024,256]{1,0:T(8,128)(2,1)} %get-tuple-element.50.refs_0_), channel_id=1, source_target_pairs={{0,1},{1,0},{2,3},{3,2},{4,5},{5,4},{6,7},{7,6},{8,9},{9,8},{10,11... | collective-permute-start | bytes 1572872 | tf_op jit(solution)/shard_map/ppermute | solution.py:74
  117.7 26.0 %collective-permute-start.9 = (bf16[256,1024]{1,0:T(8,128)(2,1)S(1)}, bf16[256,1024]{1,0:T(8,128)(2,1)}, u32[]{:S(2)}, u32[]{:S(2)}) collective-permute-start(bf16[256,1024]{1,0:T(8,128)(2,1)S(1)} %multiply_convert_fusion.7.refs_0_), channel_id=1, source_target_pairs={{0,1},{1,0},{2,3},{3,2},{4,5},{5,4},{6,7},{7,6},{8,9},{9,8},{10,11... | collective-permute-start | bytes 1572872 | tf_op jit(solution)/shard_map/ppermute | solution.py:74
  118.2 29.9 %collective-permute-start.10 = (bf16[256,1024]{1,0:T(8,128)(2,1)S(1)}, bf16[256,1024]{1,0:T(8,128)(2,1)}, u32[]{:S(2)}, u32[]{:S(2)}) collective-permute-start(bf16[256,1024]{1,0:T(8,128)(2,1)S(1)} %multiply_convert_fusion.7.refs_0_), channel_id=1, source_target_pairs={{0,2},{1,3},{2,0},{3,1},{4,6},{5,7},{6,4},{7,5},{8,10},{9,11},{10,... | collective-permute-start | bytes 1572872 | tf_op jit(solution)/shard_map/ppermute | solution.py:74
  158.7 14.2 %collective-permute-start.14 = (bf16[256,1024]{1,0:T(8,128)(2,1)S(1)}, bf16[256,1024]{1,0:T(8,128)(2,1)S(1)}, u32[]{:S(2)}, u32[]{:S(2)}) collective-permute-start(bf16[256,1024]{1,0:T(8,128)(2,1)S(1)} %fusion.5), channel_id=1, source_target_pairs={{0,2},{1,3},{2,0},{3,1},{4,6},{5,7},{6,4},{7,5},{8,10},{9,11},{10,... | collective-permute-start | bytes 1572872 | tf_op jit(solution)/shard_map/ppermute | solution.py:74
  175.4 14.3 %collective-permute-start.16 = (bf16[256,1024]{1,0:T(8,128)(2,1)S(1)}, bf16[256,1024]{1,0:T(8,128)(2,1)S(1)}, u32[]{:S(2)}, u32[]{:S(2)}) collective-permute-start(bf16[256,1024]{1,0:T(8,128)(2,1)S(1)} %get-tuple-element.100.refs_4_), channel_id=1, source_target_pairs={{0,2},{1,3},{2,0},{3,1},{4,6},{5,7},{6,4},{7,5},{8,10},{9,11},{10,... | collective-permute-start | bytes 1572872 | tf_op jit(solution)/shard_map/ppermute | solution.py:74
  211.8 14.2 %collective-permute-start.20 = (bf16[256,1024]{1,0:T(8,128)(2,1)S(1)}, bf16[256,1024]{1,0:T(8,128)(2,1)S(1)}, u32[]{:S(2)}, u32[]{:S(2)}) collective-permute-start(bf16[256,1024]{1,0:T(8,128)(2,1)S(1)} %add_convert_fusion.2), channel_id=1, source_target_pairs={{0,2},{1,3},{2,0},{3,1},{4,6},{5,7},{6,4},{7,5},{8,10},{9,11},{10,... | collective-permute-start | bytes 1572872 | tf_op jit(solution)/shard_map/ppermute | solution.py:74
  233.8 37.1 %collective-permute-start.25 = (bf16[1024,256]{1,0:T(8,128)(2,1)}, bf16[1024,256]{1,0:T(8,128)(2,1)S(1)}, u32[]{:S(2)}, u32[]{:S(2)}) collective-permute-start(bf16[1024,256]{1,0:T(8,128)(2,1)} %get-tuple-element.68), channel_id=1, source_target_pairs={{0,1},{1,0},{2,3},{3,2},{4,5},{5,4},{6,7},{7,6},{8,9},{9,8},{10,11... | collective-permute-start | bytes 1572872 | tf_op jit(solution)/shard_map/ppermute | solution.py:74
  237.2 33.7 %collective-permute-start.26 = (bf16[1024,256]{1,0:T(8,128)(2,1)S(1)}, bf16[1024,256]{1,0:T(8,128)(2,1)S(1)}, u32[]{:S(2)}, u32[]{:S(2)}) collective-permute-start(bf16[1024,256]{1,0:T(8,128)(2,1)S(1)} %add_convert_fusion.1), channel_id=1, source_target_pairs={{0,2},{1,3},{2,0},{3,1},{4,6},{5,7},{6,4},{7,5},{8,10},{9,11},{10,... | collective-permute-start | bytes 1572872 | tf_op jit(solution)/shard_map/ppermute | solution.py:74
  239.5 15.4 %collective-permute-start.23 = (bf16[256,256]{1,0:T(8,128)(2,1)S(1)}, bf16[256,256]{1,0:T(8,128)(2,1)S(1)}, u32[]{:S(2)}, u32[]{:S(2)}) collective-permute-start(bf16[256,256]{1,0:T(8,128)(2,1)S(1)} %get-tuple-element.106), channel_id=1, source_target_pairs={{0,2},{1,3},{2,0},{3,1},{4,6},{5,7},{6,4},{7,5},{8,10},{9,11},{10,... | collective-permute-start | bytes 393224 | tf_op jit(solution)/shard_map/ppermute | solution.py:74
  240.0 16.2 %collective-permute-start.24 = (bf16[256,256]{1,0:T(8,128)(2,1)S(1)}, bf16[256,256]{1,0:T(8,128)(2,1)S(1)}, u32[]{:S(2)}, u32[]{:S(2)}) collective-permute-start(bf16[256,256]{1,0:T(8,128)(2,1)S(1)} %get-tuple-element.105), channel_id=1, source_target_pairs={{0,3},{1,2},{2,1},{3,0},{4,7},{5,6},{6,5},{7,4},{8,11},{9,10},{10,... | collective-permute-start | bytes 393224 | tf_op jit(solution)/shard_map/ppermute | solution.py:74
  280.2 19.9 %collective-permute-start.35 = (bf16[2,136,1024]{2,1,0:T(8,128)(2,1)S(1)}, bf16[2,136,1024]{2,1,0:T(8,128)(2,1)S(1)}, u32[]{:S(2)}, u32[]{:S(2)}) collective-permute-start(bf16[2,136,1024]{2,1,0:T(8,128)(2,1)S(1)} %get-tuple-element.99), channel_id=1, source_target_pairs={{0,4},{4,0},{8,12},{12,8},{16,20},{20,16},{24,28},{28,24},{1,5},{5... | collective-permute-start | bytes 1671176 | tf_op jit(solution)/shard_map/ppermute | solution.py:344
  280.7 31.3 %collective-permute-start.36 = (bf16[2,136,1024]{2,1,0:T(8,128)(2,1)S(1)}, bf16[2,136,1024]{2,1,0:T(8,128)(2,1)S(1)}, u32[]{:S(2)}, u32[]{:S(2)}) collective-permute-start(bf16[2,136,1024]{2,1,0:T(8,128)(2,1)S(1)} %get-tuple-element.98), channel_id=1, source_target_pairs={{0,4},{4,0},{8,12},{12,8},{16,20},{20,16},{24,28},{28,24},{1,5},{5... | collective-permute-start | bytes 1671176 | tf_op jit(solution)/shard_map/ppermute | solution.py:344
  282.9 35.6 %collective-permute-start.29 = (bf16[256,1024]{1,0:T(8,128)(2,1)S(1)}, bf16[256,1024]{1,0:T(8,128)(2,1)S(1)}, u32[]{:S(2)}, u32[]{:S(2)}) collective-permute-start(bf16[256,1024]{1,0:T(8,128)(2,1)S(1)} %fusion.6), channel_id=1, source_target_pairs={{0,2},{1,3},{2,0},{3,1},{4,6},{5,7},{6,4},{7,5},{8,10},{9,11},{10,... | collective-permute-start | bytes 1572872 | tf_op jit(solution)/shard_map/ppermute | solution.py:74
  285.1 33.4 %collective-permute-start.28 = (bf16[256,1024]{1,0:T(8,128)(2,1)S(1)}, bf16[256,1024]{1,0:T(8,128)(2,1)S(1)}, u32[]{:S(2)}, u32[]{:S(2)}) collective-permute-start(bf16[256,1024]{1,0:T(8,128)(2,1)S(1)} %convolution_convert_fusion.1), channel_id=1, source_target_pairs={{0,1},{1,0},{2,3},{3,2},{4,5},{5,4},{6,7},{7,6},{8,9},{9,8},{10,11... | collective-permute-start | bytes 1572872 | tf_op jit(solution)/shard_map/ppermute | solution.py:74
  316.8 24.4 %collective-permute-start.38 = (bf16[136,1024]{1,0:T(8,128)(2,1)}, bf16[136,1024]{1,0:T(8,128)(2,1)}, u32[]{:S(2)}, u32[]{:S(2)}) collective-permute-start(bf16[136,1024]{1,0:T(8,128)(2,1)} %get-tuple-element.103), channel_id=1, source_target_pairs={{0,16},{4,20},{8,24},{12,28},{16,0},{20,4},{24,8},{28,12},{1,17},{... | collective-permute-start | bytes 835592 | tf_op jit(solution)/shard_map/ppermute | solution.py:344
  317.6 23.6 %collective-permute-start.39 = (bf16[136,1024]{1,0:T(8,128)(2,1)}, bf16[136,1024]{1,0:T(8,128)(2,1)}, u32[]{:S(2)}, u32[]{:S(2)}) collective-permute-start(bf16[136,1024]{1,0:T(8,128)(2,1)} %fusion.63), channel_id=1, source_target_pairs={{0,8},{4,12},{8,0},{12,4},{16,24},{20,28},{24,16},{28,20},{1,9},{5... | collective-permute-start | bytes 835592 | tf_op jit(solution)/shard_map/ppermute | solution.py:344
  322.6 21.4 %collective-permute-start.31 = (f32[8,128]{1,0:T(8,128)}, f32[8,128]{1,0:T(8,128)}, u32[]{:S(2)}, u32[]{:S(2)}) collective-permute-start(f32[8,128]{1,0:T(8,128)} %bitcast_add_fusion), channel_id=1, source_target_pairs={{0,2},{1,3},{2,0},{3,1},{4,6},{5,7},{6,4},{7,5},{8,10},{9,11},{10,... | collective-permute-start | bytes 12296 | tf_op jit(solution)/shard_map/ppermute | solution.py:568
  324.1 29.4 %collective-permute-start.44 = (bf16[576,512]{1,0:T(8,128)(2,1)}, bf16[576,512]{1,0:T(8,128)(2,1)}, u32[]{:S(2)}, u32[]{:S(2)}) collective-permute-start(bf16[576,512]{1,0:T(8,128)(2,1)} %bitcast.90), channel_id=1, source_target_pairs={{0,2},{1,3},{2,0},{3,1},{4,6},{5,7},{6,4},{7,5},{8,10},{9,11},{10,... | collective-permute-start | bytes 1769480 | tf_op jit(solution)/shard_map/ppermute | solution.py:74
  (79 other events, 612.5 us)
Sparse Core Ops, SparseCore 0:
  10.8 71.1 all-gather.5
  84.7 58.9 all-gather.3
  208.4 96.9 reduce-scatter.1

commit v3 on v2

v3 whole, which is shorter than its diff:
```python
import functools

import jax
import jax.numpy as jnp
from jax import lax
from jax.experimental import pallas as pl
from jax.experimental.pallas import tpu as pltpu
from jax.sharding import PartitionSpec as P

HEADS = 8
EPSILON = 1e-06
ROTARY_BASE = 50000.0
DOC_LEN = 8192
DOC_STRIDE = 64
HIDDEN_LOW = -1e30
LOG2_E = 1.4426950408889634
SEQ = 4
GAIN_ROWS = 8
COSTS = dict(
    pack_first=0.04,
    pack_feed=0.08,
    assemble=0.08,
    attend_forward=0.3,
    arrange=0.06,
    feed_weights=0.16,
    down_weights=0.08,
    feed_forward=0.12,
    feed_backward=0.14,
    output_weights=0.06,
    attend_backward=0.28,
    last_weights=0.12,
    join_shares=0.04,
    unpack_feed=0.18,
    unpack_last=0.06,
)

f32 = jnp.float32
bf16 = jnp.bfloat16


def dot(left, right):
    return jnp.dot(left, right, preferred_element_type=f32)


def dot_nt(left, right):
    return lax.dot_general(left, right, (((1,), (1,)), ((), ())), preferred_element_type=f32)


def dot_tn(left, right):
    return lax.dot_general(left, right, (((0,), (0,)), ((), ())), preferred_element_type=f32)


def normed_of(values):
    inverse = lax.rsqrt(jnp.mean(values * values, -1, keepdims=True) + EPSILON)
    return values * inverse, inverse


def norm_back(incoming, normed, inverse, scales):
    scaled = incoming * scales
    return inverse * (scaled - normed * jnp.mean(scaled * normed, -1, keepdims=True))


def call(kernel, outs, *args, smem=0, scratch=(), name=None):
    many = isinstance(outs, (list, tuple))
    whole = pl.BlockSpec(memory_space=pltpu.VMEM)
    return pl.pallas_call(
        kernel,
        out_shape=tuple(outs) if many else outs,
        in_specs=[
            pl.BlockSpec(memory_space=pltpu.SMEM) if at < smem else whole
            for at in range(len(args))
        ],
        out_specs=(whole,) * len(outs) if many else whole,
        scratch_shapes=list(scratch),
        compiler_params=pltpu.CompilerParams(vmem_limit_bytes=56 * 1024 * 1024),
        cost_estimate=pl.CostEstimate(flops=int(COSTS[name] * 1.15e9), transcendentals=0, bytes_accessed=0),
        name=name,
    )(*args)


def shaped(*shape, dtype=bf16):
    return jax.ShapeDtypeStruct(shape, dtype)


def after(value, *others):
    return lax.optimization_barrier((value,) + others)[0]


def swap(value, bit):
    return lax.ppermute(value, "seq", [(i, i ^ bit) for i in range(SEQ)])


def chosen(rows, columns, chunk, padded, place):
    row = lax.broadcasted_iota(jnp.int32, (rows, columns), 0)
    column = lax.broadcasted_iota(jnp.int32, (rows, columns), 1)
    block = column // padded
    inside = column - block * padded
    wanted = block * (SEQ * chunk) + place * chunk + inside
    return jnp.where((row == wanted) & (inside < chunk), 1.0, 0.0).astype(bf16)


def pack_first(place_ref, query_ref, key_ref, value_ref, output_ref, *refs):
    gain_refs, out_ref = refs[:4], refs[4]
    shard, model = query_ref.shape
    part = model // SEQ
    columns = pl.ds(pl.multiple_of(place_ref[0] * part, part), part)
    for at, ref in enumerate((query_ref, key_ref, value_ref, output_ref)):
        out_ref[:shard, at * part:(at + 1) * part] = ref[:, columns]
    out_ref[shard:, :] = jnp.zeros((GAIN_ROWS, model), bf16)
    for at, ref in enumerate(gain_refs):
        out_ref[shard:shard + 1, at * shard:(at + 1) * shard] = ref[...]


def pack_feed(place_ref, gate_ref, up_ref, down_ref, out_ref, down_out_ref):
    place = place_ref[0]
    wide = gate_ref.shape[1] // 2
    narrow = out_ref.shape[1] // 4
    chunk = down_ref.shape[0] // SEQ
    padded = down_out_ref.shape[0]
    pick = chosen(wide, narrow, chunk, padded, place)
    for number, ref in enumerate((gate_ref, up_ref)):
        for half in range(2):
            at = (2 * number + half) * narrow
            out_ref[:, at:at + narrow] = dot(
                ref[:, half * wide:(half + 1) * wide], pick
            ).astype(bf16)
    pick_rows = chosen(SEQ * chunk, padded, chunk, padded, place)
    down_out_ref[...] = dot_tn(pick_rows, down_ref[...]).astype(bf16)


def assemble(at_ref, *refs):
    blocks, out_ref = refs[:-1], refs[-1]
    rows = blocks[0].shape[0]
    for step, block in enumerate(blocks):
        out_ref[pl.ds(pl.multiple_of(at_ref[step] * rows, rows), rows), :] = block[...]


def join_shares(gate_ref, up_ref, down_ref, out_ref):
    piece = out_ref.shape[1]
    row = 0
    for ref in (gate_ref, up_ref, down_ref):
        for at in range(0, ref.shape[1], piece):
            out_ref[row:row + ref.shape[0], :] = ref[:, at:at + piece]
            row += ref.shape[0]


def unpack_feed(place_ref, *refs, shard, padded):
    blocks, (gate_ref, up_ref, down_ref) = refs[:SEQ], refs[SEQ:]
    place = place_ref[0]
    chunk = down_ref.shape[0] // SEQ
    model = down_ref.shape[1]
    piece = blocks[0].shape[1]
    wide = gate_ref.shape[1] // 2
    below = blocks[0].shape[0] - model // piece * padded
    pieces = below // shard // 2
    narrow = pieces * piece // 2
    pick = jnp.concatenate(
        [chosen(wide, narrow, chunk, padded, place ^ at) for at in range(SEQ)], 1
    )
    for number, out_ref in enumerate((gate_ref, up_ref)):
        joined = [
            jnp.concatenate(
                [
                    ref[(number * pieces + at) * shard:(number * pieces + at + 1) * shard, :]
                    for at in range(pieces)
                ], 1,
            )
            for ref in blocks
        ]
        for half in range(2):
            parts = [part[:, half * narrow:(half + 1) * narrow] for part in joined]
            out_ref[:, half * wide:(half + 1) * wide] = dot_nt(jnp.concatenate(parts, 1), pick)
    rows = jnp.concatenate(
        [chosen(SEQ * chunk, padded, chunk, padded, place ^ at) for at in range(SEQ)], 1
    )
    for at in range(model // piece):
        parts = [ref[below + at * padded:below + (at + 1) * padded, :] for ref in blocks]
        down_ref[:, at * piece:(at + 1) * piece] = dot(rows, jnp.concatenate(parts, 0))


def unpack_last(place_ref, *refs, shard):
    blocks, outs = refs[:SEQ], refs[SEQ:]
    place = place_ref[0]
    part = blocks[0].shape[1] // SEQ
    for step, block in enumerate(blocks):
        columns = pl.ds(pl.multiple_of((place ^ step) * part, part), part)
        for at in range(4):
            outs[at][:, columns] = block[:shard, at * part:(at + 1) * part].astype(f32)
    outs[4][...] = sum(block[shard:, :].astype(f32) for block in blocks)


def arrange(place_ref, *refs):
    blocks, out_ref = refs[:SEQ], refs[SEQ]
    place = place_ref[0]
    part = blocks[0].shape[1]
    for step in range(SEQ):
        rows = pl.ds(pl.multiple_of((place ^ step) * part, part), part)
        for other in range(SEQ):
            columns = pl.ds(pl.multiple_of((place ^ other) * part, part), part)
            out_ref[step * part:(step + 1) * part, columns] = blocks[other][rows, :]


def turn(rows, cosine, sine):
    return rows * cosine + pltpu.roll(rows, rows.shape[-1] // 2, axis=1) * sine


def visible(key_code, query_code, tile):
    key_wide = jnp.concatenate([key_code] * (tile // 128), axis=1)
    return (key_wide <= query_code[0:1, :]) & (key_wide >= query_code[1:2, :])


def key_codes(query_code_ref, key_code_ref):
    tiles, _, tile = query_code_ref.shape
    for step in range(tiles):
        wide = jnp.broadcast_to(query_code_ref[step, 0:1, :], (128, tile))
        key_code_ref[step * tile:(step + 1) * tile, :] = wide.T


def attend_forward(
    weight_ref, cos_ref, sin_ref, query_code_ref, own_ref, near_ref, far_ref, both_ref,
    low_ref, query_ref, key_ref, value_ref, out_ref, log_ref, gain_ref, token_ref, key_code_ref,
):
    window, model = low_ref.shape
    wt, shard, _ = weight_ref.shape
    shard = shard - GAIN_ROWS
    tiles, _, tile = query_code_ref.shape
    width = cos_ref.shape[1]
    heads = query_ref.shape[1] // width
    scale = LOG2_E * width ** (-0.5)
    for at in range(wt):
        gain_ref[0:1, at * shard:(at + 1) * shard] = weight_ref[
            at, shard:shard + 1, :shard
        ].astype(f32)

    for step, ref in enumerate((own_ref, near_ref, far_ref, both_ref)):
        token_ref[step * tile:(step + 1) * tile, :] = ref[...]
    key_codes(query_code_ref, key_code_ref)

    def project(step, carry):
        rows = pl.ds(pl.multiple_of(step * tile, tile), tile)
        normed, _ = normed_of(token_ref[rows, :].astype(f32))
        low = (normed * gain_ref[0:1, :]).astype(bf16)
        low_ref[rows, :] = low
        weight = weight_ref[:, :shard, :3 * heads * width].reshape(model, 3 * heads * width)
        raw = dot(low, weight)
        cosine = cos_ref[rows, :]
        sine = sin_ref[rows, :]
        for head in range(heads):
            at = head * width
            query_ref[rows, at:at + width] = turn(raw[:, at:at + width], cosine, sine).astype(bf16)
            at = (heads + head) * width
            key_ref[rows, head * width:(head + 1) * width] = turn(
                raw[:, at:at + width], cosine, sine
            ).astype(bf16)
        value_ref[rows, :] = raw[:, 2 * heads * width:].astype(bf16)
        return carry

    lax.fori_loop(0, window // tile, project, 0)
    for head in range(heads):
        cols = slice(head * width, (head + 1) * width)
        value_turned = value_ref[:, cols].astype(f32).T.astype(bf16)

        def one_tile(step, carry):
            rows = pl.ds(pl.multiple_of(step * tile, tile), tile)
            scores = dot_nt(key_ref[:, cols], query_ref[rows, cols])
            shown = visible(key_code_ref[...], query_code_ref[step], tile)
            scores = jnp.where(shown, scores * scale, HIDDEN_LOW)
            top = jnp.max(scores, 0, keepdims=True)
            weights = jnp.exp2(scores - top)
            total = jnp.sum(weights, 0, keepdims=True)
            result = dot(value_turned, weights.astype(bf16)) * (1.0 / total)
            out_ref[rows, cols] = result.T.astype(bf16)
            log_ref[head, step] = jnp.broadcast_to(top + jnp.log2(total), (8, tile))
            return carry

        lax.fori_loop(0, tiles, one_tile, 0)


def attend_backward(
    query_ref, key_ref, value_ref, log_ref, cos_ref, sin_ref, query_code_ref, *refs,
):
    incoming_refs = refs[:SEQ]
    grad_ref, key_sum, value_sum, incoming_ref, key_code_ref = refs[SEQ:]
    key_codes(query_code_ref, key_code_ref)
    tiles, _, tile = query_code_ref.shape
    width = cos_ref.shape[1]
    heads = query_ref.shape[1] // width
    factor = width ** (-0.5)
    scale = LOG2_E * factor
    for step, ref in enumerate(incoming_refs):
        incoming_ref[step * tile:(step + 1) * tile, :] = ref[...]
    for head in range(heads):
        cols = slice(head * width, (head + 1) * width)
        key_turned = key_ref[:, cols].astype(f32).T.astype(bf16)
        key_sum[...] = jnp.zeros_like(key_sum)
        value_sum[...] = jnp.zeros_like(value_sum)

        def one_tile(step, carry):
            rows = pl.ds(pl.multiple_of(step * tile, tile), tile)
            queries = query_ref[rows, cols]
            incoming = incoming_ref[rows, cols]
            scores = dot_nt(key_ref[:, cols], queries)
            shown = visible(key_code_ref[...], query_code_ref[step], tile)
            probs = jnp.where(shown, jnp.exp2(scores * scale - log_ref[head, step, 0:1, :]), 0.0)
            value_sum[...] += dot(probs.astype(bf16), incoming)
            prob_grad = dot_nt(value_ref[:, cols], incoming)
            inner = jnp.sum(probs * prob_grad, 0, keepdims=True)
            score_grad = (probs * (prob_grad - inner)).astype(bf16)
            key_sum[...] += dot(score_grad, queries)
            query_grad = (dot(key_turned, score_grad) * factor).T
            grad_ref[rows, cols] = turn(query_grad, cos_ref[rows, :], -sin_ref[rows, :]).astype(bf16)
            return carry

        lax.fori_loop(0, tiles, one_tile, 0)
        at = (heads + head) * width
        grad_ref[:, at:at + width] = turn(
            key_sum[...] * factor, cos_ref[...], -sin_ref[...]
        ).astype(bf16)
        at = (2 * heads + head) * width
        grad_ref[:, at:at + width] = value_sum[...].astype(bf16)


def feed_forward(
    first_ref, second_ref, weight_ref, down_ref, both_ref, active_ref, keep_ref, send_ref,
):
    rows, model = first_ref.shape
    half = down_ref.shape[0]
    low = jnp.concatenate([first_ref[...], second_ref[...]], 0)
    step = 256
    for at in range(0, half, step):
        gate_value = dot(low, weight_ref[:, at:at + step])
        up_value = dot(low, weight_ref[:, half + at:half + at + step])
        both_ref[:, at:at + step] = gate_value.astype(bf16)
        both_ref[:, half + at:half + at + step] = up_value.astype(bf16)
        active_ref[:, at:at + step] = (gate_value * jax.nn.sigmoid(gate_value) * up_value).astype(
            bf16
        )
    for at in range(0, model, step):
        total = dot(active_ref[...], down_ref[:, at:at + step])
        keep_ref[:, at:at + step] = total[:rows]
        send_ref[:, at:at + step] = total[rows:].astype(bf16)


def feed_backward(
    first_ref, second_ref, both_ref, weight_ref, down_ref, grad_ref, keep_ref, send_ref,
):
    rows, model = first_ref.shape
    half = down_ref.shape[0]
    low = jnp.concatenate([first_ref[...], second_ref[...]], 0)
    step = 256
    for at in range(0, half, step):
        active_grad = dot_nt(low, down_ref[at:at + step, :])
        gate_value = both_ref[:, at:at + step].astype(f32)
        up_value = both_ref[:, half + at:half + at + step].astype(f32)
        share = jax.nn.sigmoid(gate_value)
        scaled = active_grad * share
        grad_ref[:, at:at + step] = (
            scaled * up_value * (1.0 + gate_value * (1.0 - share))
        ).astype(bf16)
        grad_ref[:, half + at:half + at + step] = (scaled * gate_value).astype(bf16)
    for at in range(0, model, step):
        total = dot_nt(grad_ref[...], weight_ref[at:at + step, :])
        keep_ref[:, at:at + step] = total[:rows]
        send_ref[:, at:at + step] = total[rows:].astype(bf16)


def halves_out(side, full, shard, columns, keep_ref, send_ref):
    for level in range(full.shape[0] // shard // 2):
        to = slice(level * shard, (level + 1) * shard)
        for at, ref in ((2 * level + side, keep_ref), (2 * level + 1 - side, send_ref)):
            rows = pl.ds(pl.multiple_of(at * shard, shard), shard)
            ref[to, :] = full[rows, columns]


def feed_weights(
    side_ref, own_ref, near_ref, far_ref, both_ref, near_grad, far_grad,
    gate_keep, gate_send, up_keep, up_send, full, *, shard,
):
    low = jnp.concatenate([own_ref[...], near_ref[...], far_ref[...], both_ref[...]], 0)
    grad = jnp.concatenate([near_grad[...], far_grad[...]], 0)
    full[...] = dot_tn(low, grad).astype(bf16)
    half = gate_keep.shape[1]
    side = side_ref[0]
    halves_out(side, full, shard, slice(0, half), gate_keep, gate_send)
    halves_out(side, full, shard, slice(half, 2 * half), up_keep, up_send)


def down_weights(
    side_ref, own_ref, near_ref, far_ref, both_ref, near_active, far_active, keep_ref, send_ref,
    full, *, padded,
):
    grad = jnp.concatenate([own_ref[...], near_ref[...], far_ref[...], both_ref[...]], 0)
    active = jnp.concatenate([near_active[...], far_active[...]], 0)
    full[...] = dot_tn(active, grad).astype(bf16)
    halves_out(side_ref[0], full, padded, slice(None), keep_ref, send_ref)


def output_weights(place_ref, low_ref, *refs):
    pieces, outs = refs[:SEQ], refs[SEQ:]
    place = place_ref[0]
    part = outs[0].shape[1]
    for step in range(SEQ):
        columns = pl.ds(pl.multiple_of((place ^ step) * part, part), part)
        for other in range(SEQ):
            rows = pl.ds(pl.multiple_of((place ^ other) * part, part), part)
            outs[step][rows, :] = dot_tn(pieces[other][...], low_ref[:, columns]).astype(
                outs[step].dtype
            )


def last_weights(at_ref, low_ref, grad_ref, keep_ref, near_ref, far_ref, sum_ref, *refs):
    out_ref, full = refs
    wt, total, model = out_ref.shape
    shard = total - GAIN_ROWS
    part = keep_ref.shape[1]
    full[:, :3 * part] = dot_tn(low_ref[...], grad_ref[...]).astype(bf16)
    full[:, 3 * part:] = (
        keep_ref[...] + near_ref[...].astype(f32) + far_ref[...].astype(f32)
    ).astype(bf16)
    for step in range(wt):
        at = at_ref[step]
        out_ref[step, :shard, :] = full[pl.ds(pl.multiple_of(at * shard, shard), shard), :]
        out_ref[step, shard:, :] = sum_ref[at]


def pick_level(level, table):
    return jnp.where(
        level == 0, table[0],
        jnp.where(level == 1, table[1], jnp.where(level == 2, table[2], table[3])),
    )


def gather_start(own):
    level = lax.axis_index("wt") // 2

    def send(value, pairs):
        return lax.ppermute(value, "wt", pairs)

    def across(value):
        return send(value, [(at, at ^ 1) for at in range(8)])

    right = send(own, [(at, at + 2) for at in range(6)])
    left = send(own, [(at, at - 2) for at in range(2, 8)])
    own_x = across(own)
    right2 = send(after(right, own_x), [(at, at + 2) for at in range(2, 6)])
    left2 = send(after(left, own_x), [(at, at - 2) for at in range(2, 6)])
    one = jnp.where(level == 0, left, right)
    one_x = across(one)
    onward = after(jnp.where(level == 2, right2, left2), one_x)
    two = jnp.where(level == 0, left2, jnp.where(level == 3, right2, left))
    two_x = across(two)
    third = send(onward, [(4, 6), (5, 7), (2, 0), (3, 1)])
    return (own, one, two, own_x, one_x, two_x), onward, third


def gather_end(started, onward, third):
    here = lax.axis_index("wt")
    level = here // 2
    side = here % 2
    three = jnp.where((level == 1) | (level == 2), onward, third)
    three_x = lax.ppermute(three, "wt", [(at, at ^ 1) for at in range(8)])
    levels = [level] + [
        pick_level(level, table) for table in ((1, 0, 1, 2), (2, 2, 3, 1), (3, 3, 0, 0))
    ]
    whose = [2 * at + side for at in levels] + [2 * at + 1 - side for at in levels]
    blocks = (*started[:3], three, *started[3:], three_x)
    return blocks, jnp.stack(whose).astype(jnp.int32)


def across(value, wt):
    return lax.ppermute(value, "wt", [(at, at ^ 1) for at in range(wt)])


def scatter_levels(value, wt):
    return lax.psum_scatter(
        value, "wt", scatter_dimension=0, tiled=True,
        axis_index_groups=[list(range(side, wt, 2)) for side in range(2)],
    )


def add_low(left, right):
    return (left.astype(f32) + right.astype(f32)).astype(bf16)


def on_device(
    tokens, positions, doc_ids, block_ids, entry_gain, query_weight, key_weight, value_weight,
    output_weight, attend_gain, middle_gain, gate_weight, up_weight, down_weight, closing_gain,
    cotangent,
):
    place = lax.axis_index("seq")
    order = [place ^ step for step in range(SEQ)]
    here = jnp.reshape(place, (1,)).astype(jnp.int32)
    rows, model = tokens.shape
    window = rows * SEQ
    shard = query_weight.shape[0]
    wt = model // shard
    part = model // SEQ
    width = model // HEADS
    heads = HEADS // SEQ
    hidden = gate_weight.shape[1]
    chunk = hidden // (wt * SEQ)
    padded = (chunk + 15) // 16 * 16
    hidden_part = padded * wt
    piece = 256

    def gather_blocks(own):
        far = swap(own, 2)
        near = swap(own, 1)
        return own, near, far, swap(far, 1)

    lines = wt == 8
    first_own = call(
        pack_first, shaped(shard + GAIN_ROWS, model),
        here, query_weight, key_weight, value_weight, output_weight,
        *(gain[None] for gain in (entry_gain, attend_gain, middle_gain, closing_gain)),
        smem=1, name="pack_first",
    )
    first = lax.all_gather(first_own, "wt", axis=0, tiled=False)
    gate_up_own, down_own = call(
        pack_feed, (shaped(shard, 2 * hidden_part), shaped(padded, model)),
        here, gate_weight, up_weight, after(down_weight, first_own), smem=1, name="pack_feed",
    )
    down_part = lax.all_gather(down_own, "wt", axis=0, tiled=True)
    if lines:
        gate_up_blocks, onward, third = gather_start(gate_up_own)
    token_blocks = gather_blocks(tokens)
    cotangent_far = swap(after(cotangent, token_blocks[2]), 2)

    offsets = jnp.arange(window, dtype=jnp.int32)
    leading = doc_ids == doc_ids[0]
    boundary = jnp.sum(leading.astype(jnp.int32))
    places = jnp.where(leading, DOC_LEN - boundary + offsets, offsets - boundary)
    codes = doc_ids * DOC_STRIDE + block_ids
    lows = doc_ids * DOC_STRIDE
    packed = jnp.stack([places, codes, lows]).reshape(3, SEQ, rows)
    packed = jnp.concatenate(
        [lax.dynamic_index_in_dim(packed, at, 1, keepdims=False) for at in order], 1
    )
    half = width // 2
    frequency = ROTARY_BASE ** (-2.0 * jnp.arange(half, dtype=f32) / width)
    angles = packed[0].astype(f32)[:, None] * frequency[None, :]
    cosine = jnp.cos(angles)
    sine = jnp.sin(angles)
    cosine = jnp.concatenate([cosine, cosine], 1)
    sine = jnp.concatenate([-sine, sine], 1)
    query_code = jnp.broadcast_to(
        packed[1:3].astype(f32).reshape(2, SEQ, rows).transpose(1, 0, 2)[:, :, None, :], (SEQ, 2, 4, rows)
    ).transpose(0, 2, 1, 3).reshape(SEQ, 8, rows)

    waited = (cosine, sine, query_code, *token_blocks, cotangent_far)
    if lines:
        waited += (onward,)
    first = after(first, *waited)
    output_own = first[:, :shard, 3 * part:].reshape(model, part)
    gains = first[:, shard, :4 * shard].reshape(wt, 4, shard).transpose(1, 0, 2).reshape(4, model)
    gains = gains.astype(f32)
    first = after(first, output_own)
    if lines:
        gate_up_blocks, sources = gather_end(gate_up_blocks, onward, third)
        first = after(first, gate_up_blocks[3])
    entry_full, attend_full, middle_full, closing_full = [gains[at:at + 1] for at in range(4)]
    low_shape = shaped(window, heads * width)
    pair_cost = 2 * heads * window * window * width
    entry_low, query_low, key_low, value_low, attended, log_totals = call(
        attend_forward,
        (shaped(window, model), low_shape, low_shape, low_shape, low_shape,
         shaped(heads, SEQ, 8, rows, dtype=f32)),
        first, cosine, sine, query_code, *token_blocks,
        scratch=(
            pltpu.VMEM((8, model), f32), pltpu.VMEM((window, model), bf16),
            pltpu.VMEM((window, 128), f32),
        ),
        name="attend_forward",
    )
    output_far = after(swap(output_own, 2), attended)
    output_rows = call(
        arrange, shaped(model, model),
        here, output_own, swap(output_own, 1), output_far, swap(output_far, 1), smem=1,
        name="arrange",
    )

    if lines:
        gate_up = call(
            assemble, shaped(model, 2 * hidden_part),
            sources, *gate_up_blocks[:-1], after(gate_up_blocks[-1], attended), smem=1,
            name="assemble",
        )
    else:
        gate_up = lax.all_gather(gate_up_own, "wt", axis=0, tiled=True)

    def exchange(blocks):
        return [blocks[0], swap(blocks[1], 1), swap(blocks[2], 2), swap(blocks[3], 3)]

    joined = exchange([attended[at * rows:(at + 1) * rows] for at in range(SEQ)])
    joined = [joined[0], joined[1]] + [after(got, gate_up, output_rows) for got in joined[2:]]
    inputs = tokens.astype(f32)
    mixed = dot(jnp.concatenate(joined, 1), output_rows)
    attend_normed, attend_inverse = normed_of(mixed)
    hidden_state = inputs + attend_normed * attend_full
    middle_normed, middle_inverse = normed_of(hidden_state)
    middle_low = (middle_normed * middle_full).astype(bf16)

    full = shaped(rows, model, dtype=f32)
    both_shape = shaped(2 * rows, 2 * hidden_part)

    def forward(first_rows, second_rows):
        return call(
            feed_forward, (both_shape, shaped(2 * rows, hidden_part), full, shaped(rows, model)),
            first_rows, second_rows, gate_up, down_part, name="feed_forward",
        )

    def backward(first_rows, second_rows, both):
        return call(
            feed_backward, (both_shape, full, shaped(rows, model)),
            first_rows, second_rows, both, gate_up, down_part, name="feed_backward",
        )

    def chip_sum(values, weights, product):
        second = product(values[rows:], weights).astype(bf16)
        return product(values[:rows], weights) + swap(second, 1).astype(f32)

    middle_far = swap(middle_low, 2)
    middle_near = swap(middle_low, 1)
    fed_near = forward(middle_low, middle_near)
    middle_far = after(middle_far, fed_near[0])
    channel_near = fed_near[2] + swap(fed_near[3], 1).astype(f32)
    channel_send = channel_near.astype(bf16)
    far_other = swap(channel_send, 2)
    middle_both = after(swap(middle_far, 1), channel_send)
    fed_far = forward(middle_far, middle_both)
    far_other = after(far_other, fed_far[0])
    channel_far = fed_far[2] + swap(fed_far[3], 1).astype(f32)
    near_other = swap(channel_far.astype(bf16), 2)

    def close(channel_out, cotangents):
        normed, inverse = normed_of(channel_out)
        back = norm_back(cotangents.astype(f32), normed, inverse, closing_full)
        return normed, back.astype(bf16)

    _, low_far = close(channel_far + far_other.astype(f32), cotangent_far)
    low_both = swap(low_far, 1)
    back_far = backward(low_far, low_both, fed_far[0])
    near_other = after(near_other, back_far[0])
    middle_send = (back_far[1] + swap(back_far[2], 1).astype(f32)).astype(bf16)
    far_got = swap(middle_send, 2)
    closing_normed, channel_low = close(
        channel_near + after(near_other, middle_send).astype(f32), cotangent
    )
    layer_output = (hidden_state + closing_normed * closing_full).astype(bf16)
    incoming = cotangent.astype(f32)
    closing_sum = jnp.sum(incoming * closing_normed, 0)
    low_near = swap(channel_low, 1)
    down_shape = shaped(hidden_part // 2, model)
    side = jnp.reshape(lax.axis_index("wt") % 2, (1,)).astype(jnp.int32)
    down_keep, down_send = call(
        functools.partial(down_weights, padded=padded), (down_shape, down_shape),
        side, channel_low, low_near, low_far, low_both, fed_near[1], fed_far[1], smem=1,
        scratch=(pltpu.VMEM((hidden_part, model), bf16),), name="down_weights",
    )
    down_got = across(down_send, wt)
    back_near = backward(channel_low, after(low_near, down_keep), fed_near[0])
    near_got = back_near[1] + swap(back_near[2], 1).astype(f32)
    gate_shape = shaped(model // 2, hidden_part)
    gate_keep, gate_send, up_keep, up_send = call(
        functools.partial(feed_weights, shard=shard),
        (gate_shape,) * 4, side, middle_low, middle_near, middle_far, middle_both,
        after(back_near[0], near_got), back_far[0], smem=1,
        scratch=(pltpu.VMEM((model, 2 * hidden_part), bf16),), name="feed_weights",
    )
    gate_got = across(gate_send, wt)
    up_got = across(up_send, wt)
    down_sum = add_low(down_keep, after(down_got, gate_keep))
    down_share = scatter_levels(down_sum, wt)
    middle_grad = near_got + after(far_got, gate_keep, down_sum).astype(f32)

    hidden_grad = incoming + norm_back(middle_grad, middle_normed, middle_inverse, middle_full)
    middle_sum = jnp.sum(middle_grad * middle_normed, 0)
    attend_sum = jnp.sum(hidden_grad * attend_normed, 0)
    mixed_low = norm_back(hidden_grad, attend_normed, attend_inverse, attend_full).astype(bf16)
    attended_grad = dot_nt(mixed_low, output_rows).astype(bf16)
    attended_back = exchange([attended_grad[:, at * part:(at + 1) * part] for at in range(SEQ)])
    output_grads = call(
        output_weights,
        (shaped(model, part, dtype=f32), shaped(model, part), shaped(model, part, dtype=f32),
         shaped(model, part)),
        here, after(mixed_low, attended_grad), *joined, smem=1,
        name="output_weights",
    )
    attended_back[1:] = [after(got, output_grads[0]) for got in attended_back[1:]]
    output_far = (output_grads[2] + swap(output_grads[3], 1).astype(f32)).astype(bf16)
    output_near = swap(output_grads[1], 1)
    output_far = after(output_far, *attended_back)
    gate_sum = add_low(gate_keep, after(gate_got, down_share, *attended_back[1:]))
    gate_share = scatter_levels(gate_sum, wt)
    attended_back[0] = after(attended_back[0], output_far, gate_sum)
    output_got = swap(output_far, 2)
    qkv_grad = call(
        attend_backward, shaped(window, 3 * part),
        query_low, key_low, value_low, log_totals, cosine, sine, query_code,
        *attended_back,
        scratch=(
            pltpu.VMEM((window, width), f32), pltpu.VMEM((window, width), f32),
            pltpu.VMEM((window, heads * width), bf16), pltpu.VMEM((window, 128), f32),
        ), name="attend_backward",
    )
    gain_rows = jnp.stack([attend_sum, middle_sum, closing_sum]).astype(bf16)
    gain_rows = gain_rows.reshape(3, wt, shard).transpose(1, 0, 2).reshape(wt, 1, 3 * shard)
    gain_rows = jnp.pad(gain_rows, ((0, 0), (0, GAIN_ROWS - 1), (0, model - 3 * shard)))
    mine = lax.axis_index("wt")
    if lines:
        whose = [mine ^ at for at in (0, 2, 4, 6, 1, 3, 5, 7)]
    else:
        levels = range(0, wt, 2)
        whose = [at + mine % 2 for at in levels] + [at + 1 - mine % 2 for at in levels]
    last = call(
        last_weights, shaped(wt, shard + GAIN_ROWS, model),
        jnp.stack([jnp.asarray(at, jnp.int32) for at in whose]),
        entry_low, qkv_grad, output_grads[0], output_near, after(output_got, qkv_grad), gain_rows,
        smem=1, scratch=(pltpu.VMEM((model, model), bf16),), name="last_weights",
    )
    up_sum = add_low(up_keep, after(up_got, last))
    up_share = scatter_levels(up_sum, wt)
    if lines:

        def send(value, bit):
            return lax.ppermute(value, "wt", [(at, at ^ bit) for at in range(wt)])

        far_x = across(last[6:8], wt)
        far = add_low(last[2:4], after(far_x, up_sum))
        near_x = across(after(last[4:6], far), wt)
        last_z = [send(far[1], 6), send(far[0], 4)]
        near = last[0:2].astype(f32) + near_x.astype(f32)
        near_send = near[1].astype(bf16)
        last_z.append(send(near_send, 2))
    else:
        last_rows = wt // 2 * (shard + GAIN_ROWS)
        last_halves = last.reshape(2, last_rows, model)
        last_share = scatter_levels(
            add_low(last_halves[0], across(last_halves[1], wt)), wt
        )
        near_send = last_share

    qkv_weight = first[:, :shard, :3 * part].reshape(model, 3 * part)
    entry_far = chip_sum(qkv_grad[2 * rows:], qkv_weight, dot_nt).astype(bf16)
    entry_grad = chip_sum(after(qkv_grad[:2 * rows], entry_far), qkv_weight, dot_nt)
    entry_grad = entry_grad + swap(entry_far, 2).astype(f32)
    entry_normed, entry_inverse = normed_of(inputs)
    input_grad = hidden_grad + norm_back(entry_grad, entry_normed, entry_inverse, entry_full)
    entry_sum = jnp.sum(entry_grad * entry_normed, 0).reshape(8, model // 8)
    for axis, size in (("seq", SEQ), ("wt", wt)):
        bit = 1
        while bit < size:
            entry_sum = entry_sum + lax.ppermute(
                entry_sum, axis, [(at, at ^ bit) for at in range(size)]
            )
            bit *= 2
    grad_entry = lax.dynamic_slice_in_dim(entry_sum.reshape(model), mine * shard, shard)

    share = call(
        join_shares, shaped((2 * hidden_part * shard + model * padded) // piece, piece),
        after(gate_share, near_send), up_share, down_share, name="join_shares",
    )
    if lines:
        last_z = [after(value, share) for value in last_z]
        last_share = (near[0] + sum(value.astype(f32) for value in last_z)).astype(bf16)
    share_got = gather_blocks(share)
    last_got = gather_blocks(last_share)
    grad_gate, grad_up, grad_down = call(
        functools.partial(unpack_feed, shard=shard, padded=padded),
        (shaped(shard, hidden, dtype=f32), shaped(shard, hidden, dtype=f32),
         shaped(SEQ * chunk, model, dtype=f32)),
        here, *share_got, smem=1, name="unpack_feed",
    )
    weight_shape = shaped(shard, model, dtype=f32)
    grad_query, grad_key, grad_value, grad_output, gain_sums = call(
        functools.partial(unpack_last, shard=shard),
        (weight_shape,) * 4 + (shaped(GAIN_ROWS, model, dtype=f32),),
        here, last_share, last_got[1], after(last_got[2], grad_down),
        last_got[3], smem=1, name="unpack_last",
    )
    grad_attend, grad_middle, grad_closing = [
        gain_sums[0, at * shard:(at + 1) * shard] for at in range(3)
    ]
    return (
        layer_output, input_grad, grad_entry, grad_query, grad_key, grad_value, grad_output,
        grad_attend, grad_middle, grad_gate, grad_up, grad_down, grad_closing,
    )


def solution(mesh):
    rows = P(("wt", "seq"), None)
    weight = P("wt", None)
    gain = P("wt")
    return jax.shard_map(
        on_device,
        mesh=mesh,
        in_specs=(
            rows, P(("wt", "seq")), gain, gain, gain, weight, weight, weight, weight, gain, gain,
            weight, weight, weight, gain, rows,
        ),
        out_specs=(
            rows, rows, gain, weight, weight, weight, weight, gain, gain, weight, weight, weight,
            gain,
        ),
        check_vma=False,
    )
```

time: 386 us -> 368 us (0.953)
  waiting for transfers between devices: 191 us -> 122 us
  Pallas kernels: 74.9 us -> 104 us
  matrix products: 26.6 us -> 9.3 us
  starting transfers between devices: 32.8 us -> 49.9 us
  other arithmetic: 20.2 us -> 36.6 us
  local copies, waits for them, and re-layouts: 18.2 us -> 23.6 us
    ppermute x0 -> x14, waiting for transfers between devices: none -> 69.9 us  [the longest x8 42.9 us: send(): return lax.ppermute(value, 'wt', pairs)]
    all_gather x1, waiting for transfers between devices: 49.2 us -> 0.11 us  [on_device(): first = lax.all_gather(first_own, 'wt', axis=0, tiled=False)]
    ppermute x36 -> x37, waiting for transfers between devices: 66.6 us -> 22.5 us  [swap(): return lax.ppermute(value, 'seq', [(i, i ^ bit) for i in range(SEQ)])]
    ppermute x5 -> x3, waiting for transfers between devices: 43.1 us -> 8.32 us  [send(): return lax.ppermute(value, 'wt', [(at, at ^ bit) for at in range(wt)])]
    pallas_call x11 -> x17, Pallas kernels: 74.9 us -> 104 us  [call(): pl.pallas_call(kernel, out_shape=tuple(outs) if many else outs, in_specs=...]
    all_gather x1, waiting for transfers between devices: 24.8 us -> 3.32 us  [on_device(): down_part = lax.all_gather(down_own, 'wt', axis=0, tiled=True)]
    ppermute x0 -> x14, starting transfers between devices: none -> 20.5 us  [the longest x8 12.3 us: send(): return lax.ppermute(value, 'wt', pairs)]
    reduce_scatter x1 -> x3, waiting for transfers between devices: 0.01 us -> 11.4 us  [scatter_levels(): lax.psum_scatter(value, 'wt', scatter_dimension=0, tiled=True, axis_index...]
  transfers between devices with their start and end apart: 49 -> 64, of which waited for: 25 -> 22; matrix products, arithmetic and copies ran while one was open for 12% -> 14% of each run, Pallas kernels for 14% -> 24%
where the time goes in v3:
time: 368 us; the launch traced here: 361 us
  waiting for transfers between devices  122 us (33%)
  Pallas kernels  104 us (28%)
  starting transfers between devices  49.9 us (14%)
  other arithmetic  36.6 us (10%)
  local copies, waits for them, and re-layouts  23.6 us (6%)
  between operations  15.9 us (4%)
  matrix products  9.3 us (3%)
    pallas_call x17, Pallas kernels, call(): pl.pallas_call(kernel, out_shape=tuple(outs) if many else outs, in_specs=...  104 us
    ppermute x8, waiting for transfers between devices, send(): return lax.ppermute(value, 'wt', pairs)  42.9 us
    ppermute x5, waiting for transfers between devices, across(): return lax.ppermute(value, 'wt', [(at, at ^ 1) for at in range(wt)])  27 us
    ppermute x37, waiting for transfers between devices, swap(): return lax.ppermute(value, 'seq', [(i, i ^ bit) for i in range(SEQ)])  22.5 us
    ppermute x37, starting transfers between devices, swap(): return lax.ppermute(value, 'seq', [(i, i ^ bit) for i in range(SEQ)])  20.9 us
    ppermute x8, starting transfers between devices, send(): return lax.ppermute(value, 'wt', pairs)  12.3 us
    reduce_scatter x3, waiting for transfers between devices, scatter_levels(): lax.psum_scatter(value, 'wt', scatter_dimension=0, tiled=True, axis_index...  11.4 us
    unnamed x132, local copies, waits for them, and re-layouts  10.3 us
  transfers between devices with their start and end apart: 64, of which 22 were waited for; matrix products, arithmetic and copies ran while one was open for 14% of the time, Pallas kernels for 24%

profile of v3, /device:TPU:0, one launch (start us, length us, event | category | flops | bytes accessed | tf_op | source)
XLA Modules:
  0.0 361.3 jit_solution(7618217992591814634)
XLA Ops:
  18.6 4.6 %collective-permute-start.4 = (bf16[128,1536]{1,0:T(8,128)(2,1)}, bf16[128,1536]{1,0:T(8,128)(2,1)S(1)}, u32[]{:S(2)}, u32[]{:S(2)}) collective-permute-start(bf16[128,1536]{1,0:T(8,128)(2,1)} %get-tuple-element.93.refs_0_), channel_id=1, source_target_pairs={{0,8},{4,12},{8,16},{12,20},{16,24},{20,28},{1,9},{5,13},{9,17},{1... | collective-permute-start | bytes 1179656 | tf_op jit(solution)/shard_map/ppermute | solution.py:437
  26.5 9.2 %collective-permute-done.7 = bf16[128,1536]{1,0:T(8,128)(2,1)S(1)} collective-permute-done((bf16[128,1536]{1,0:T(8,128)(2,1)}, bf16[128,1536]{1,0:T(8,128)(2,1)S(1)}, u32[]{:S(2)}, u32[]{:S(2)}) %collective-permute-start.7) | collective-permute-done | bytes 393248 | tf_op jit(solution)/shard_map/ppermute | solution.py:437
  40.4 11.3 %collective-permute-done.8 = bf16[128,1536]{1,0:T(8,128)(2,1)S(1)} collective-permute-done((bf16[128,1536]{1,0:T(8,128)(2,1)S(1)}, bf16[128,1536]{1,0:T(8,128)(2,1)S(1)}, u32[]{:S(2)}, u32[]{:S(2)}) %collective-permute-start.8) | collective-permute-done | bytes 393248 | tf_op jit(solution)/shard_map/ppermute | solution.py:437
  54.4 13.5 %collective-permute-done.9.refs_5_ = bf16[128,1536]{1,0:T(8,128)(2,1)S(1)} collective-permute-done((bf16[128,1536]{1,0:T(8,128)(2,1)S(1)}, bf16[128,1536]{1,0:T(8,128)(2,1)S(1)}, u32[]{:S(2)}, u32[]{:S(2)}) %collective-permute-start.9) | collective-permute-done | bytes 393248 | tf_op jit(solution)/shard_map/ppermute | solution.py:437
  77.3 6.1 %collective-permute-done.10 = bf16[128,1536]{1,0:T(8,128)(2,1)S(1)} collective-permute-done((bf16[128,1536]{1,0:T(8,128)(2,1)S(1)}, bf16[128,1536]{1,0:T(8,128)(2,1)S(1)}, u32[]{:S(2)}, u32[]{:S(2)}) %collective-permute-start.10) | collective-permute-done | bytes 393248 | tf_op jit(solution)/shard_map/ppermute | solution.py:437
  86.4 14.1 %attend_forward.1 = (bf16[1024,1024]{1,0:T(8,128)(2,1)}, bf16[1024,256]{1,0:T(8,128)(2,1)}, bf16[1024,256]{1,0:T(8,128)(2,1)}, bf16[1024,256]{1,0:T(8,128)(2,1)}...) custom-call(bf16[8,136,1024]{2,1,0:T(8,128)(2,1)} %bitcast.90, f32[1024,128]{1,0:T(8,128)} %pad_maximum_fusion.cos_ref, ...), custom_call_target="tpu_custom_call" | custom-call | flops 345000000 | tf_op jit(solution)/shard_map/attend_forward/pallas_call | solution.py:66
  104.6 3.7 %assemble.1.weight_ref = bf16[1024,1536]{1,0:T(8,128)(2,1)} custom-call(s32[8]{0:T(128)} %stack.90.at_ref, bf16[128,1536]{1,0:T(8,128)(2,1)} %get-tuple-element.93.refs_0_, bf16[128,1536]{1,0:T(8,128)(2,1)} %copy-done.26, bf16[128,1536]{1,0:T(8,128)(2,1)} %copy-done.25, bf16[128,1536]{1,0:T(8,128)(2,1)} %copy-done.24, bf16[128,1536]{1,0:T(8,128)(2,1)} %copy-done.38, ...), custom_call_target="tpu_custom_call" | custom-call | flops 92000000 | tf_op jit(solution)/shard_map/assemble/pallas_call | solution.py:66
  122.6 6.4 %feed_forward.2 = (bf16[512,1536]{1,0:T(8,128)(2,1)}, bf16[512,768]{1,0:T(8,128)(2,1)}, f32[256,1024]{1,0:T(8,128)}, bf16[256,1024]{1,0:T(8,128)(2,1)}) custom-call(bf16[256,1024]{1,0:T(8,128)(2,1)} %copy-done.11, bf16[256,1024]{1,0:T(8,128)(2,1)} %collective-permute-done.19.second_ref.near_ref, bf16[1024,1536]{1,0:T(8,128)(2,1)} %assemble.1.weight_ref, ...), custom_call_target="tpu_custom_call" | custom-call | flops 138000000 | tf_op jit(solution)/shard_map/feed_forward/pallas_call | solution.py:66
  135.7 6.4 %feed_forward.3 = (bf16[512,1536]{1,0:T(8,128)(2,1)}, bf16[512,768]{1,0:T(8,128)(2,1)}, f32[256,1024]{1,0:T(8,128)}, bf16[256,1024]{1,0:T(8,128)(2,1)}) custom-call(bf16[256,1024]{1,0:T(8,128)(2,1)} %collective-permute-done.21.first_ref.far_ref, bf16[256,1024]{1,0:T(8,128)(2,1)} %copy-done.21, bf16[1024,1536]{1,0:T(8,128)(2,1)} %assemble.1.weight_ref, ...), custom_call_target="tpu_custom_call" | custom-call | flops 138000000 | tf_op jit(solution)/shard_map/feed_forward/pallas_call | solution.py:66
  142.3 5.7 %collective-permute-done.25 = bf16[256,1024]{1,0:T(8,128)(2,1)S(1)} collective-permute-done((bf16[256,1024]{1,0:T(8,128)(2,1)S(1)}, bf16[256,1024]{1,0:T(8,128)(2,1)S(1)}, u32[]{:S(2)}, u32[]{:S(2)}) %collective-permute-start.25) | collective-permute-done | bytes 524320 | tf_op jit(solution)/shard_map/ppermute | solution.py:90
  153.2 7.1 %feed_backward.2 = (bf16[512,1536]{1,0:T(8,128)(2,1)}, f32[256,1024]{1,0:T(8,128)}, bf16[256,1024]{1,0:T(8,128)(2,1)}) custom-call(bf16[256,1024]{1,0:T(8,128)(2,1)} %copy-done.4, bf16[256,1024]{1,0:T(8,128)(2,1)} %copy-done.14, bf16[512,1536]{1,0:T(8,128)(2,1)} %get-tuple-element.113.both_ref, bf16[1024,1536]{1,0:T(8,128)(2,1)} %assemble.1.weight_ref, ...), custom_call_target="tpu_custom_call" | custom-call | flops 161000000 | tf_op jit(solution)/shard_map/feed_backward/pallas_call | solution.py:66
  160.5 4.4 %collective-permute-done.24 = bf16[256,1024]{1,0:T(8,128)(2,1)S(1)} collective-permute-done((bf16[256,1024]{1,0:T(8,128)(2,1)S(1)}, bf16[256,1024]{1,0:T(8,128)(2,1)S(1)}, u32[]{:S(2)}, u32[]{:S(2)}) %collective-permute-start.24) | collective-permute-done | bytes 524320 | tf_op jit(solution)/shard_map/ppermute | solution.py:90
  172.2 5.0 %down_weights.1 = (bf16[384,1024]{1,0:T(8,128)(2,1)}, bf16[384,1024]{1,0:T(8,128)(2,1)}) custom-call(s32[1]{0:T(128)} %bitcast.25.side_ref, bf16[256,1024]{1,0:T(8,128)(2,1)} %copy-done.5, bf16[256,1024]{1,0:T(8,128)(2,1)} %copy-done.15, bf16[256,1024]{1,0:T(8,128)(2,1)} %copy-done.4, bf16[256,1024]{1,0:T(8,128)(2,1)} %copy-done.14, ...), custom_call_target="tpu_custom_call" | custom-call | flops 92000000 | tf_op jit(solution)/shard_map/down_weights/pallas_call | solution.py:66
  177.3 7.4 %feed_backward.3 = (bf16[512,1536]{1,0:T(8,128)(2,1)}, f32[256,1024]{1,0:T(8,128)}, bf16[256,1024]{1,0:T(8,128)(2,1)}) custom-call(bf16[256,1024]{1,0:T(8,128)(2,1)} %copy-done.5, bf16[256,1024]{1,0:T(8,128)(2,1)} %copy-done.15, bf16[512,1536]{1,0:T(8,128)(2,1)} %get-tuple-element.108.both_ref, bf16[1024,1536]{1,0:T(8,128)(2,1)} %assemble.1.weight_ref, ...), custom_call_target="tpu_custom_call" | custom-call | flops 161000000 | tf_op jit(solution)/shard_map/feed_backward/pallas_call | solution.py:66
  188.7 8.1 %feed_weights.1 = (bf16[512,768]{1,0:T(8,128)(2,1)}, bf16[512,768]{1,0:T(8,128)(2,1)}, bf16[512,768]{1,0:T(8,128)(2,1)}, bf16[512,768]{1,0:T(8,128)(2,1)}) custom-call(s32[1]{0:T(128)} %bitcast.25.side_ref, bf16[256,1024]{1,0:T(8,128)(2,1)} %copy-done.11, bf16[256,1024]{1,0:T(8,128)(2,1)} %collective-permute-done.19.second_ref.near_ref, ...), custom_call_target="tpu_custom_call" | custom-call | flops 184000000 | tf_op jit(solution)/shard_map/feed_weights/pallas_call | solution.py:66
  198.2 6.9 %collective-permute-done.31 = bf16[384,1024]{1,0:T(8,128)(2,1)S(1)} collective-permute-done((bf16[384,1024]{1,0:T(8,128)(2,1)S(1)}, bf16[384,1024]{1,0:T(8,128)(2,1)S(1)}, u32[]{:S(2)}, u32[]{:S(2)}) %collective-permute-start.31) | collective-permute-done | bytes 786464 | tf_op jit(solution)/shard_map/ppermute | solution.py:471
  222.3 3.4 collective-permute-done.34.refs_2_
  225.7 11.3 %reduce-scatter.4.cloned.1.call-done.down_ref = bf16[96,1024]{1,0:T(8,128)(2,1)} async-done(((bf16[384,1024]{1,0:T(8,128)(2,1)}), bf16[96,1024]{1,0:T(8,128)(2,1)}) %reduce-scatter.4.cloned.1.call-update) | async-done | bytes 196624 | tf_op jit(solution)/shard_map/reduce_scatter | solution.py:475
  247.4 14.2 %attend_backward.1.grad_ref = bf16[1024,768]{1,0:T(8,128)(2,1)} custom-call(bf16[1024,256]{1,0:T(8,128)(2,1)} %get-tuple-element.132.query_ref, bf16[1024,256]{1,0:T(8,128)(2,1)} %get-tuple-element.133.key_ref, bf16[1024,256]{1,0:T(8,128)(2,1)} %get-tuple-element.134.value_ref, f32[2,4,8,256]{3,2,1,0:T(8,128)} %get-tuple-element.135.log_ref, ...), custom_call_target="tpu_custom_call" | custom-call | flops 322000000 | tf_op jit(solution)/shard_map/attend_backward/pallas_call | solution.py:66
  262.8 6.3 %last_weights.1 = bf16[8,136,1024]{2,1,0:T(8,128)(2,1)} custom-call(s32[8]{0:T(128)} %stack.99.at_ref, bf16[1024,1024]{1,0:T(8,128)(2,1)} %get-tuple-element.148.low_ref, bf16[1024,768]{1,0:T(8,128)(2,1)} %attend_backward.1.grad_ref, f32[1024,256]{1,0:T(8,128)} %get-tuple-element.139.keep_ref, bf16[1024,256]{1,0:T(8,128)(2,1)} %collective-permute-done.45.near_ref, ...), custom_call_target="tpu_custom_call" | custom-call | flops 138000000 | tf_op jit(solution)/shard_map/last_weights/pallas_call | solution.py:66
  274.6 12.0 %collective-permute-done.47 = bf16[2,136,1024]{2,1,0:T(8,128)(2,1)} collective-permute-done((bf16[2,136,1024]{2,1,0:T(8,128)(2,1)}, bf16[2,136,1024]{2,1,0:T(8,128)(2,1)}, u32[]{:S(2)}, u32[]{:S(2)}) %collective-permute-start.47) | collective-permute-done | bytes 557088 | tf_op jit(solution)/shard_map/ppermute | solution.py:471
  294.3 8.1 %collective-permute-done.49 = bf16[2,136,1024]{2,1,0:T(8,128)(2,1)S(1)} collective-permute-done((bf16[2,136,1024]{2,1,0:T(8,128)(2,1)}, bf16[2,136,1024]{2,1,0:T(8,128)(2,1)S(1)}, u32[]{:S(2)}, u32[]{:S(2)}) %collective-permute-start.49) | collective-permute-done | bytes 557088 | tf_op jit(solution)/shard_map/ppermute | solution.py:471
  310.9 8.3 %collective-permute-done.51 = bf16[136,1024]{1,0:T(8,128)(2,1)} collective-permute-done((bf16[136,1024]{1,0:T(8,128)(2,1)}, bf16[136,1024]{1,0:T(8,128)(2,1)}, u32[]{:S(2)}, u32[]{:S(2)}) %collective-permute-start.51) | collective-permute-done | bytes 278560 | tf_op jit(solution)/shard_map/ppermute | solution.py:726
  340.3 8.7 %unpack_feed.1 = (f32[128,2816]{1,0:T(8,128)}, f32[128,2816]{1,0:T(8,128)}, f32[352,1024]{1,0:T(8,128)}) custom-call(s32[1]{0:T(128)} %bitcast.place_ref, bf16[1152,256]{1,0:T(8,128)(2,1)} %join_shares.1.refs_0_, bf16[1152,256]{1,0:T(8,128)(2,1)} %copy-done.31, bf16[1152,256]{1,0:T(8,128)(2,1)} %collective-permute-done.56.refs_2_, bf16[1152,256]{1,0:T(8,128)(2,1)} %copy-done.32), custom_call_target="tpu_custom_call" | custom-call | flops 207000000 | tf_op jit(solution)/shard_map/unpack_feed/pallas_call | solution.py:66
  (336 shorter events, 153.0 us)
Async XLA Ops:
  7.2 66.1 %all-gather.6.cloned.1.call-start = ((), (), s32[]{:S(2)}) async-start(), calls=%async_computation.7 | async-start | bytes 2506752 | tf_op jit(solution)/shard_map/all_gather | solution.py:518
  9.3 113.3 %all-gather.4.cloned.1.call-start = ((), (), s32[]{:S(2)}) async-start(), calls=%async_computation.3 | async-start | bytes 1769472 | tf_op jit(solution)/shard_map/all_gather | solution.py:523
  9.3 44.2 %collective-permute-start.1 = (bf16[256,1024]{1,0:T(8,128)(2,1)S(1)}, bf16[256,1024]{1,0:T(8,128)(2,1)}, u32[]{:S(2)}, u32[]{:S(2)}) collective-permute-start(bf16[256,1024]{1,0:T(8,128)(2,1)S(1)} %copy-done.8), channel_id=1, source_target_pairs={{0,2},{1,3},{2,0},{3,1},{4,6},{5,7},{6,4},{7,5},{8,10},{9,11},{10,... | collective-permute-start | bytes 1572872 | tf_op jit(solution)/shard_map/ppermute | solution.py:90
  12.4 60.8 %collective-permute-start = (bf16[256,1024]{1,0:T(8,128)(2,1)S(1)}, bf16[256,1024]{1,0:T(8,128)(2,1)}, u32[]{:S(2)}, u32[]{:S(2)}) collective-permute-start(bf16[256,1024]{1,0:T(8,128)(2,1)S(1)} %copy-done.8), channel_id=1, source_target_pairs={{0,1},{1,0},{2,3},{3,2},{4,5},{5,4},{6,7},{7,6},{8,9},{9,8},{10,11... | collective-permute-start | bytes 1572872 | tf_op jit(solution)/shard_map/ppermute | solution.py:90
  15.8 19.9 %collective-permute-start.7 = (bf16[128,1536]{1,0:T(8,128)(2,1)}, bf16[128,1536]{1,0:T(8,128)(2,1)S(1)}, u32[]{:S(2)}, u32[]{:S(2)}) collective-permute-start(bf16[128,1536]{1,0:T(8,128)(2,1)} %get-tuple-element.93.refs_0_), channel_id=1, source_target_pairs={{8,0},{12,4},{16,8},{20,12},{24,16},{28,20},{9,1},{13,5},{17,9},{2... | collective-permute-start | bytes 1179656 | tf_op jit(solution)/shard_map/ppermute | solution.py:437
  17.1 18.7 %collective-permute-start.5 = (bf16[128,1536]{1,0:T(8,128)(2,1)}, bf16[128,1536]{1,0:T(8,128)(2,1)S(1)}, u32[]{:S(2)}, u32[]{:S(2)}) collective-permute-start(bf16[128,1536]{1,0:T(8,128)(2,1)} %get-tuple-element.93.refs_0_), channel_id=1, source_target_pairs={{0,4},{4,0},{8,12},{12,8},{16,20},{20,16},{24,28},{28,24},{1,5},{5... | collective-permute-start | bytes 1179656 | tf_op jit(solution)/shard_map/ppermute | solution.py:437
  18.6 21.0 %collective-permute-start.4 = (bf16[128,1536]{1,0:T(8,128)(2,1)}, bf16[128,1536]{1,0:T(8,128)(2,1)S(1)}, u32[]{:S(2)}, u32[]{:S(2)}) collective-permute-start(bf16[128,1536]{1,0:T(8,128)(2,1)} %get-tuple-element.93.refs_0_), channel_id=1, source_target_pairs={{0,8},{4,12},{8,16},{12,20},{16,24},{20,28},{1,9},{5,13},{9,17},{1... | collective-permute-start | bytes 1179656 | tf_op jit(solution)/shard_map/ppermute | solution.py:437
  23.2 213.8 %reduce-scatter.4.cloned.1.call-start = ((), (), s32[]{:S(2)}) async-start(), calls=%async_computation.4 | async-start | bytes 983040 | tf_op jit(solution)/shard_map/reduce_scatter | solution.py:475
  53.5 19.6 %collective-permute-start.3 = (bf16[256,1024]{1,0:T(8,128)(2,1)S(1)}, bf16[256,1024]{1,0:T(8,128)(2,1)S(1)}, u32[]{:S(2)}, u32[]{:S(2)}) collective-permute-start(bf16[256,1024]{1,0:T(8,128)(2,1)S(1)} %copy-done.6), channel_id=1, source_target_pairs={{0,2},{1,3},{2,0},{3,1},{4,6},{5,7},{6,4},{7,5},{8,10},{9,11},{10,... | collective-permute-start | bytes 1572872 | tf_op jit(solution)/shard_map/ppermute | solution.py:90
  53.6 19.5 %collective-permute-start.2 = (bf16[256,1024]{1,0:T(8,128)(2,1)}, bf16[256,1024]{1,0:T(8,128)(2,1)}, u32[]{:S(2)}, u32[]{:S(2)}) collective-permute-start(bf16[256,1024]{1,0:T(8,128)(2,1)} %collective-permute-done.1.far_ref), channel_id=1, source_target_pairs={{0,1},{1,0},{2,3},{3,2},{4,5},{5,4},{6,7},{7,6},{8,9},{9,8},{10,11... | collective-permute-start | bytes 1572872 | tf_op jit(solution)/shard_map/ppermute | solution.py:90
  74.5 26.0 %collective-permute-start.16 = (bf16[1024,256]{1,0:T(8,128)(2,1)S(1)}, bf16[1024,256]{1,0:T(8,128)(2,1)}, u32[]{:S(2)}, u32[]{:S(2)}) collective-permute-start(bf16[1024,256]{1,0:T(8,128)(2,1)S(1)} %bitcast.93), channel_id=1, source_target_pairs={{0,2},{1,3},{2,0},{3,1},{4,6},{5,7},{6,4},{7,5},{8,10},{9,11},{10,... | collective-permute-start | bytes 1572872 | tf_op jit(solution)/shard_map/ppermute | solution.py:90
  86.4 22.9 %collective-permute-start.15 = (bf16[1024,256]{1,0:T(8,128)(2,1)S(1)}, bf16[1024,256]{1,0:T(8,128)(2,1)S(1)}, u32[]{:S(2)}, u32[]{:S(2)}) collective-permute-start(bf16[1024,256]{1,0:T(8,128)(2,1)S(1)} %bitcast.94), channel_id=1, source_target_pairs={{0,1},{1,0},{2,3},{3,2},{4,5},{5,4},{6,7},{7,6},{8,9},{9,8},{10,11... | collective-permute-start | bytes 1572872 | tf_op jit(solution)/shard_map/ppermute | solution.py:90
  184.8 20.3 %collective-permute-start.31 = (bf16[384,1024]{1,0:T(8,128)(2,1)S(1)}, bf16[384,1024]{1,0:T(8,128)(2,1)S(1)}, u32[]{:S(2)}, u32[]{:S(2)}) collective-permute-start(bf16[384,1024]{1,0:T(8,128)(2,1)S(1)} %copy-done.63), channel_id=1, source_target_pairs={{0,4},{4,0},{8,12},{12,8},{16,20},{20,16},{24,28},{28,24},{1,5},{5... | collective-permute-start | bytes 2359304 | tf_op jit(solution)/shard_map/ppermute | solution.py:471
  186.8 19.7 %collective-permute-start.30 = (bf16[256,1024]{1,0:T(8,128)(2,1)}, bf16[256,1024]{1,0:T(8,128)(2,1)}, u32[]{:S(2)}, u32[]{:S(2)}) collective-permute-start(bf16[256,1024]{1,0:T(8,128)(2,1)} %add_convert_fusion.6), channel_id=1, source_target_pairs={{0,2},{1,3},{2,0},{3,1},{4,6},{5,7},{6,4},{7,5},{8,10},{9,11},{10,... | collective-permute-start | bytes 1572872 | tf_op jit(solution)/shard_map/ppermute | solution.py:90
  196.8 29.0 %collective-permute-start.36 = (bf16[512,768]{1,0:T(8,128)(2,1)}, bf16[512,768]{1,0:T(8,128)(2,1)}, u32[]{:S(2)}, u32[]{:S(2)}) collective-permute-start(bf16[512,768]{1,0:T(8,128)(2,1)} %get-tuple-element.144), channel_id=1, source_target_pairs={{0,4},{4,0},{8,12},{12,8},{16,20},{20,16},{24,28},{28,24},{1,5},{5... | collective-permute-start | bytes 2359304 | tf_op jit(solution)/shard_map/ppermute | solution.py:471
  206.4 100.4 %reduce-scatter.6.cloned.1.call-start = ((), (), s32[]{:S(2)}) async-start(), calls=%async_computation.5 | async-start | bytes 983040 | tf_op jit(solution)/shard_map/reduce_scatter | solution.py:475
  216.4 23.0 %collective-permute-start.32 = (bf16[1024,256]{1,0:T(8,128)(2,1)}, bf16[1024,256]{1,0:T(8,128)(2,1)}, u32[]{:S(2)}, u32[]{:S(2)}) collective-permute-start(bf16[1024,256]{1,0:T(8,128)(2,1)} %get-tuple-element.138), channel_id=1, source_target_pairs={{0,1},{1,0},{2,3},{3,2},{4,5},{5,4},{6,7},{7,6},{8,9},{9,8},{10,11... | collective-permute-start | bytes 1572872 | tf_op jit(solution)/shard_map/ppermute | solution.py:90
  239.3 67.5 %reduce-scatter.8.cloned.1.call-start = ((), (), s32[]{:S(2)}) async-start(), calls=%async_computation.6 | async-start | bytes 983040 | tf_op jit(solution)/shard_map/reduce_scatter | solution.py:475
  241.8 21.0 %collective-permute-start.46 = (bf16[1024,256]{1,0:T(8,128)(2,1)}, bf16[1024,256]{1,0:T(8,128)(2,1)}, u32[]{:S(2)}, u32[]{:S(2)}) collective-permute-start(bf16[1024,256]{1,0:T(8,128)(2,1)} %add_convert_fusion.4), channel_id=1, source_target_pairs={{0,2},{1,3},{2,0},{3,1},{4,6},{5,7},{6,4},{7,5},{8,10},{9,11},{10,... | collective-permute-start | bytes 1572872 | tf_op jit(solution)/shard_map/ppermute | solution.py:90
  243.3 19.6 %collective-permute-start.45 = (bf16[1024,256]{1,0:T(8,128)(2,1)}, bf16[1024,256]{1,0:T(8,128)(2,1)}, u32[]{:S(2)}, u32[]{:S(2)}) collective-permute-start(bf16[1024,256]{1,0:T(8,128)(2,1)} %get-tuple-element.149), channel_id=1, source_target_pairs={{0,1},{1,0},{2,3},{3,2},{4,5},{5,4},{6,7},{7,6},{8,9},{9,8},{10,11... | collective-permute-start | bytes 1572872 | tf_op jit(solution)/shard_map/ppermute | solution.py:90
  245.3 28.2 %collective-permute-start.48 = (bf16[512,768]{1,0:T(8,128)(2,1)S(1)}, bf16[512,768]{1,0:T(8,128)(2,1)S(1)}, u32[]{:S(2)}, u32[]{:S(2)}) collective-permute-start(bf16[512,768]{1,0:T(8,128)(2,1)S(1)} %copy-done.62), channel_id=1, source_target_pairs={{0,4},{4,0},{8,12},{12,8},{16,20},{20,16},{24,28},{28,24},{1,5},{5... | collective-permute-start | bytes 2359304 | tf_op jit(solution)/shard_map/ppermute | solution.py:471
  292.4 26.8 %collective-permute-start.50 = (bf16[136,1024]{1,0:T(8,128)(2,1)}, bf16[136,1024]{1,0:T(8,128)(2,1)}, u32[]{:S(2)}, u32[]{:S(2)}) collective-permute-start(bf16[136,1024]{1,0:T(8,128)(2,1)} %get-tuple-element.192), channel_id=1, source_target_pairs={{0,24},{4,28},{8,16},{12,20},{16,8},{20,12},{24,0},{28,4},{1,25},{... | collective-permute-start | bytes 835592 | tf_op jit(solution)/shard_map/ppermute | solution.py:726
  294.3 24.9 %collective-permute-start.51 = (bf16[136,1024]{1,0:T(8,128)(2,1)}, bf16[136,1024]{1,0:T(8,128)(2,1)}, u32[]{:S(2)}, u32[]{:S(2)}) collective-permute-start(bf16[136,1024]{1,0:T(8,128)(2,1)} %get-tuple-element.193), channel_id=1, source_target_pairs={{0,16},{4,20},{8,24},{12,28},{16,0},{20,4},{24,8},{28,12},{1,17},{... | collective-permute-start | bytes 835592 | tf_op jit(solution)/shard_map/ppermute | solution.py:726
  308.8 22.2 %collective-permute-start.56 = (bf16[1152,256]{1,0:T(8,128)(2,1)}, bf16[1152,256]{1,0:T(8,128)(2,1)}, u32[]{:S(2)}, u32[]{:S(2)}) collective-permute-start(bf16[1152,256]{1,0:T(8,128)(2,1)} %join_shares.1.refs_0_), channel_id=1, source_target_pairs={{0,2},{1,3},{2,0},{3,1},{4,6},{5,7},{6,4},{7,5},{8,10},{9,11},{10,... | collective-permute-start | bytes 1769480 | tf_op jit(solution)/shard_map/ppermute | solution.py:90
  (104 other events, 1195.2 us)
Sparse Core Ops, SparseCore 0:
  10.8 62.4 all-gather.5
  75.5 47.0 all-gather.3
  206.5 30.5 reduce-scatter.3
  239.8 22.5 reduce-scatter.5
  274.7 21.9 reduce-scatter.7

commit v4 on v3

--- a/solution.py
+++ b/solution.py
@@ -17,21 +17,26 @@
 SEQ = 4
 GAIN_ROWS = 8
 COSTS = dict(
-    pack_first=0.04,
-    pack_feed=0.08,
-    assemble=0.08,
-    attend_forward=0.3,
-    arrange=0.06,
-    feed_weights=0.16,
-    down_weights=0.08,
-    feed_forward=0.12,
-    feed_backward=0.14,
-    output_weights=0.06,
-    attend_backward=0.28,
-    last_weights=0.12,
-    join_shares=0.04,
-    unpack_feed=0.18,
-    unpack_last=0.06,
+    pack_first=0.004,
+    pack_feed=0.008,
+    assemble=0.008,
+    attend_forward=0.03,
+    arrange=0.006,
+    feed_weights=0.016,
+    down_weights=0.008,
+    feed_forward=0.012,
+    feed_backward=0.014,
+    output_weights=0.006,
+    attend_backward=0.028,
+    last_weights=0.012,
+    join_shares=0.004,
+    middle_backward=0.008,
+    add_rows=0.002,
+    others=0.002,
+    output_and_gains=0.002,
+    assemble_part=0.002,
+    unpack_feed=0.018000000000000002,
+    unpack_last=0.006,
 )
 
 f32 = jnp.float32
@@ -128,11 +133,41 @@
     down_out_ref[...] = dot_tn(pick_rows, down_ref[...]).astype(bf16)
 
 
+def blocks_of(at_ref, refs):
+    step = 0
+    for ref in refs:
+        for at in range(ref.shape[0]):
+            yield at_ref[step], ref.at[at]
+            step += 1
+
+
 def assemble(at_ref, *refs):
-    blocks, out_ref = refs[:-1], refs[-1]
-    rows = blocks[0].shape[0]
-    for step, block in enumerate(blocks):
-        out_ref[pl.ds(pl.multiple_of(at_ref[step] * rows, rows), rows), :] = block[...]
+    out_ref = refs[-1]
+    rows = refs[0].shape[1]
+    for at, block in blocks_of(at_ref, refs[:-1]):
+        out_ref[pl.ds(pl.multiple_of(at * rows, rows), rows), :] = block[...]
+
+
+def others(at_ref, ref, out_ref):
+    for step in range(out_ref.shape[0]):
+        out_ref[step] = ref[at_ref[step]]
+
+
+def output_and_gains(at_ref, *refs):
+    refs, (output_ref, gain_ref) = refs[:-2], refs[-2:]
+    shard = refs[0].shape[1] - GAIN_ROWS
+    part = output_ref.shape[1]
+    for step, (at, block) in enumerate(blocks_of(at_ref, refs)):
+        rows = pl.ds(pl.multiple_of(at * shard, shard), shard)
+        output_ref[rows, :] = block[:shard, 3 * part:]
+        if shard % 128:
+            columns = pl.ds(step * shard, shard)
+        else:
+            columns = pl.ds(pl.multiple_of(at * shard, shard), shard)
+        for number in range(4):
+            gain_ref[number:number + 1, columns] = block[
+                shard:shard + 1, number * shard:(number + 1) * shard
+            ].astype(f32)
 
 
 def join_shares(gate_ref, up_ref, down_ref, out_ref):
@@ -179,7 +214,7 @@
 
 
 def unpack_last(place_ref, *refs, shard):
-    blocks, outs = refs[:SEQ], refs[SEQ:]
+    blocks, (gain_ref, *weights), outs = refs[:SEQ], refs[SEQ:SEQ + 4], refs[SEQ + 4:]
     place = place_ref[0]
     part = blocks[0].shape[1] // SEQ
     for step, block in enumerate(blocks):
@@ -187,6 +222,11 @@
         for at in range(4):
             outs[at][:, columns] = block[:shard, at * part:(at + 1) * part].astype(f32)
     outs[4][...] = sum(block[shard:, :].astype(f32) for block in blocks)
+    total = sum(
+        jnp.sum(ref[...].astype(f32) * out[...], 1, keepdims=True)
+        for ref, out in zip(weights, outs[:3])
+    )
+    outs[5][...] = total.T / gain_ref[...].astype(f32)
 
 
 def arrange(place_ref, *refs):
@@ -217,21 +257,20 @@
 
 
 def attend_forward(
-    weight_ref, cos_ref, sin_ref, query_code_ref, own_ref, near_ref, far_ref, both_ref,
-    low_ref, query_ref, key_ref, value_ref, out_ref, log_ref, gain_ref, token_ref, key_code_ref,
+    at_ref, gain_ref, cos_ref, sin_ref, query_code_ref, own_ref, near_ref, far_ref, both_ref,
+    *refs,
 ):
+    firsts, refs = refs[:-9], refs[-9:]
+    low_ref, query_ref, key_ref, value_ref, out_ref, log_ref, weight_ref, token_ref, key_code_ref = refs
     window, model = low_ref.shape
-    wt, shard, _ = weight_ref.shape
-    shard = shard - GAIN_ROWS
+    shard = firsts[0].shape[1] - GAIN_ROWS
     tiles, _, tile = query_code_ref.shape
     width = cos_ref.shape[1]
     heads = query_ref.shape[1] // width
     scale = LOG2_E * width ** (-0.5)
-    for at in range(wt):
-        gain_ref[0:1, at * shard:(at + 1) * shard] = weight_ref[
-            at, shard:shard + 1, :shard
-        ].astype(f32)
-
+    for at, block in blocks_of(at_ref, firsts):
+        rows = pl.ds(pl.multiple_of(at * shard, shard), shard)
+        weight_ref[rows, :] = block[:shard, :3 * heads * width]
     for step, ref in enumerate((own_ref, near_ref, far_ref, both_ref)):
         token_ref[step * tile:(step + 1) * tile, :] = ref[...]
     key_codes(query_code_ref, key_code_ref)
@@ -241,8 +280,7 @@
         normed, _ = normed_of(token_ref[rows, :].astype(f32))
         low = (normed * gain_ref[0:1, :]).astype(bf16)
         low_ref[rows, :] = low
-        weight = weight_ref[:, :shard, :3 * heads * width].reshape(model, 3 * heads * width)
-        raw = dot(low, weight)
+        raw = dot(low, weight_ref[...])
         cosine = cos_ref[rows, :]
         sine = sin_ref[rows, :]
         for head in range(heads):
@@ -395,6 +433,43 @@
     halves_out(side_ref[0], full, padded, slice(None), keep_ref, send_ref)
 
 
+def folded(values):
+    return jnp.sum(values.reshape(-1, 8, values.shape[-1]), 0)
+
+
+def middle_backward(
+    keep_ref, near_ref, far_ref, hidden_ref, mixed_ref, incoming_ref, gain_ref, weight_ref,
+    grad_ref, low_ref, sum_ref, *outs,
+):
+    rows = keep_ref.shape[0]
+    step = 64
+    middle_scale = gain_ref[2:3, :]
+    attend_scale = gain_ref[1:2, :]
+
+    def some(at, sums):
+        part = pl.ds(pl.multiple_of(at * step, step), step)
+        middle_grad = (
+            keep_ref[part, :] + near_ref[part, :].astype(f32) + far_ref[part, :].astype(f32)
+        )
+        normed, inverse = normed_of(hidden_ref[part, :])
+        grad = incoming_ref[part, :].astype(f32) + norm_back(
+            middle_grad, normed, inverse, middle_scale
+        )
+        grad_ref[part, :] = grad
+        middle_sum = sums[1] + folded(middle_grad * normed)
+        normed, inverse = normed_of(mixed_ref[part, :])
+        low_ref[part, :] = norm_back(grad, normed, inverse, attend_scale).astype(bf16)
+        return sums[0] + folded(grad * normed), middle_sum
+
+    empty = jnp.zeros((8, keep_ref.shape[1]), f32)
+    sums = lax.fori_loop(0, rows // step, some, (empty, empty))
+    sum_ref[0:8, :] = sums[0]
+    sum_ref[8:16, :] = sums[1]
+    size = outs[0].shape[1]
+    for at, ref in enumerate(outs):
+        ref[...] = dot_nt(low_ref[...], weight_ref[at * size:(at + 1) * size, :]).astype(bf16)
+
+
 def output_weights(place_ref, low_ref, *refs):
     pieces, outs = refs[:SEQ], refs[SEQ:]
     place = place_ref[0]
@@ -409,62 +484,29 @@
 
 
 def last_weights(at_ref, low_ref, grad_ref, keep_ref, near_ref, far_ref, sum_ref, *refs):
-    out_ref, full = refs
-    wt, total, model = out_ref.shape
+    outs, full = refs[:2], refs[2]
+    wt = at_ref.shape[0]
+    model = outs[0].shape[1]
+    total = outs[0].shape[0] // (wt // 2)
     shard = total - GAIN_ROWS
     part = keep_ref.shape[1]
     full[:, :3 * part] = dot_tn(low_ref[...], grad_ref[...]).astype(bf16)
     full[:, 3 * part:] = (
         keep_ref[...] + near_ref[...].astype(f32) + far_ref[...].astype(f32)
     ).astype(bf16)
-    for step in range(wt):
-        at = at_ref[step]
-        out_ref[step, :shard, :] = full[pl.ds(pl.multiple_of(at * shard, shard), shard), :]
-        out_ref[step, shard:, :] = sum_ref[at]
-
-
-def pick_level(level, table):
-    return jnp.where(
-        level == 0, table[0],
-        jnp.where(level == 1, table[1], jnp.where(level == 2, table[2], table[3])),
-    )
-
-
-def gather_start(own):
-    level = lax.axis_index("wt") // 2
-
-    def send(value, pairs):
-        return lax.ppermute(value, "wt", pairs)
-
-    def across(value):
-        return send(value, [(at, at ^ 1) for at in range(8)])
-
-    right = send(own, [(at, at + 2) for at in range(6)])
-    left = send(own, [(at, at - 2) for at in range(2, 8)])
-    own_x = across(own)
-    right2 = send(after(right, own_x), [(at, at + 2) for at in range(2, 6)])
-    left2 = send(after(left, own_x), [(at, at - 2) for at in range(2, 6)])
-    one = jnp.where(level == 0, left, right)
-    one_x = across(one)
-    onward = after(jnp.where(level == 2, right2, left2), one_x)
-    two = jnp.where(level == 0, left2, jnp.where(level == 3, right2, left))
-    two_x = across(two)
-    third = send(onward, [(4, 6), (5, 7), (2, 0), (3, 1)])
-    return (own, one, two, own_x, one_x, two_x), onward, third
-
-
-def gather_end(started, onward, third):
-    here = lax.axis_index("wt")
-    level = here // 2
-    side = here % 2
-    three = jnp.where((level == 1) | (level == 2), onward, third)
-    three_x = lax.ppermute(three, "wt", [(at, at ^ 1) for at in range(8)])
-    levels = [level] + [
-        pick_level(level, table) for table in ((1, 0, 1, 2), (2, 2, 3, 1), (3, 3, 0, 0))
-    ]
-    whose = [2 * at + side for at in levels] + [2 * at + 1 - side for at in levels]
-    blocks = (*started[:3], three, *started[3:], three_x)
-    return blocks, jnp.stack(whose).astype(jnp.int32)
+    for number, ref in enumerate(outs):
+        for step in range(wt // 2):
+            at = at_ref[number * (wt // 2) + step]
+            row = step * total
+            ref[row:row + shard, :] = full[pl.ds(pl.multiple_of(at * shard, shard), shard), :]
+            ref[row + shard:row + total, :] = sum_ref[at]
+
+
+def gather_levels(own, wt):
+    return lax.all_gather(
+        own, "wt", axis=0, tiled=False,
+        axis_index_groups=[list(range(side, wt, 2)) for side in range(2)],
+    )
 
 
 def across(value, wt):
@@ -478,8 +520,21 @@
     )
 
 
+def add_rows(left_ref, right_ref, out_ref):
+    step = 32
+
+    def some(at, carry):
+        rows = pl.ds(pl.multiple_of(at * step, step), step)
+        out_ref[rows, :] = (
+            left_ref[rows, :].astype(f32) + right_ref[rows, :].astype(f32)
+        ).astype(bf16)
+        return carry
+
+    lax.fori_loop(0, out_ref.shape[0] // step, some, 0, unroll=2)
+
+
 def add_low(left, right):
-    return (left.astype(f32) + right.astype(f32)).astype(bf16)
+    return call(add_rows, shaped(*left.shape), left, right, name="add_rows")
 
 
 def on_device(
@@ -515,14 +570,37 @@
         *(gain[None] for gain in (entry_gain, attend_gain, middle_gain, closing_gain)),
         smem=1, name="pack_first",
     )
-    first = lax.all_gather(first_own, "wt", axis=0, tiled=False)
     gate_up_own, down_own = call(
         pack_feed, (shaped(shard, 2 * hidden_part), shaped(padded, model)),
         here, gate_weight, up_weight, after(down_weight, first_own), smem=1, name="pack_feed",
     )
-    down_part = lax.all_gather(down_own, "wt", axis=0, tiled=True)
+    mine = lax.axis_index("wt")
+    level = mine // 2
+    xside = mine % 2
+
+    def numbers(*values):
+        return jnp.stack([jnp.asarray(value, jnp.int32) for value in values])
+
     if lines:
-        gate_up_blocks, onward, third = gather_start(gate_up_own)
+        around = numbers(level ^ 1, level ^ 2, level ^ 3)
+        whose = numbers(
+            *[2 * at + xside for at in range(4)],
+            *[2 * (level ^ at) + 1 - xside for at in range(4)],
+        )
+        first_z = gather_levels(first_own, wt)
+        gate_up_z = gather_levels(gate_up_own, wt)
+        first_x = across(first_own, wt)
+        gate_up_x = across(gate_up_own, wt)
+        down_x = across(down_own, wt)
+        down_pair = jnp.where(
+            xside == 0, jnp.stack([down_own, down_x]), jnp.stack([down_x, down_own])
+        )
+        down_part = gather_levels(down_pair, wt).reshape(hidden_part, model)
+    else:
+        whose = jnp.arange(wt, dtype=jnp.int32)
+        first_z = lax.all_gather(first_own, "wt", axis=0, tiled=False)
+        gate_up_z = lax.all_gather(gate_up_own, "wt", axis=0, tiled=False)
+        down_part = lax.all_gather(down_own, "wt", axis=0, tiled=True)
     token_blocks = gather_blocks(tokens)
     cotangent_far = swap(after(cotangent, token_blocks[2]), 2)
 
@@ -549,29 +627,41 @@
 
     waited = (cosine, sine, query_code, *token_blocks, cotangent_far)
     if lines:
-        waited += (onward,)
-    first = after(first, *waited)
-    output_own = first[:, :shard, 3 * part:].reshape(model, part)
-    gains = first[:, shard, :4 * shard].reshape(wt, 4, shard).transpose(1, 0, 2).reshape(4, model)
-    gains = gains.astype(f32)
-    first = after(first, output_own)
-    if lines:
-        gate_up_blocks, sources = gather_end(gate_up_blocks, onward, third)
-        first = after(first, gate_up_blocks[3])
+        first_z = after(first_z, *waited, first_x, gate_up_x, down_pair)
+        rest = call(
+            others, shaped(3, shard + GAIN_ROWS, model), around, first_z, smem=1, name="others",
+        )
+        firsts = (first_z, first_x[None], across(rest, wt))
+    else:
+        firsts = (after(first_z, *waited),)
+    output_own, gains = call(
+        output_and_gains, (shaped(model, part), shaped(8, model, dtype=f32)),
+        whose, *firsts, smem=1, name="output_and_gains",
+    )
     entry_full, attend_full, middle_full, closing_full = [gains[at:at + 1] for at in range(4)]
     low_shape = shaped(window, heads * width)
     pair_cost = 2 * heads * window * window * width
-    entry_low, query_low, key_low, value_low, attended, log_totals = call(
+    entry_low, query_low, key_low, value_low, attended, log_totals, qkv_weight = call(
         attend_forward,
         (shaped(window, model), low_shape, low_shape, low_shape, low_shape,
-         shaped(heads, SEQ, 8, rows, dtype=f32)),
-        first, cosine, sine, query_code, *token_blocks,
+         shaped(heads, SEQ, 8, rows, dtype=f32), shaped(model, 3 * part)),
+        whose, entry_full, cosine, sine, query_code, *token_blocks,
+        after(firsts[0], output_own), *firsts[1:], smem=1,
         scratch=(
-            pltpu.VMEM((8, model), f32), pltpu.VMEM((window, model), bf16),
+            pltpu.VMEM((window, model), bf16),
             pltpu.VMEM((window, 128), f32),
         ),
         name="attend_forward",
     )
+    if lines:
+        gate_up_z = after(gate_up_z, attended)
+        rest = call(
+            others, shaped(3, shard, 2 * hidden_part), around, gate_up_z, smem=1, name="others",
+        )
+        attended, rest = lax.optimization_barrier((attended, rest))
+        gate_ups = (gate_up_z, gate_up_x[None], across(rest, wt))
+    else:
+        gate_ups = (gate_up_z,)
     output_far = after(swap(output_own, 2), attended)
     output_rows = call(
         arrange, shaped(model, model),
@@ -579,20 +669,15 @@
         name="arrange",
     )
 
-    if lines:
-        gate_up = call(
-            assemble, shaped(model, 2 * hidden_part),
-            sources, *gate_up_blocks[:-1], after(gate_up_blocks[-1], attended), smem=1,
-            name="assemble",
-        )
-    else:
-        gate_up = lax.all_gather(gate_up_own, "wt", axis=0, tiled=True)
+    gate_up = call(
+        assemble, shaped(model, 2 * hidden_part), whose, *gate_ups, smem=1, name="assemble",
+    )
 
     def exchange(blocks):
         return [blocks[0], swap(blocks[1], 1), swap(blocks[2], 2), swap(blocks[3], 3)]
 
     joined = exchange([attended[at * rows:(at + 1) * rows] for at in range(SEQ)])
-    joined = [joined[0], joined[1]] + [after(got, gate_up, output_rows) for got in joined[2:]]
+    joined = [joined[0], joined[1]] + [after(got, output_rows) for got in joined[2:]]
     inputs = tokens.astype(f32)
     mixed = dot(jnp.concatenate(joined, 1), output_rows)
     attend_normed, attend_inverse = normed_of(mixed)
@@ -659,7 +744,7 @@
     )
     down_got = across(down_send, wt)
     back_near = backward(channel_low, after(low_near, down_keep), fed_near[0])
-    near_got = back_near[1] + swap(back_near[2], 1).astype(f32)
+    near_got = swap(back_near[2], 1)
     gate_shape = shaped(model // 2, hidden_part)
     gate_keep, gate_send, up_keep, up_send = call(
         functools.partial(feed_weights, shard=shard),
@@ -669,28 +754,30 @@
     )
     gate_got = across(gate_send, wt)
     up_got = across(up_send, wt)
-    down_sum = add_low(down_keep, after(down_got, gate_keep))
+    far_got = after(far_got, gate_keep)
+    down_sum = add_low(down_keep, after(down_got, far_got))
     down_share = scatter_levels(down_sum, wt)
-    middle_grad = near_got + after(far_got, gate_keep, down_sum).astype(f32)
-
-    hidden_grad = incoming + norm_back(middle_grad, middle_normed, middle_inverse, middle_full)
-    middle_sum = jnp.sum(middle_grad * middle_normed, 0)
-    attend_sum = jnp.sum(hidden_grad * attend_normed, 0)
-    mixed_low = norm_back(hidden_grad, attend_normed, attend_inverse, attend_full).astype(bf16)
-    attended_grad = dot_nt(mixed_low, output_rows).astype(bf16)
-    attended_back = exchange([attended_grad[:, at * part:(at + 1) * part] for at in range(SEQ)])
+    hidden_grad, mixed_low, middle_sums, *attended_grads = call(
+        middle_backward,
+        (full, shaped(rows, model), shaped(16, model, dtype=f32)) + (shaped(rows, part),) * SEQ,
+        back_near[1], near_got, after(far_got, down_sum), hidden_state, mixed, cotangent, gains,
+        output_rows, name="middle_backward",
+    )
+    attend_sum = jnp.sum(middle_sums[:8], 0)
+    middle_sum = jnp.sum(middle_sums[8:], 0)
+    attended_back = exchange(attended_grads)
     output_grads = call(
         output_weights,
         (shaped(model, part, dtype=f32), shaped(model, part), shaped(model, part, dtype=f32),
          shaped(model, part)),
-        here, after(mixed_low, attended_grad), *joined, smem=1,
+        here, after(mixed_low, attended_grads[1]), *joined, smem=1,
         name="output_weights",
     )
     attended_back[1:] = [after(got, output_grads[0]) for got in attended_back[1:]]
     output_far = (output_grads[2] + swap(output_grads[3], 1).astype(f32)).astype(bf16)
     output_near = swap(output_grads[1], 1)
     output_far = after(output_far, *attended_back)
-    gate_sum = add_low(gate_keep, after(gate_got, down_share, *attended_back[1:]))
+    gate_sum = add_low(gate_keep, after(gate_got, *attended_back[1:]))
     gate_share = scatter_levels(gate_sum, wt)
     attended_back[0] = after(attended_back[0], output_far, gate_sum)
     output_got = swap(output_far, 2)
@@ -706,83 +793,52 @@
     gain_rows = jnp.stack([attend_sum, middle_sum, closing_sum]).astype(bf16)
     gain_rows = gain_rows.reshape(3, wt, shard).transpose(1, 0, 2).reshape(wt, 1, 3 * shard)
     gain_rows = jnp.pad(gain_rows, ((0, 0), (0, GAIN_ROWS - 1), (0, model - 3 * shard)))
-    mine = lax.axis_index("wt")
-    if lines:
-        whose = [mine ^ at for at in (0, 2, 4, 6, 1, 3, 5, 7)]
-    else:
-        levels = range(0, wt, 2)
-        whose = [at + mine % 2 for at in levels] + [at + 1 - mine % 2 for at in levels]
-    last = call(
-        last_weights, shaped(wt, shard + GAIN_ROWS, model),
-        jnp.stack([jnp.asarray(at, jnp.int32) for at in whose]),
-        entry_low, qkv_grad, output_grads[0], output_near, after(output_got, qkv_grad), gain_rows,
+    levels = range(0, wt, 2)
+    whose = numbers(*[at + xside for at in levels], *[at + 1 - xside for at in levels])
+    up_sum = add_low(up_keep, after(up_got, down_share, qkv_grad))
+    up_share = scatter_levels(up_sum, wt)
+    last_shape = shaped(wt // 2 * (shard + GAIN_ROWS), model)
+    last_keep, last_send = call(
+        last_weights, (last_shape, last_shape),
+        whose, entry_low, after(qkv_grad, up_sum), output_grads[0], output_near, after(output_got, qkv_grad), gain_rows,
         smem=1, scratch=(pltpu.VMEM((model, model), bf16),), name="last_weights",
     )
-    up_sum = add_low(up_keep, after(up_got, last))
-    up_share = scatter_levels(up_sum, wt)
-    if lines:
-
-        def send(value, bit):
-            return lax.ppermute(value, "wt", [(at, at ^ bit) for at in range(wt)])
-
-        far_x = across(last[6:8], wt)
-        far = add_low(last[2:4], after(far_x, up_sum))
-        near_x = across(after(last[4:6], far), wt)
-        last_z = [send(far[1], 6), send(far[0], 4)]
-        near = last[0:2].astype(f32) + near_x.astype(f32)
-        near_send = near[1].astype(bf16)
-        last_z.append(send(near_send, 2))
-    else:
-        last_rows = wt // 2 * (shard + GAIN_ROWS)
-        last_halves = last.reshape(2, last_rows, model)
-        last_share = scatter_levels(
-            add_low(last_halves[0], across(last_halves[1], wt)), wt
-        )
-        near_send = last_share
-
-    qkv_weight = first[:, :shard, :3 * part].reshape(model, 3 * part)
+    qkv_grad = after(qkv_grad, last_send)
+
     entry_far = chip_sum(qkv_grad[2 * rows:], qkv_weight, dot_nt).astype(bf16)
-    entry_grad = chip_sum(after(qkv_grad[:2 * rows], entry_far), qkv_weight, dot_nt)
-    entry_grad = entry_grad + swap(entry_far, 2).astype(f32)
-    entry_normed, entry_inverse = normed_of(inputs)
-    input_grad = hidden_grad + norm_back(entry_grad, entry_normed, entry_inverse, entry_full)
-    entry_sum = jnp.sum(entry_grad * entry_normed, 0).reshape(8, model // 8)
-    for axis, size in (("seq", SEQ), ("wt", wt)):
-        bit = 1
-        while bit < size:
-            entry_sum = entry_sum + lax.ppermute(
-                entry_sum, axis, [(at, at ^ bit) for at in range(size)]
-            )
-            bit *= 2
-    grad_entry = lax.dynamic_slice_in_dim(entry_sum.reshape(model), mine * shard, shard)
-
+    entry_near = chip_sum(after(qkv_grad[:2 * rows], entry_far), qkv_weight, dot_nt)
+    last_sum = add_low(last_keep, after(across(last_send, wt), gate_share, up_sum, entry_near))
+    last_share = scatter_levels(last_sum, wt)
+    entry_got = swap(entry_far, 2)
     share = call(
         join_shares, shaped((2 * hidden_part * shard + model * padded) // piece, piece),
-        after(gate_share, near_send), up_share, down_share, name="join_shares",
-    )
-    if lines:
-        last_z = [after(value, share) for value in last_z]
-        last_share = (near[0] + sum(value.astype(f32) for value in last_z)).astype(bf16)
+        after(gate_share, last_sum), up_share, down_share, name="join_shares",
+    )
     share_got = gather_blocks(share)
-    last_got = gather_blocks(last_share)
     grad_gate, grad_up, grad_down = call(
         functools.partial(unpack_feed, shard=shard, padded=padded),
         (shaped(shard, hidden, dtype=f32), shaped(shard, hidden, dtype=f32),
          shaped(SEQ * chunk, model, dtype=f32)),
         here, *share_got, smem=1, name="unpack_feed",
     )
+    entry_grad = entry_near + after(entry_got, grad_down).astype(f32)
+    entry_normed, entry_inverse = normed_of(inputs)
+    input_grad = hidden_grad + norm_back(entry_grad, entry_normed, entry_inverse, entry_full)
+    last_got = gather_blocks(after(last_share, grad_down))
     weight_shape = shaped(shard, model, dtype=f32)
-    grad_query, grad_key, grad_value, grad_output, gain_sums = call(
+    grad_query, grad_key, grad_value, grad_output, gain_sums, grad_entry = call(
         functools.partial(unpack_last, shard=shard),
-        (weight_shape,) * 4 + (shaped(GAIN_ROWS, model, dtype=f32),),
-        here, last_share, last_got[1], after(last_got[2], grad_down),
-        last_got[3], smem=1, name="unpack_last",
+        (weight_shape,) * 4
+        + (shaped(GAIN_ROWS, model, dtype=f32), shaped(1, shard, dtype=f32)),
+        here, last_share, last_got[1], last_got[2],
+        last_got[3], entry_gain[None], query_weight, key_weight, value_weight, smem=1,
+        name="unpack_last",
     )
     grad_attend, grad_middle, grad_closing = [
         gain_sums[0, at * shard:(at + 1) * shard] for at in range(3)
     ]
     return (
-        layer_output, input_grad, grad_entry, grad_query, grad_key, grad_value, grad_output,
+        layer_output, input_grad, grad_entry[0], grad_query, grad_key, grad_value, grad_output,
         grad_attend, grad_middle, grad_gate, grad_up, grad_down, grad_closing,
     )
 

time: 368 us -> 348 us (0.946)
  Pallas kernels: 104 us -> 128 us
  starting transfers between devices: 49.9 us -> 29.6 us
  other arithmetic: 36.6 us -> 18.2 us
  local copies, waits for them, and re-layouts: 23.6 us -> 17.2 us
  waiting for transfers between devices: 122 us -> 127 us
    ppermute x17 -> x0, waiting for transfers between devices: 57.7 us -> none  [the longest x8 42.9 us: send(): return lax.ppermute(value, 'wt', pairs)]
    ppermute x37, waiting for transfers between devices: 22.5 us -> 64.9 us  [swap(): return lax.ppermute(value, 'seq', [(i, i ^ bit) for i in range(SEQ)])]
    ppermute x5 -> x9, waiting for transfers between devices: 27 us -> 58.1 us  [across(): return lax.ppermute(value, 'wt', [(at, at ^ 1) for at in range(wt)])]
    pallas_call x17 -> x25, Pallas kernels: 104 us -> 128 us  [call(): pl.pallas_call(kernel, out_shape=tuple(outs) if many else outs, in_specs=...]
    ppermute x17 -> x0, starting transfers between devices: 22.7 us -> none  [the longest x8 12.3 us: send(): return lax.ppermute(value, 'wt', pairs)]
    reduce_scatter x3 -> x4, waiting for transfers between devices: 11.4 us -> 0.07 us  [scatter_levels(): lax.psum_scatter(value, 'wt', scatter_dimension=0, tiled=True, axis_index...]
    convert_element_type x7 -> x0, other arithmetic: 8.26 us -> none  [the longest x4 5.88 us: add_low(): return (left.astype(f32) + right.astype(f32)).astype(bf16)]
    ppermute x5 -> x9, starting transfers between devices: 6.12 us -> 11.1 us  [across(): return lax.ppermute(value, 'wt', [(at, at ^ 1) for at in range(wt)])]
  transfers between devices with their start and end apart: 64 -> 53, of which waited for: 22 -> 24; matrix products, arithmetic and copies ran while one was open for 14% -> 7% of each run, Pallas kernels for 24% -> 34%
where the time goes in v4:
time: 348 us; the launch traced here: 342 us
  Pallas kernels  128 us (37%)
  waiting for transfers between devices  127 us (36%)
  starting transfers between devices  29.6 us (9%)
  other arithmetic  18.2 us (5%)
  local copies, waits for them, and re-layouts  17.2 us (5%)
  between operations  15.7 us (5%)
  matrix products  5.71 us (2%)
    pallas_call x25, Pallas kernels, call(): pl.pallas_call(kernel, out_shape=tuple(outs) if many else outs, in_specs=...  128 us
    ppermute x37, waiting for transfers between devices, swap(): return lax.ppermute(value, 'seq', [(i, i ^ bit) for i in range(SEQ)])  64.9 us
    ppermute x9, waiting for transfers between devices, across(): return lax.ppermute(value, 'wt', [(at, at ^ 1) for at in range(wt)])  58.1 us
    ppermute x37, starting transfers between devices, swap(): return lax.ppermute(value, 'seq', [(i, i ^ bit) for i in range(SEQ)])  18.1 us
    unnamed x106, local copies, waits for them, and re-layouts  11.2 us
    ppermute x9, starting transfers between devices, across(): return lax.ppermute(value, 'wt', [(at, at ^ 1) for at in range(wt)])  11.1 us
  transfers between devices with their start and end apart: 53, of which 24 were waited for; matrix products, arithmetic and copies ran while one was open for 7% of the time, Pallas kernels for 34%

profile of v4, /device:TPU:0, one launch (start us, length us, event | category | flops | bytes accessed | tf_op | source)
XLA Modules:
  0.0 341.5 jit_solution(3091489783482868699)
XLA Ops:
  21.2 4.7 %collective-permute-done.1.far_ref = bf16[256,1024]{1,0:T(8,128)(2,1)} collective-permute-done((bf16[256,1024]{1,0:T(8,128)(2,1)S(1)}, bf16[256,1024]{1,0:T(8,128)(2,1)}, u32[]{:S(2)}, u32[]{:S(2)}) %collective-permute-start.1) | collective-permute-done | bytes 524320 | tf_op jit(solution)/shard_map/ppermute | solution.py:95
  32.5 5.8 %collective-permute-done.3 = bf16[256,1024]{1,0:T(8,128)(2,1)S(1)} collective-permute-done((bf16[256,1024]{1,0:T(8,128)(2,1)S(1)}, bf16[256,1024]{1,0:T(8,128)(2,1)S(1)}, u32[]{:S(2)}, u32[]{:S(2)}) %collective-permute-start.3) | collective-permute-done | bytes 524320 | tf_op jit(solution)/shard_map/ppermute | solution.py:95
  38.3 3.6 %all-gather.8.cloned.1.call-done = bf16[544,1024]{1,0:T(8,128)(2,1)} async-done(((bf16[136,1024]{1,0:T(8,128)(2,1)}), bf16[544,1024]{1,0:T(8,128)(2,1)}) %all-gather.8.cloned.1.call-update) | async-done | bytes 1114128 | tf_op jit(solution)/shard_map/all_gather | solution.py:506
  46.8 19.1 %collective-permute-done.6.refs_2_ = bf16[3,136,1024]{2,1,0:T(8,128)(2,1)S(1)} collective-permute-done((bf16[3,136,1024]{2,1,0:T(8,128)(2,1)}, bf16[3,136,1024]{2,1,0:T(8,128)(2,1)S(1)}, u32[]{:S(2)}, u32[]{:S(2)}) %collective-permute-start.6) | collective-permute-done | bytes 835616 | tf_op jit(solution)/shard_map/ppermute | solution.py:513
  73.1 14.6 %attend_forward.1 = (bf16[1024,1024]{1,0:T(8,128)(2,1)}, bf16[1024,256]{1,0:T(8,128)(2,1)}, bf16[1024,256]{1,0:T(8,128)(2,1)}, bf16[1024,256]{1,0:T(8,128)(2,1)}...) custom-call(s32[8]{0:T(128)} %stack.104.at_ref, ...), custom_call_target="tpu_custom_call" | custom-call | flops 34500000 | tf_op jit(solution)/shard_map/attend_forward/pallas_call | solution.py:71
  103.7 17.6 %collective-permute-done.14.refs_2_ = bf16[3,128,1536]{2,1,0:T(8,128)(2,1)S(1)} collective-permute-done((bf16[3,128,1536]{2,1,0:T(8,128)(2,1)}, bf16[3,128,1536]{2,1,0:T(8,128)(2,1)S(1)}, u32[]{:S(2)}, u32[]{:S(2)}) %collective-permute-start.14) | collective-permute-done | bytes 1179680 | tf_op jit(solution)/shard_map/ppermute | solution.py:513
  122.3 3.7 %assemble.1.weight_ref = bf16[1024,1536]{1,0:T(8,128)(2,1)} custom-call(s32[8]{0:T(128)} %stack.104.at_ref, bf16[4,128,1536]{2,1,0:T(8,128)(2,1)} %bitcast.77, bf16[1,128,1536]{2,1,0:T(8,128)(2,1)} %bitcast.25.refs_1_, bf16[3,128,1536]{2,1,0:T(8,128)(2,1)} %copy-done.17), custom_call_target="tpu_custom_call" | custom-call | flops 9200000 | tf_op jit(solution)/shard_map/assemble/pallas_call | solution.py:71
  126.1 6.4 %feed_forward.2 = (bf16[512,1536]{1,0:T(8,128)(2,1)}, bf16[512,768]{1,0:T(8,128)(2,1)}, f32[256,1024]{1,0:T(8,128)}, bf16[256,1024]{1,0:T(8,128)(2,1)}) custom-call(bf16[256,1024]{1,0:T(8,128)(2,1)} %copy-done.8, bf16[256,1024]{1,0:T(8,128)(2,1)} %collective-permute-done.13.second_ref.near_ref, bf16[1024,1536]{1,0:T(8,128)(2,1)} %assemble.1.weight_ref, ...), custom_call_target="tpu_custom_call" | custom-call | flops 13800000 | tf_op jit(solution)/shard_map/feed_forward/pallas_call | solution.py:71
  137.4 6.4 %feed_forward.3 = (bf16[512,1536]{1,0:T(8,128)(2,1)}, bf16[512,768]{1,0:T(8,128)(2,1)}, f32[256,1024]{1,0:T(8,128)}, bf16[256,1024]{1,0:T(8,128)(2,1)}) custom-call(bf16[256,1024]{1,0:T(8,128)(2,1)} %collective-permute-done.17.first_ref.far_ref, bf16[256,1024]{1,0:T(8,128)(2,1)} %copy-done.14, bf16[1024,1536]{1,0:T(8,128)(2,1)} %assemble.1.weight_ref, ...), custom_call_target="tpu_custom_call" | custom-call | flops 13800000 | tf_op jit(solution)/shard_map/feed_forward/pallas_call | solution.py:71
  143.8 6.2 %collective-permute-done.21 = bf16[256,1024]{1,0:T(8,128)(2,1)S(1)} collective-permute-done((bf16[256,1024]{1,0:T(8,128)(2,1)S(1)}, bf16[256,1024]{1,0:T(8,128)(2,1)S(1)}, u32[]{:S(2)}, u32[]{:S(2)}) %collective-permute-start.21) | collective-permute-done | bytes 524320 | tf_op jit(solution)/shard_map/ppermute | solution.py:95
  155.1 7.1 %feed_backward.2 = (bf16[512,1536]{1,0:T(8,128)(2,1)}, f32[256,1024]{1,0:T(8,128)}, bf16[256,1024]{1,0:T(8,128)(2,1)}) custom-call(bf16[256,1024]{1,0:T(8,128)(2,1)} %copy-done.5, bf16[256,1024]{1,0:T(8,128)(2,1)} %copy-done.12, bf16[512,1536]{1,0:T(8,128)(2,1)} %get-tuple-element.124.both_ref, bf16[1024,1536]{1,0:T(8,128)(2,1)} %assemble.1.weight_ref, ...), custom_call_target="tpu_custom_call" | custom-call | flops 16100000 | tf_op jit(solution)/shard_map/feed_backward/pallas_call | solution.py:71
  162.4 4.4 %collective-permute-done.20 = bf16[256,1024]{1,0:T(8,128)(2,1)S(1)} collective-permute-done((bf16[256,1024]{1,0:T(8,128)(2,1)S(1)}, bf16[256,1024]{1,0:T(8,128)(2,1)S(1)}, u32[]{:S(2)}, u32[]{:S(2)}) %collective-permute-start.20) | collective-permute-done | bytes 524320 | tf_op jit(solution)/shard_map/ppermute | solution.py:95
  172.8 5.0 %down_weights.1 = (bf16[384,1024]{1,0:T(8,128)(2,1)}, bf16[384,1024]{1,0:T(8,128)(2,1)}) custom-call(s32[1]{0:T(128)} %bitcast.side_ref, bf16[256,1024]{1,0:T(8,128)(2,1)} %copy-done.6, bf16[256,1024]{1,0:T(8,128)(2,1)} %copy-done.13, bf16[256,1024]{1,0:T(8,128)(2,1)} %copy-done.5, bf16[256,1024]{1,0:T(8,128)(2,1)} %copy-done.12, ...), custom_call_target="tpu_custom_call" | custom-call | flops 9200000 | tf_op jit(solution)/shard_map/down_weights/pallas_call | solution.py:71
  179.3 7.3 %feed_backward.3 = (bf16[512,1536]{1,0:T(8,128)(2,1)}, f32[256,1024]{1,0:T(8,128)}, bf16[256,1024]{1,0:T(8,128)(2,1)}) custom-call(bf16[256,1024]{1,0:T(8,128)(2,1)} %copy-done.6, bf16[256,1024]{1,0:T(8,128)(2,1)} %copy-done.13, bf16[512,1536]{1,0:T(8,128)(2,1)} %get-tuple-element.119.both_ref, bf16[1024,1536]{1,0:T(8,128)(2,1)} %assemble.1.weight_ref, ...), custom_call_target="tpu_custom_call" | custom-call | flops 16100000 | tf_op jit(solution)/shard_map/feed_backward/pallas_call | solution.py:71
  188.7 7.9 %feed_weights.1 = (bf16[512,768]{1,0:T(8,128)(2,1)}, bf16[512,768]{1,0:T(8,128)(2,1)}, bf16[512,768]{1,0:T(8,128)(2,1)}, bf16[512,768]{1,0:T(8,128)(2,1)}) custom-call(s32[1]{0:T(128)} %bitcast.side_ref, bf16[256,1024]{1,0:T(8,128)(2,1)} %copy-done.8, bf16[256,1024]{1,0:T(8,128)(2,1)} %collective-permute-done.13.second_ref.near_ref, ...), custom_call_target="tpu_custom_call" | custom-call | flops 18400000 | tf_op jit(solution)/shard_map/feed_weights/pallas_call | solution.py:71
  196.6 4.3 %collective-permute-done.26.far_ref = bf16[256,1024]{1,0:T(8,128)(2,1)S(1)} collective-permute-done((bf16[256,1024]{1,0:T(8,128)(2,1)S(1)}, bf16[256,1024]{1,0:T(8,128)(2,1)S(1)}, u32[]{:S(2)}, u32[]{:S(2)}) %collective-permute-start.26) | collective-permute-done | bytes 524320 | tf_op jit(solution)/shard_map/ppermute | solution.py:95
  205.0 6.0 %middle_backward.1 = (f32[256,1024]{1,0:T(8,128)}, bf16[256,1024]{1,0:T(8,128)(2,1)}, f32[16,1024]{1,0:T(8,128)}, bf16[256,256]{1,0:T(8,128)(2,1)}, bf16[256,256...) custom-call(f32[256,1024]{1,0:T(8,128)} %get-tuple-element.135.keep_ref, ...), custom_call_target="tpu_custom_call" | custom-call | flops 9200000 | tf_op jit(solution)/shard_map/middle_backward/pallas_call | solution.py:71
  219.6 3.5 %collective-permute-done.30.refs_2_ = bf16[256,256]{1,0:T(8,128)(2,1)S(1)} collective-permute-done((bf16[256,256]{1,0:T(8,128)(2,1)}, bf16[256,256]{1,0:T(8,128)(2,1)S(1)}, u32[]{:S(2)}, u32[]{:S(2)}) %collective-permute-start.30) | collective-permute-done | bytes 131104 | tf_op jit(solution)/shard_map/ppermute | solution.py:95
  231.7 14.2 %attend_backward.1.grad_ref = bf16[1024,768]{1,0:T(8,128)(2,1)} custom-call(bf16[1024,256]{1,0:T(8,128)(2,1)} %get-tuple-element.145.query_ref, bf16[1024,256]{1,0:T(8,128)(2,1)} %get-tuple-element.146.key_ref, bf16[1024,256]{1,0:T(8,128)(2,1)} %get-tuple-element.147.value_ref, f32[2,4,8,256]{3,2,1,0:T(8,128)} %get-tuple-element.148.log_ref, ...), custom_call_target="tpu_custom_call" | custom-call | flops 32200000 | tf_op jit(solution)/shard_map/attend_backward/pallas_call | solution.py:71
  250.1 6.4 %last_weights.1 = (bf16[544,1024]{1,0:T(8,128)(2,1)}, bf16[544,1024]{1,0:T(8,128)(2,1)}) custom-call(s32[8]{0:T(128)} %stack.121.at_ref, bf16[1024,1024]{1,0:T(8,128)(2,1)} %get-tuple-element.165.low_ref, bf16[1024,768]{1,0:T(8,128)(2,1)} %attend_backward.1.grad_ref, f32[1024,256]{1,0:T(8,128)} %get-tuple-element.155.keep_ref, bf16[1024,256]{1,0:T(8,128)(2,1)} %copy-done.29, ...), custom_call_target="tpu_custom_call" | custom-call | flops 13800000 | tf_op jit(solution)/shard_map/last_weights/pallas_call | solution.py:71
  263.9 20.8 %collective-permute-done.39.right_ref = bf16[544,1024]{1,0:T(8,128)(2,1)} collective-permute-done((bf16[544,1024]{1,0:T(8,128)(2,1)}, bf16[544,1024]{1,0:T(8,128)(2,1)}, u32[]{:S(2)}, u32[]{:S(2)}) %collective-permute-start.39) | collective-permute-done | bytes 1114144 | tf_op jit(solution)/shard_map/ppermute | solution.py:513
  291.4 13.1 %collective-permute-done.41.refs_2_ = bf16[1152,256]{1,0:T(8,128)(2,1)S(1)} collective-permute-done((bf16[1152,256]{1,0:T(8,128)(2,1)}, bf16[1152,256]{1,0:T(8,128)(2,1)S(1)}, u32[]{:S(2)}, u32[]{:S(2)}) %collective-permute-start.41) | collective-permute-done | bytes 589856 | tf_op jit(solution)/shard_map/ppermute | solution.py:95
  307.7 8.8 %unpack_feed.1 = (f32[128,2816]{1,0:T(8,128)}, f32[128,2816]{1,0:T(8,128)}, f32[352,1024]{1,0:T(8,128)}) custom-call(s32[1]{0:T(128)} %bitcast.8.place_ref, bf16[1152,256]{1,0:T(8,128)(2,1)} %join_shares.1.refs_0_, bf16[1152,256]{1,0:T(8,128)(2,1)} %copy-done.25, bf16[1152,256]{1,0:T(8,128)(2,1)} %copy-done.24, bf16[1152,256]{1,0:T(8,128)(2,1)} %copy-done.26), custom_call_target="tpu_custom_call" | custom-call | flops 20700000 | tf_op jit(solution)/shard_map/unpack_feed/pallas_call | solution.py:71
  321.0 6.6 %collective-permute-done.44.refs_2_ = bf16[136,1024]{1,0:T(8,128)(2,1)S(1)} collective-permute-done((bf16[136,1024]{1,0:T(8,128)(2,1)}, bf16[136,1024]{1,0:T(8,128)(2,1)S(1)}, u32[]{:S(2)}, u32[]{:S(2)}) %collective-permute-start.44) | collective-permute-done | bytes 278560 | tf_op jit(solution)/shard_map/ppermute | solution.py:95
  (274 shorter events, 122.3 us)
Async XLA Ops:
  7.2 34.8 %all-gather.8.cloned.1.call-start = ((), (), s32[]{:S(2)}) async-start(), calls=%async_computation.9 | async-start | bytes 1392640 | tf_op jit(solution)/shard_map/all_gather | solution.py:506
  9.3 78.5 %all-gather.10.cloned.1.call-start = ((), (), s32[]{:S(2)}) async-start(), calls=%async_computation.10 | async-start | bytes 1966080 | tf_op jit(solution)/shard_map/all_gather | solution.py:506
  9.3 23.2 %collective-permute-start.4 = (bf16[136,1024]{1,0:T(8,128)(2,1)}, bf16[136,1024]{1,0:T(8,128)(2,1)S(1)}, u32[]{:S(2)}, u32[]{:S(2)}) collective-permute-start(bf16[136,1024]{1,0:T(8,128)(2,1)} %pack_first.1), channel_id=1, source_target_pairs={{0,4},{4,0},{8,12},{12,8},{16,20},{20,16},{24,28},{28,24},{1,5},{5... | collective-permute-start | bytes 835592 | tf_op jit(solution)/shard_map/ppermute | solution.py:513
  13.9 18.7 %collective-permute-start = (bf16[256,1024]{1,0:T(8,128)(2,1)S(1)}, bf16[256,1024]{1,0:T(8,128)(2,1)}, u32[]{:S(2)}, u32[]{:S(2)}) collective-permute-start(bf16[256,1024]{1,0:T(8,128)(2,1)S(1)} %copy-done.3), channel_id=1, source_target_pairs={{0,1},{1,0},{2,3},{3,2},{4,5},{5,4},{6,7},{7,6},{8,9},{9,8},{10,11... | collective-permute-start | bytes 1572872 | tf_op jit(solution)/shard_map/ppermute | solution.py:95
  17.3 15.2 %collective-permute-start.5 = (bf16[128,1536]{1,0:T(8,128)(2,1)}, bf16[128,1536]{1,0:T(8,128)(2,1)}, u32[]{:S(2)}, u32[]{:S(2)}) collective-permute-start(bf16[128,1536]{1,0:T(8,128)(2,1)} %get-tuple-element.104), channel_id=1, source_target_pairs={{0,4},{4,0},{8,12},{12,8},{16,20},{20,16},{24,28},{28,24},{1,5},{5... | collective-permute-start | bytes 1179656 | tf_op jit(solution)/shard_map/ppermute | solution.py:513
  17.8 108.2 %all-gather.6.cloned.1.call-start = ((), (), s32[]{:S(2)}) async-start(), calls=%async_computation.4 | async-start | bytes 1966080 | tf_op jit(solution)/shard_map/all_gather | solution.py:506
  44.2 21.7 %collective-permute-start.6 = (bf16[3,136,1024]{2,1,0:T(8,128)(2,1)}, bf16[3,136,1024]{2,1,0:T(8,128)(2,1)S(1)}, u32[]{:S(2)}, u32[]{:S(2)}) collective-permute-start(bf16[3,136,1024]{2,1,0:T(8,128)(2,1)} %others.2), channel_id=1, source_target_pairs={{0,4},{4,0},{8,12},{12,8},{16,20},{20,16},{24,28},{28,24},{1,5},{5... | collective-permute-start | bytes 2506760 | tf_op jit(solution)/shard_map/ppermute | solution.py:513
  45.6 25.1 %collective-permute-start.15 = (bf16[96,1024]{1,0:T(8,128)(2,1)S(1)}, bf16[96,1024]{1,0:T(8,128)(2,1)S(1)}, u32[]{:S(2)}, u32[]{:S(2)}) collective-permute-start(bf16[96,1024]{1,0:T(8,128)(2,1)S(1)} %copy-done.40), channel_id=1, source_target_pairs={{0,4},{4,0},{8,12},{12,8},{16,20},{20,16},{24,28},{28,24},{1,5},{5... | collective-permute-start | bytes 589832 | tf_op jit(solution)/shard_map/ppermute | solution.py:513
  69.2 21.2 %collective-permute-start.10 = (bf16[1024,256]{1,0:T(8,128)(2,1)}, bf16[1024,256]{1,0:T(8,128)(2,1)S(1)}, u32[]{:S(2)}, u32[]{:S(2)}) collective-permute-start(bf16[1024,256]{1,0:T(8,128)(2,1)} %get-tuple-element.107.refs_0_), channel_id=1, source_target_pairs={{0,2},{1,3},{2,0},{3,1},{4,6},{5,7},{6,4},{7,5},{8,10},{9,11},{10,... | collective-permute-start | bytes 1572872 | tf_op jit(solution)/shard_map/ppermute | solution.py:95
  71.5 174.5 %reduce-scatter.5.cloned.1.call-start = ((), (), s32[]{:S(2)}) async-start(), calls=%async_computation.5 | async-start | bytes 983040 | tf_op jit(solution)/shard_map/reduce_scatter | solution.py:517
  71.6 21.4 %collective-permute-start.9 = (bf16[1024,256]{1,0:T(8,128)(2,1)}, bf16[1024,256]{1,0:T(8,128)(2,1)S(1)}, u32[]{:S(2)}, u32[]{:S(2)}) collective-permute-start(bf16[1024,256]{1,0:T(8,128)(2,1)} %get-tuple-element.107.refs_0_), channel_id=1, source_target_pairs={{0,1},{1,0},{2,3},{3,2},{4,5},{5,4},{6,7},{7,6},{8,9},{9,8},{10,11... | collective-permute-start | bytes 1572872 | tf_op jit(solution)/shard_map/ppermute | solution.py:95
  92.9 28.4 %collective-permute-start.14 = (bf16[3,128,1536]{2,1,0:T(8,128)(2,1)}, bf16[3,128,1536]{2,1,0:T(8,128)(2,1)S(1)}, u32[]{:S(2)}, u32[]{:S(2)}) collective-permute-start(bf16[3,128,1536]{2,1,0:T(8,128)(2,1)} %others.3), channel_id=1, source_target_pairs={{0,4},{4,0},{8,12},{12,8},{16,20},{20,16},{24,28},{28,24},{1,5},{5... | collective-permute-start | bytes 3538952 | tf_op jit(solution)/shard_map/ppermute | solution.py:513
  103.2 22.9 %collective-permute-start.13 = (bf16[256,1024]{1,0:T(8,128)(2,1)S(1)}, bf16[256,1024]{1,0:T(8,128)(2,1)}, u32[]{:S(2)}, u32[]{:S(2)}) collective-permute-start(bf16[256,1024]{1,0:T(8,128)(2,1)S(1)} %multiply_convert_fusion.1.first_ref.own_ref), channel_id=1, source_target_pairs={{0,1},{1,0},{2,3},{3,2},{4,5},{5,4},{6,7},{7,6},{8,9},{9,8},{10,11... | collective-permute-start | bytes 1572872 | tf_op jit(solution)/shard_map/ppermute | solution.py:95
  103.2 29.2 %collective-permute-start.17 = (bf16[256,1024]{1,0:T(8,128)(2,1)S(1)}, bf16[256,1024]{1,0:T(8,128)(2,1)}, u32[]{:S(2)}, u32[]{:S(2)}) collective-permute-start(bf16[256,1024]{1,0:T(8,128)(2,1)S(1)} %multiply_convert_fusion.1.first_ref.own_ref), channel_id=1, source_target_pairs={{0,2},{1,3},{2,0},{3,1},{4,6},{5,7},{6,4},{7,5},{8,10},{9,11},{10,... | collective-permute-start | bytes 1572872 | tf_op jit(solution)/shard_map/ppermute | solution.py:95
  177.9 23.1 %collective-permute-start.27 = (bf16[384,1024]{1,0:T(8,128)(2,1)}, bf16[384,1024]{1,0:T(8,128)(2,1)S(1)}, u32[]{:S(2)}, u32[]{:S(2)}) collective-permute-start(bf16[384,1024]{1,0:T(8,128)(2,1)} %get-tuple-element.141), channel_id=1, source_target_pairs={{0,4},{4,0},{8,12},{12,8},{16,20},{20,16},{24,28},{28,24},{1,5},{5... | collective-permute-start | bytes 2359304 | tf_op jit(solution)/shard_map/ppermute | solution.py:513
  204.3 59.6 %reduce-scatter.7.cloned.1.call-start = ((), (), s32[]{:S(2)}) async-start(), calls=%async_computation.6 | async-start | bytes 983040 | tf_op jit(solution)/shard_map/reduce_scatter | solution.py:517
  204.4 19.2 %collective-permute-start.32 = (bf16[512,768]{1,0:T(8,128)(2,1)S(1)}, bf16[512,768]{1,0:T(8,128)(2,1)S(1)}, u32[]{:S(2)}, u32[]{:S(2)}) collective-permute-start(bf16[512,768]{1,0:T(8,128)(2,1)S(1)} %copy-done.50), channel_id=1, source_target_pairs={{0,4},{4,0},{8,12},{12,8},{16,20},{20,16},{24,28},{28,24},{1,5},{5... | collective-permute-start | bytes 2359304 | tf_op jit(solution)/shard_map/ppermute | solution.py:513
  227.0 60.9 %reduce-scatter.9.cloned.1.call-start = ((), (), s32[]{:S(2)}) async-start(), calls=%async_computation.7 | async-start | bytes 983040 | tf_op jit(solution)/shard_map/reduce_scatter | solution.py:517
  227.1 18.8 %collective-permute-start.33 = (bf16[512,768]{1,0:T(8,128)(2,1)}, bf16[512,768]{1,0:T(8,128)(2,1)S(1)}, u32[]{:S(2)}, u32[]{:S(2)}) collective-permute-start(bf16[512,768]{1,0:T(8,128)(2,1)} %get-tuple-element.167), channel_id=1, source_target_pairs={{0,4},{4,0},{8,12},{12,8},{16,20},{20,16},{24,28},{28,24},{1,5},{5... | collective-permute-start | bytes 2359304 | tf_op jit(solution)/shard_map/ppermute | solution.py:513
  229.0 16.9 %collective-permute-start.35 = (bf16[1024,256]{1,0:T(8,128)(2,1)}, bf16[1024,256]{1,0:T(8,128)(2,1)S(1)}, u32[]{:S(2)}, u32[]{:S(2)}) collective-permute-start(bf16[1024,256]{1,0:T(8,128)(2,1)} %add_convert_fusion), channel_id=1, source_target_pairs={{0,2},{1,3},{2,0},{3,1},{4,6},{5,7},{6,4},{7,5},{8,10},{9,11},{10,... | collective-permute-start | bytes 1572872 | tf_op jit(solution)/shard_map/ppermute | solution.py:95
  229.5 19.8 %collective-permute-start.34 = (bf16[1024,256]{1,0:T(8,128)(2,1)}, bf16[1024,256]{1,0:T(8,128)(2,1)S(1)}, u32[]{:S(2)}, u32[]{:S(2)}) collective-permute-start(bf16[1024,256]{1,0:T(8,128)(2,1)} %get-tuple-element.170), channel_id=1, source_target_pairs={{0,1},{1,0},{2,3},{3,2},{4,5},{5,4},{6,7},{7,6},{8,9},{9,8},{10,11... | collective-permute-start | bytes 1572872 | tf_op jit(solution)/shard_map/ppermute | solution.py:95
  257.8 61.3 %reduce-scatter.11.cloned.1.call-start = ((), (), s32[]{:S(2)}) async-start(), calls=%async_computation.8 | async-start | bytes 1392640 | tf_op jit(solution)/shard_map/reduce_scatter | solution.py:517
  257.9 26.9 %collective-permute-start.39 = (bf16[544,1024]{1,0:T(8,128)(2,1)}, bf16[544,1024]{1,0:T(8,128)(2,1)}, u32[]{:S(2)}, u32[]{:S(2)}) collective-permute-start(bf16[544,1024]{1,0:T(8,128)(2,1)} %get-tuple-element.173), channel_id=1, source_target_pairs={{0,4},{4,0},{8,12},{12,8},{16,20},{20,16},{24,28},{28,24},{1,5},{5... | collective-permute-start | bytes 3342344 | tf_op jit(solution)/shard_map/ppermute | solution.py:513
  291.4 14.6 %collective-permute-start.40 = (bf16[1152,256]{1,0:T(8,128)(2,1)}, bf16[1152,256]{1,0:T(8,128)(2,1)S(1)}, u32[]{:S(2)}, u32[]{:S(2)}) collective-permute-start(bf16[1152,256]{1,0:T(8,128)(2,1)} %join_shares.1.refs_0_), channel_id=1, source_target_pairs={{0,1},{1,0},{2,3},{3,2},{4,5},{5,4},{6,7},{7,6},{8,9},{9,8},{10,11... | collective-permute-start | bytes 1769480 | tf_op jit(solution)/shard_map/ppermute | solution.py:95
  (80 other events, 565.4 us)
Sparse Core Ops, SparseCore 0:
  10.2 31.7 all-gather.7
  44.1 36.5 all-gather.9
  82.8 36.0 all-gather.5
  204.5 20.9 reduce-scatter.4
  228.2 22.5 reduce-scatter.6
  257.9 22.2 reduce-scatter.8
  288.0 27.1 reduce-scatter.10
